TPU v7x, 32 devices: a whole 2x2x4 slice. The times are simulated.
32 devices in a mesh: dp: 8 (over y, x, core), mp: 4 (over z).
Axes of the slice: x: 2, y: 2, z: 4, core: 2. Of those that a mesh axis runs over, the one named last changes fastest.
Arguments:
- inputs: bfloat16 [8192, 2048], P(('dp', 'mp')), may hold values from -6 to 6
- keys_values: bfloat16 [8192, 2, 2048], P('dp', None, 'mp'), may hold values from -6 to 6
- segment_ids: int32 [8, 1024], P('dp'), may hold values from 0 to 15, never falling along the last dimension, each value on 1 to 512 neighbouring positions
- gain_first: float32 [2048], replicated, may hold values from 0.25 to 1.75
- gain_second: float32 [2048], replicated, may hold values from 0.25 to 1.75
- w_query: bfloat16 [2048, 2048], P('dp', 'mp'), may hold values from -0.125 to 0.125
- w_out: bfloat16 [2048, 2048], P('mp', 'dp'), may hold values from -0.5 to 0.5
- w_gate: bfloat16 [2048, 5504], P('dp', 'mp'), may hold values from -0.125 to 0.125
- w_up: bfloat16 [2048, 5504], P('dp', 'mp'), may hold values from -0.125 to 0.125
- w_down: bfloat16 [5504, 2048], P('mp', 'dp'), may hold values from -0.15625 to 0.15625
- cotangent: bfloat16 [8192, 2048], P(('dp', 'mp')), may hold values from -6 to 6
Outputs:
- output: bfloat16 [8192, 2048], P(('dp', 'mp'))
- grad_input: float32 [8192, 2048], P(('dp', 'mp'))
- grad_kv: float32 [8192, 2, 2048], P('dp', None, 'mp')
- grad_gain_first: float32 [2048], replicated
- grad_gain_second: float32 [2048], replicated
- grad_query: float32 [2048, 2048], P('dp', 'mp')
- grad_out: float32 [2048, 2048], P('mp', 'dp')
- grad_gate: float32 [2048, 5504], P('dp', 'mp')
- grad_up: float32 [2048, 5504], P('dp', 'mp')
- grad_down: float32 [5504, 2048], P('mp', 'dp')
Inputs may be any that keep to these rules, and one draw needn't show every extreme that they name: `segment_ids`: along each sequence the id never falls; each of the 16 documents holds 1 to 512 tokens, and one holds exactly 512.
All inputs are finite; a program needn't handle non-finite values.
Results may differ from a plain program's by a relative error of at most 0.017.
Values may be sent and summed in bfloat16 or wider, within the bound.
A program may use at most 192 MiB of HBM per device.

v0:
```python
import jax
import jax.numpy as jnp
from jax import lax
from jax.sharding import PartitionSpec as P

HEAD_DIM = 128


epsilon = 1e-06


def contract(left, right, left_dim, right_dim):
    return lax.dot_general(
        left, right, (((left_dim,), (right_dim,)), ((), ())), preferred_element_type=jnp.float32
    )


def root_inverse(values):
    return lax.rsqrt(jnp.mean(values * values, axis=-1, keepdims=True) + epsilon)


def norm_back(grad_normed, scaled, inverse, gain):
    grad_scaled = grad_normed * gain
    grad_values = inverse * (
        grad_scaled - scaled * jnp.mean(grad_scaled * scaled, axis=-1, keepdims=True)
    )
    return (grad_values, jnp.sum(grad_normed * scaled, axis=0))


def body(
    inputs,
    keys_values,
    segment_ids,
    gain_first,
    gain_second,
    w_query,
    w_out,
    w_gate,
    w_up,
    w_down,
    cotangent,
):
    query_full, out_full = (
        lax.all_gather(w_query, "dp", axis=0, tiled=True),
        lax.all_gather(w_out, "dp", axis=1, tiled=True),
    )
    gate_full, up_full, down_full = (
        lax.all_gather(w_gate, "dp", axis=0, tiled=True),
        lax.all_gather(w_up, "dp", axis=0, tiled=True),
        lax.all_gather(w_down, "dp", axis=1, tiled=True),
    )
    tokens = inputs.astype(jnp.float32)
    inverse_first = root_inverse(tokens)
    scaled_first = tokens * inverse_first
    normed_first = (scaled_first * gain_first).astype(jnp.bfloat16)
    rows_first = lax.all_gather(normed_first, "mp", axis=0, tiled=True)
    queries = contract(rows_first, query_full, 1, 0).astype(jnp.bfloat16)
    seq_len = rows_first.shape[0]
    local_width = queries.shape[1]
    head_count = local_width // HEAD_DIM
    block_rows = min(512, seq_len)
    block_count = seq_len // block_rows
    score_scale = HEAD_DIM ** (-0.5)
    key_heads = keys_values[:, 0, :].reshape(seq_len, head_count, HEAD_DIM)
    value_heads = keys_values[:, 1, :].reshape(seq_len, head_count, HEAD_DIM)
    segments = segment_ids[0]
    key_pos = jnp.arange(seq_len, dtype=jnp.int32)

    def block_scores(first_row):
        query_block = lax.dynamic_slice_in_dim(queries, first_row, block_rows, 0).reshape(
            block_rows, head_count, HEAD_DIM
        )
        scores = (
            jnp.einsum("qhd,khd->hqk", query_block, key_heads, preferred_element_type=jnp.float32)
            * score_scale
        )
        query_pos = first_row + jnp.arange(block_rows, dtype=jnp.int32)
        query_seg = lax.dynamic_slice_in_dim(segments, first_row, block_rows, 0)
        allowed = (query_pos[:, None] >= key_pos[None, :]) & (
            query_seg[:, None] == segments[None, :]
        )
        return (query_block, jnp.where(allowed[None], scores, -1e30))

    def forward_block(block_index):
        query_block, scores = block_scores(block_index * block_rows)
        row_max = jnp.max(scores, axis=-1, keepdims=True)
        raised = jnp.exp(scores - row_max)
        row_total = jnp.sum(raised, axis=-1, keepdims=True)
        weights_low = (raised / row_total).astype(jnp.bfloat16)
        blended = jnp.einsum(
            "hqk,khd->qhd", weights_low, value_heads, preferred_element_type=jnp.float32
        )
        return (
            blended.reshape(block_rows, local_width).astype(jnp.bfloat16),
            (row_max + jnp.log(row_total))[..., 0],
        )

    context_blocks, log_totals = lax.map(forward_block, jnp.arange(block_count, dtype=jnp.int32))
    context = context_blocks.reshape(seq_len, local_width)
    attn_part = lax.psum_scatter(
        contract(context, out_full, 1, 0), "mp", scatter_dimension=0, tiled=True
    )
    residual = tokens + attn_part
    inverse_second = root_inverse(residual)
    scaled_second = residual * inverse_second
    normed_second = (scaled_second * gain_second).astype(jnp.bfloat16)
    rows_second = lax.all_gather(normed_second, "mp", axis=0, tiled=True)
    gate_proj = contract(rows_second, gate_full, 1, 0)
    up_proj = contract(rows_second, up_full, 1, 0)
    sigmoid_gate = jax.nn.sigmoid(gate_proj)
    silu_gate = gate_proj * sigmoid_gate
    hidden = (silu_gate * up_proj).astype(jnp.bfloat16)
    ffn_part = lax.psum_scatter(
        contract(hidden, down_full, 1, 0).astype(jnp.bfloat16),
        "mp",
        scatter_dimension=0,
        tiled=True,
    ).astype(jnp.float32)
    output = (residual + ffn_part).astype(jnp.bfloat16)
    cot_rows = lax.all_gather(cotangent, "mp", axis=0, tiled=True)
    grad_down_w = contract(hidden, cot_rows, 0, 0)
    grad_hidden = contract(cot_rows, down_full, 1, 1)
    grad_gate_act = (
        grad_hidden * up_proj * sigmoid_gate * (1.0 + gate_proj * (1.0 - sigmoid_gate))
    ).astype(jnp.bfloat16)
    grad_up_act = (grad_hidden * silu_gate).astype(jnp.bfloat16)
    grad_gate_w = contract(rows_second, grad_gate_act, 0, 0)
    grad_up_w = contract(rows_second, grad_up_act, 0, 0)
    grad_normed_second = lax.psum_scatter(
        contract(grad_gate_act, gate_full, 1, 1) + contract(grad_up_act, up_full, 1, 1),
        "mp",
        scatter_dimension=0,
        tiled=True,
    )
    grad_from_norm, gain_second_part = norm_back(
        grad_normed_second, scaled_second, inverse_second, gain_second
    )
    grad_residual = cotangent.astype(jnp.float32) + grad_from_norm
    attn_cot = lax.all_gather(grad_residual.astype(jnp.bfloat16), "mp", axis=0, tiled=True)
    grad_out_w = contract(context, attn_cot, 0, 0)
    grad_context = contract(attn_cot, out_full, 1, 1).astype(jnp.bfloat16)

    def backward_block(state_pair, block_index):
        grad_keys, grad_values = state_pair
        first_row = block_index * block_rows
        query_block, scores = block_scores(first_row)
        log_total = lax.dynamic_index_in_dim(log_totals, block_index, 0, keepdims=False)
        weights = jnp.exp(scores - log_total[..., None])
        grad_block = lax.dynamic_slice_in_dim(grad_context, first_row, block_rows, 0).reshape(
            block_rows, head_count, HEAD_DIM
        )
        grad_weights = jnp.einsum(
            "qhd,khd->hqk", grad_block, value_heads, preferred_element_type=jnp.float32
        )
        spread = jnp.sum(weights * grad_weights, axis=-1, keepdims=True)
        grad_scores = (weights * (grad_weights - spread)).astype(jnp.bfloat16)
        grad_query_block = (
            jnp.einsum("hqk,khd->qhd", grad_scores, key_heads, preferred_element_type=jnp.float32)
            * score_scale
        ).astype(jnp.bfloat16)
        grad_keys = (
            grad_keys
            + jnp.einsum(
                "hqk,qhd->khd", grad_scores, query_block, preferred_element_type=jnp.float32
            )
            * score_scale
        )
        grad_values = grad_values + jnp.einsum(
            "hqk,qhd->khd",
            weights.astype(jnp.bfloat16),
            grad_block,
            preferred_element_type=jnp.float32,
        )
        return ((grad_keys, grad_values), grad_query_block.reshape(block_rows, local_width))

    zero_state = jnp.zeros((seq_len, head_count, HEAD_DIM), jnp.float32)
    (grad_keys, grad_values), grad_query_blocks = lax.scan(
        backward_block, (zero_state, zero_state), jnp.arange(block_count, dtype=jnp.int32)
    )
    grad_queries = grad_query_blocks.reshape(seq_len, local_width)
    grad_kv = jnp.stack(
        [grad_keys.reshape(seq_len, local_width), grad_values.reshape(seq_len, local_width)], axis=1
    )
    grad_query_w = contract(rows_first, grad_queries, 0, 0)
    grad_normed_first = lax.psum_scatter(
        contract(grad_queries, query_full, 1, 1).astype(jnp.bfloat16),
        "mp",
        scatter_dimension=0,
        tiled=True,
    ).astype(jnp.float32)
    grad_from_first, gain_first_part = norm_back(
        grad_normed_first, scaled_first, inverse_first, gain_first
    )
    grad_input = grad_residual + grad_from_first
    gain_first_sum, gain_second_sum = lax.psum((gain_first_part, gain_second_part), ("dp", "mp"))
    query_shard, out_shard, gate_shard, up_shard, down_shard = (
        lax.psum_scatter(
            grad_query_w.astype(jnp.bfloat16), "dp", scatter_dimension=0, tiled=True
        ).astype(jnp.float32),
        lax.psum_scatter(
            grad_out_w.astype(jnp.bfloat16), "dp", scatter_dimension=1, tiled=True
        ).astype(jnp.float32),
        lax.psum_scatter(
            grad_gate_w.astype(jnp.bfloat16), "dp", scatter_dimension=0, tiled=True
        ).astype(jnp.float32),
        lax.psum_scatter(
            grad_up_w.astype(jnp.bfloat16), "dp", scatter_dimension=0, tiled=True
        ).astype(jnp.float32),
        lax.psum_scatter(
            grad_down_w.astype(jnp.bfloat16), "dp", scatter_dimension=1, tiled=True
        ).astype(jnp.float32),
    )
    return (
        output,
        grad_input,
        grad_kv,
        gain_first_sum,
        gain_second_sum,
        query_shard,
        out_shard,
        gate_shard,
        up_shard,
        down_shard,
    )


def solution(mesh):
    in_specs = (
        P(("dp", "mp"), None),
        P("dp", None, "mp"),
        P("dp", None),
        P(),
        P(),
        P("dp", "mp"),
        P("mp", "dp"),
        P("dp", "mp"),
        P("dp", "mp"),
        P("mp", "dp"),
        P(("dp", "mp"), None),
    )
    out_specs = (
        P(("dp", "mp"), None),
        P(("dp", "mp"), None),
        P("dp", None, "mp"),
        P(),
        P(),
        P("dp", "mp"),
        P("mp", "dp"),
        P("dp", "mp"),
        P("dp", "mp"),
        P("mp", "dp"),
    )
    return jax.shard_map(body, mesh=mesh, in_specs=in_specs, out_specs=out_specs, check_vma=False)
```

profile of v0, /device:TPU:0, one launch (start us, length us, event | category | flops | bytes accessed | tf_op | source)
XLA Modules:
  0.0 1317.7 jit_solution(3761415516102076378)
XLA Ops:
  27.4 13.1 all-gather.12.cloned.1.call-done
  40.5 82.9 %all-gather.10.cloned.1.call-done = bf16[1024,2048]{1,0:T(8,128)(2,1)} async-done(((bf16[256,2048]{1,0:T(8,128)(2,1)}), bf16[1024,2048]{1,0:T(8,128)(2,1)}) %all-gather.10.cloned.1.call-update) | async-done | bytes 4194320 | tf_op jit(solution)/shard_map/all_gather | solution.py:56
  133.0 23.4 %while.28 = (s32[]{:T(128)}, bf16[2,512,512]{2,1,0:T(8,128)(2,1)}, f32[2,4,512]{2,1,0:T(4,128)S(1)}, s32[2]{0:T(128)S(1)}, s32[1024]{0:T(1024)S(1)}, /*index=5*/...) while((s32[]{:T(128)}, bf16[2,512,512]{2,1,0:T(8,128)(2,1)}, ...), condition=%wide.region_4.5_spmd.clone, body=%wide.region_1.4_spmd.clone.sunk | while | flops 1100741120 | bytes 33634516 | solution.py:98
  156.4 7.9 fusion.39
  165.0 142.5 %reduce-scatter.10.cloned.1.call-done = f32[256,2048]{1,0:T(8,128)} async-done(((f32[1024,2048]{1,0:T(8,128)}), f32[256,2048]{1,0:T(8,128)}) %reduce-scatter.10.cloned.1.call-update) | async-done | bytes 2097168 | tf_op jit(solution)/shard_map/reduce_scatter | solution.py:100
  313.4 40.3 %all-gather.20.cloned.1.call-done = bf16[2048,1376]{0,1:T(8,128)(2,1)} async-done(((bf16[256,1376]{0,1:T(8,128)(2,1)}), bf16[2048,1376]{0,1:T(8,128)(2,1)}) %all-gather.20.cloned.1.call-update) | async-done | bytes 5636112 | tf_op jit(solution)/shard_map/all_gather | solution.py:49
  353.8 82.8 %all-gather.16.cloned.1.call-done = bf16[1024,2048]{1,0:T(8,128)(2,1)} async-done(((bf16[256,2048]{1,0:T(8,128)(2,1)}), bf16[1024,2048]{1,0:T(8,128)(2,1)}) %all-gather.16.cloned.1.call-update) | async-done | bytes 4194320 | tf_op jit(solution)/shard_map/all_gather | solution.py:107
  436.5 10.9 fusion.41
  447.5 33.3 %all-gather.18.cloned.1.call-done = bf16[2048,1376]{0,1:T(8,128)(2,1)} async-done(((bf16[256,1376]{0,1:T(8,128)(2,1)}), bf16[2048,1376]{0,1:T(8,128)(2,1)}) %all-gather.18.cloned.1.call-update) | async-done | bytes 5636112 | tf_op jit(solution)/shard_map/all_gather | solution.py:48
  480.8 10.9 fusion.40
  491.7 71.5 %all-gather.24.cloned.1.call-done = bf16[1024,2048]{1,0:T(8,128)(2,1)} async-done(((bf16[256,2048]{1,0:T(8,128)(2,1)}), bf16[1024,2048]{1,0:T(8,128)(2,1)}) %all-gather.24.cloned.1.call-update) | async-done | bytes 4194320 | tf_op jit(solution)/shard_map/all_gather | solution.py:120
  563.1 44.2 %all-gather.22.cloned.1.call-done = bf16[1376,2048]{1,0:T(8,128)(2,1)} async-done(((bf16[1376,256]{1,0:T(8,128)(2,1)}), bf16[1376,2048]{1,0:T(8,128)(2,1)}) %all-gather.22.cloned.1.call-update) | async-done | bytes 5636112 | tf_op jit(solution)/shard_map/all_gather | solution.py:50
  607.4 15.3 %multiply_convert_fusion.1 = (bf16[1024,1376]{0,1:T(8,128)(2,1)S(1)}, bf16[1024,1376]{0,1:T(8,128)(2,1)S(1)}, bf16[1024,1376]{0,1:T(8,128)(2,1)}) fusion(f32[1024,1376]{0,1:T(8,128)} %fusion.40, f32[1024,1376]{0,1:T(8,128)} %fusion.41, bf16[1024,2048]{1,0:T(8,128)(2,1)} %all-gather.24.cloned.1.call-done, bf16[1376,2048]{1,0:T(8,128)(2,1)} %all-gather.22.cloned.1.call-done), kind=kOutput, calls=%fused_computation.42 | convolution fusion | flops 5792497664 | bytes 29556736 | tf_op jit(solution)/shard_map/dot_general | solution.py:13
  622.7 6.8 fusion.42
  629.5 11.3 convolution_add_fusion
  641.0 144.6 %reduce-scatter.14.cloned.1.call-done = f32[256,2048]{1,0:T(8,128)} async-done(((f32[1024,2048]{1,0:T(8,128)}), f32[256,2048]{1,0:T(8,128)}) %reduce-scatter.14.cloned.1.call-update) | async-done | bytes 2097168 | tf_op jit(solution)/shard_map/reduce_scatter | solution.py:129
  790.7 10.4 convolution_convert_fusion.2
  803.1 9.9 convolution_convert_fusion
  815.5 10.3 convolution_convert_fusion.1
  825.9 46.4 %all-gather.26.cloned.1.call-done = bf16[1024,2048]{1,0:T(8,128)(2,1)} async-done(((bf16[256,2048]{1,0:T(8,128)(2,1)}), bf16[1024,2048]{1,0:T(8,128)(2,1)}) %all-gather.26.cloned.1.call-update) | async-done | bytes 4194320 | tf_op jit(solution)/shard_map/all_gather | solution.py:139
  879.6 51.1 %while.29 = (s32[]{:T(128)}, f32[1024,4,128]{0,2,1:T(8,128)S(1)}, f32[1024,4,128]{0,2,1:T(8,128)}, bf16[2,512,512]{2,1,0:T(8,128)(2,1)}, s32[2]{0:T(128)S(1)}, /...) while((s32[]{:T(128)}, f32[1024,4,128]{0,2,1:T(8,128)S(1)}, ...), condition=%wide.region_12.13_spmd.clone, body=%wide.region_10.12_spmd.clone.sunk | while | flops 2720528896 | bytes 92871008 | solution.py:177
  937.1 6.3 convolution_convert_fusion.5
  943.4 6.3 convolution_convert_fusion.3
  950.1 11.2 convolution_convert_fusion.4
  963.6 31.0 %reduce-scatter.24.cloned.1.call-done = bf16[256,1376]{0,1:T(8,128)(2,1)} async-done(((bf16[2048,1376]{0,1:T(8,128)(2,1)}), bf16[256,1376]{0,1:T(8,128)(2,1)}) %reduce-scatter.24.cloned.1.call-update) | async-done | bytes 704528 | tf_op jit(solution)/shard_map/reduce_scatter | solution.py:206
  996.9 59.5 %reduce-scatter.22.cloned.1.call-done = bf16[256,1376]{0,1:T(8,128)(2,1)} async-done(((bf16[2048,1376]{0,1:T(8,128)(2,1)}), bf16[256,1376]{0,1:T(8,128)(2,1)}) %reduce-scatter.22.cloned.1.call-update) | async-done | bytes 704528 | tf_op jit(solution)/shard_map/reduce_scatter | solution.py:203
  1063.5 8.3 pad_maximum_fusion
  1071.9 28.9 %reduce-scatter.18.cloned.1.call-done = bf16[256,512]{1,0:T(8,128)(2,1)} async-done(((bf16[2048,512]{1,0:T(8,128)(2,1)}), bf16[256,512]{1,0:T(8,128)(2,1)}) %reduce-scatter.18.cloned.1.call-update) | async-done | bytes 262160 | tf_op jit(solution)/shard_map/reduce_scatter | solution.py:197
  1102.6 42.9 %reduce-scatter.20.cloned.1.call-done = bf16[512,256]{1,0:T(8,128)(2,1)} async-done(((bf16[512,2048]{1,0:T(8,128)(2,1)}), bf16[512,256]{1,0:T(8,128)(2,1)}) %reduce-scatter.20.cloned.1.call-update) | async-done | bytes 262160 | tf_op jit(solution)/shard_map/reduce_scatter | solution.py:200
  1147.3 77.2 %reduce-scatter.16.cloned.1.call-done = bf16[256,2048]{1,0:T(8,128)(2,1)} async-done(((bf16[1024,2048]{1,0:T(8,128)(2,1)}), bf16[256,2048]{1,0:T(8,128)(2,1)}) %reduce-scatter.16.cloned.1.call-update) | async-done | bytes 1048592 | tf_op jit(solution)/shard_map/reduce_scatter | solution.py:185
  1226.5 43.0 %all-reduce = (f32[2048]{0:T(1024)}, f32[2048]{0:T(1024)}) all-reduce(f32[2048]{0:T(1024)S(1)} %get-tuple-element.230, f32[2048]{0:T(1024)S(1)} %copy-done.19), channel_id=1, replica_groups=mesh['dp'=8,'mp'=4] {'dp','mp'}, use_global_device_ids=true, to_apply=%region_16.17 | all-reduce | flops 4096 | bytes 32768 | tf_op jit(solution)/shard_map/psum | solution.py:195
  1269.5 35.5 %reduce-scatter.12.cloned.1.call-done = bf16[256,2048]{1,0:T(8,128)(2,1)} async-done(((bf16[1024,2048]{1,0:T(8,128)(2,1)}), bf16[256,2048]{1,0:T(8,128)(2,1)}) %reduce-scatter.12.cloned.1.call-update) | async-done | bytes 1048592 | tf_op jit(solution)/shard_map/reduce_scatter | solution.py:113
  (187 shorter events, 150.1 us)
Async XLA Ops:
  7.2 33.4 %all-gather.12.cloned.1.call-start = ((), (), s32[]{:S(2)}) async-start(), calls=%async_computation.10 | async-start | bytes 2359296 | tf_op jit(solution)/shard_map/all_gather | solution.py:44
  7.9 115.6 %all-gather.10.cloned.1.call-start = ((), (), s32[]{:S(2)}) async-start(), calls=%async_computation.9 | async-start | bytes 5242880 | tf_op jit(solution)/shard_map/all_gather | solution.py:56
  12.6 143.8 %all-gather.14.cloned.1.call-start = ((), (), s32[]{:S(2)}) async-start(), calls=%async_computation.11 | async-start | bytes 2359296 | tf_op jit(solution)/shard_map/all_gather | solution.py:45
  13.3 294.2 %reduce-scatter.10.cloned.1.call-start = ((), (), s32[]{:S(2)}) async-start(), calls=%async_computation.12 | async-start | bytes 10485760 | tf_op jit(solution)/shard_map/reduce_scatter | solution.py:100
  27.4 105.6 %copy-start.15 = (s32[1,1024]{1,0:T(1,128)S(1)}, s32[1,1024]{1,0:T(1,128)}, u32[]{:S(2)}) copy-start(s32[1,1024]{1,0:T(1,128)} %param.17) | copy-start | bytes 12292
  164.3 143.2 %copy-start.5 = (bf16[256,2048]{1,0:T(8,128)(2,1)S(1)}, bf16[256,2048]{1,0:T(8,128)(2,1)}, u32[]{:S(2)}) copy-start(bf16[256,2048]{1,0:T(8,128)(2,1)} %param.15) | copy-start | bytes 3145732
  164.3 145.1 %copy-start.16 = (f32[2048]{0:T(1024)S(1)}, f32[2048]{0:T(1024)}, u32[]{:S(2)}) copy-start(f32[2048]{0:T(1024)} %param.19) | copy-start | bytes 24580
  164.4 189.4 %all-gather.20.cloned.1.call-start = ((), (), s32[]{:S(2)}) async-start(), calls=%async_computation.15 | async-start | bytes 6340608 | tf_op jit(solution)/shard_map/all_gather | solution.py:49
  165.0 271.6 %all-gather.16.cloned.1.call-start = ((), (), s32[]{:S(2)}) async-start(), calls=%async_computation.13 | async-start | bytes 5242880 | tf_op jit(solution)/shard_map/all_gather | solution.py:107
  309.4 479.0 %copy-start = (f32[256,2048]{1,0:T(8,128)}, f32[256,2048]{1,0:T(8,128)S(1)}, u32[]{:S(2)}) copy-start(f32[256,2048]{1,0:T(8,128)S(1)} %get-tuple-element.277) | copy-start | bytes 6291460
  309.5 479.0 %copy-start.20 = (f32[256]{0:T(256)}, f32[256]{0:T(256)S(1)}, u32[]{:S(2)}) copy-start(f32[256]{0:T(256)S(1)} %add_rsqrt_fusion) | copy-start | bytes 3076
  310.9 169.8 %all-gather.18.cloned.1.call-start = ((), (), s32[]{:S(2)}) async-start(), calls=%async_computation.14 | async-start | bytes 6340608 | tf_op jit(solution)/shard_map/all_gather | solution.py:48
  311.7 251.4 %all-gather.24.cloned.1.call-start = ((), (), s32[]{:S(2)}) async-start(), calls=%async_computation.18 | async-start | bytes 5242880 | tf_op jit(solution)/shard_map/all_gather | solution.py:120
  312.4 294.9 %all-gather.22.cloned.1.call-start = ((), (), s32[]{:S(2)}) async-start(), calls=%async_computation.16 | async-start | bytes 6340608 | tf_op jit(solution)/shard_map/all_gather | solution.py:50
  313.2 472.3 %reduce-scatter.14.cloned.1.call-start = ((), (), s32[]{:S(2)}) async-start(), calls=%async_computation.19 | async-start | bytes 10485760 | tf_op jit(solution)/shard_map/reduce_scatter | solution.py:129
  640.9 148.1 %copy-start.8 = (bf16[256,2048]{1,0:T(8,128)(2,1)S(1)}, bf16[256,2048]{1,0:T(8,128)(2,1)}, u32[]{:S(2)}) copy-start(bf16[256,2048]{1,0:T(8,128)(2,1)} %param.25) | copy-start | bytes 3145732
  640.9 231.4 %all-gather.26.cloned.1.call-start = ((), (), s32[]{:S(2)}) async-start(), calls=%async_computation.20 | async-start | bytes 5242880 | tf_op jit(solution)/shard_map/all_gather | solution.py:139
  790.7 170.7 %reduce-scatter.26.cloned.1.call-start = ((), (), s32[]{:S(2)}) async-start(), calls=%async_computation.26 | async-start | bytes 6340608 | tf_op jit(solution)/shard_map/reduce_scatter | solution.py:209
  801.2 193.4 %reduce-scatter.24.cloned.1.call-start = ((), (), s32[]{:S(2)}) async-start(), calls=%async_computation.25 | async-start | bytes 6340608 | tf_op jit(solution)/shard_map/reduce_scatter | solution.py:206
  813.0 243.4 %reduce-scatter.22.cloned.1.call-start = ((), (), s32[]{:S(2)}) async-start(), calls=%async_computation.24 | async-start | bytes 6340608 | tf_op jit(solution)/shard_map/reduce_scatter | solution.py:203
  825.9 274.9 %reduce-scatter.18.cloned.1.call-start = ((), (), s32[]{:S(2)}) async-start(), calls=%async_computation.22 | async-start | bytes 2359296 | tf_op jit(solution)/shard_map/reduce_scatter | solution.py:197
  937.0 208.5 %reduce-scatter.20.cloned.1.call-start = ((), (), s32[]{:S(2)}) async-start(), calls=%async_computation.23 | async-start | bytes 2359296 | tf_op jit(solution)/shard_map/reduce_scatter | solution.py:200
  943.4 281.1 %reduce-scatter.16.cloned.1.call-start = ((), (), s32[]{:S(2)}) async-start(), calls=%async_computation.21 | async-start | bytes 5242880 | tf_op jit(solution)/shard_map/reduce_scatter | solution.py:185
  949.8 355.3 %reduce-scatter.12.cloned.1.call-start = ((), (), s32[]{:S(2)}) async-start(), calls=%async_computation.17 | async-start | bytes 5242880 | tf_op jit(solution)/shard_map/reduce_scatter | solution.py:113
  1063.5 161.0 %copy-start.6 = (bf16[256,2048]{1,0:T(8,128)(2,1)S(1)}, bf16[256,2048]{1,0:T(8,128)(2,1)}, u32[]{:S(2)}) copy-start(bf16[256,2048]{1,0:T(8,128)(2,1)} %param.15) | copy-start | bytes 3145732
  1063.5 161.0 %copy-start.18 = (f32[2048]{0:T(1024)S(1)}, f32[2048]{0:T(1024)}, u32[]{:S(2)}) copy-start(f32[2048]{0:T(1024)} %param.18) | copy-start | bytes 24580
  1063.5 161.0 %copy-start.23 = (f32[256]{0:T(256)S(1)}, f32[256]{0:T(256)}, u32[]{:S(2)}) copy-start(f32[256]{0:T(256)} %copy-done.22) | copy-start | bytes 3076
  1063.5 163.1 %copy-start.19 = (f32[2048]{0:T(1024)S(1)}, f32[2048]{0:T(1024)}, u32[]{:S(2)}) copy-start(f32[2048]{0:T(1024)} %get-tuple-element.228) | copy-start | bytes 24580
  1063.5 241.6 %copy-start.1 = (f32[256,2048]{1,0:T(8,128)S(1)}, f32[256,2048]{1,0:T(8,128)}, u32[]{:S(2)}) copy-start(f32[256,2048]{1,0:T(8,128)} %copy-done) | copy-start | bytes 6291460
  1063.5 241.6 %copy-start.17 = (f32[2048]{0:T(1024)S(1)}, f32[2048]{0:T(1024)}, u32[]{:S(2)}) copy-start(f32[2048]{0:T(1024)} %param.19) | copy-start | bytes 24580
  1063.5 241.6 %copy-start.21 = (f32[256]{0:T(256)S(1)}, f32[256]{0:T(256)}, u32[]{:S(2)}) copy-start(f32[256]{0:T(256)} %copy-done.20) | copy-start | bytes 3076
  1063.5 241.6 %copy-start.25 = (f32[256]{0:T(256)S(1)}, f32[256]{0:T(256)}, u32[]{:S(2)}) copy-start(f32[256]{0:T(256)} %copy-done.24) | copy-start | bytes 3076
  (16 other events, 174.5 us)
Sparse Core Ops, SparseCore 0:
  9.9 30.5 all-gather.11
  42.7 80.7 all-gather.9
  125.4 26.7 all-gather.13
  164.5 142.9 reduce-scatter.9
  309.2 44.4 all-gather.19
  355.7 80.7 all-gather.15
  438.4 42.2 all-gather.17
  482.3 80.7 all-gather.23
  565.0 42.2 all-gather.21
  641.0 144.4 reduce-scatter.13
  790.8 81.4 all-gather.25
  875.6 56.9 reduce-scatter.25
  936.1 58.4 reduce-scatter.23
  997.9 58.4 reduce-scatter.21
  1059.5 41.1 reduce-scatter.17
  1104.3 41.2 reduce-scatter.19
  1147.7 76.7 reduce-scatter.15
  1226.7 78.3 reduce-scatter.11
where the time goes:
time: 1330 us; the launch traced here: 1320 us
  waiting for transfers between devices  981 us (74%)
  matrix products  175 us (13%)
  other arithmetic  49.8 us (4%)
  local copies, waits for them, and re-layouts  46.3 us (3%)
  blocking collectives  43 us (3%)
  between operations  15.1 us (1%)
    reduce_scatter x1, waiting for transfers between devices, body(): lax.psum_scatter(contract(grad_gate_act, gate_full, 1, 1) + contract(grad...  145 us
    reduce_scatter x1, waiting for transfers between devices, body(): lax.psum_scatter(contract(context, out_full, 1, 0), 'mp', scatter_dimensi...  142 us
    dot_general x15, matrix products, contract(): lax.dot_general(left, right, (((left_dim,), (right_dim,)), ((), ())), pre...  136 us
    all_gather x1, waiting for transfers between devices, body(): rows_first = lax.all_gather(normed_first, 'mp', axis=0, tiled=True)  82.9 us
    all_gather x1, waiting for transfers between devices, body(): rows_second = lax.all_gather(normed_second, 'mp', axis=0, tiled=True)  82.8 us
    reduce_scatter x1, waiting for transfers between devices, body(): lax.psum_scatter(contract(grad_queries, query_full, 1, 1).astype(jnp.bflo...  77.2 us
    all_gather x1, waiting for transfers between devices, body(): cot_rows = lax.all_gather(cotangent, 'mp', axis=0, tiled=True)  71.5 us
    reduce_scatter x1, waiting for transfers between devices, body(): lax.psum_scatter(grad_gate_w.astype(jnp.bfloat16), 'dp', scatter_dimensio...  59.5 us
  transfers between devices with their start and end apart: 18, of which 16 were waited for; matrix products, arithmetic and copies ran while one was open for 16% of the time, Pallas kernels for 0%

commit v1 on v0

--- a/solution.py
+++ b/solution.py
@@ -1,12 +1,793 @@
 import jax
 import jax.numpy as jnp
 from jax import lax
+from jax.experimental import pallas as pl
+from jax.experimental.pallas import tpu as pltpu
 from jax.sharding import PartitionSpec as P
 
+f32 = jnp.float32
+bf16 = jnp.bfloat16
 HEAD_DIM = 128
-
-
 epsilon = 1e-06
+MESH = pl.DeviceIdType.MESH
+Z_LOW, Z_HIGH, CORE, SIDE, DEEP = 1, 2, 4, 8, 16
+ANY = pl.BlockSpec(memory_space=pl.ANY)
+VM = pl.BlockSpec(memory_space=pltpu.VMEM)
+
+
+class Place:
+    def __init__(self):
+        self.dp = lax.axis_index("dp")
+        self.mp = lax.axis_index("mp")
+
+    def bit(self, mask):
+        return ((self.dp * 4 + self.mp) // mask) % 2
+
+    def partner(self, mask):
+        flip_dp, flip_mp = mask // 4, mask % 4
+        return (self.flip(self.dp, flip_dp), self.flip(self.mp, flip_mp))
+
+    def flip(self, value, flips):
+        for mask in (1, 2, 4):
+            if flips & mask:
+                value = value + mask - 2 * mask * ((value // mask) % 2)
+        return value
+
+
+class Copies:
+    def __init__(self, place, send_sems, recv_sems, local_sems=None):
+        self.place, self.send_sems, self.recv_sems = place, send_sems, recv_sems
+        self.local_sems = local_sems
+        self.count = 0
+        self.local_count = 0
+        self.pending = []
+
+    def describe(self, source, target, device, slot):
+        return pltpu.make_async_remote_copy(
+            src_ref=source, dst_ref=target, send_sem=self.send_sems.at[slot],
+            recv_sem=self.recv_sems.at[slot], device_id=device, device_id_type=MESH)
+
+    def swap(self, source, target, mask):
+        slot = self.count
+        self.count += 1
+        copy = self.describe(source, target, self.place.partner(mask), slot)
+        copy.start()
+        item = {"copy": copy, "got": False}
+        self.pending.append(item)
+        return item
+
+    def got(self, item):
+        if not item["got"]:
+            item["got"] = True
+            if "get_if" in item:
+                @pl.when(item["get_if"])
+                def _():
+                    item["get"].wait_recv()
+            else:
+                item["copy"].wait_recv()
+
+    def step(self, block, mp_send, mp_get, direction, send_if, get_if):
+        slot = self.count
+        self.count += 1
+        place = self.place
+        other = jnp.clip(place.mp + direction, 0, 3)
+        sent, target = block(mp_send)
+        copy = self.describe(sent, target, (place.dp, other), slot)
+
+        @pl.when(send_if)
+        def _():
+            copy.start()
+        sent2, target2 = block(mp_get)
+        get = self.describe(sent2, target2, (place.dp, other), slot)
+        item = {"copy": copy, "got": False, "send_if": send_if, "get_if": get_if, "get": get}
+        self.pending.append(item)
+        return item
+
+    def local(self, source, target):
+        copy = pltpu.make_async_copy(source, target, self.local_sems.at[self.local_count])
+        self.local_count += 1
+        copy.start()
+        return copy
+
+    def finish(self):
+        for item in self.pending:
+            self.got(item)
+        for item in self.pending:
+            if "send_if" in item:
+                @pl.when(item["send_if"])
+                def _():
+                    item["copy"].wait_send()
+            elif "sent" not in item:
+                item["copy"].wait_send()
+
+
+def greet(place, masks):
+    barrier = pltpu.get_barrier_semaphore()
+    for mask in masks:
+        pl.semaphore_signal(barrier, inc=1, device_id=place.partner(mask), device_id_type=MESH)
+    pl.semaphore_wait(barrier, len(masks))
+
+
+def gather_kernel(first, cot, wq, wo, wg, wu, wd, rows, cots, query, wide, out, gate, up, down,
+                  send_sems, recv_sems, local_sems):
+    place = Place()
+    dp, mp = place.dp, place.mp
+    side, high = place.bit(SIDE), place.bit(Z_HIGH)
+    locals_ = []
+    copies = Copies(place, send_sems, recv_sems, local_sems)
+
+    half = wd.shape[0] // 2
+    blk = wd.shape[1]
+    share = first.shape[0]
+    zrow = wo.shape[0]
+    flip = place.flip
+    greet(place, (1, 2, 3, CORE, SIDE, DEEP))
+
+    locals_.append(copies.local(first, rows.at[pl.ds(mp * share, share), :]))
+    locals_.append(copies.local(cot, cots.at[0:share, :]))
+    locals_.append(copies.local(wq, query.at[pl.ds(dp * blk, blk), :]))
+    locals_.append(copies.local(wo, out.at[pl.ds(mp * zrow, zrow), pl.ds(dp * blk, blk)]))
+    mats = ((wg, gate), (wu, up), (wd, down))
+    for weight, whole in mats:
+        locals_.append(copies.local(weight.at[pl.ds(side * half, half), :],
+                                    whole.at[pl.ds(high * half, half), pl.ds(dp * blk, blk)]))
+
+    zcol = wq.shape[1]
+    locals_.append(copies.local(wq, wide.at[:, pl.ds(mp * zcol, zcol)]))
+    def tile(whole, z, d):
+        return whole.at[pl.ds(z * half, half), pl.ds(d * blk, blk)]
+
+    nchunk = 2
+    chunk = share // nchunk
+
+    def row_block(c, source_is_input):
+        def get(m):
+            target = rows.at[pl.ds(m * share + c * chunk, chunk), :]
+            source = first.at[pl.ds(c * chunk, chunk), :] if source_is_input else target
+            return source, target
+        return get
+
+    def out_block(source_is_input):
+        def get(m):
+            target = out.at[pl.ds(m * zrow, zrow), pl.ds(dp * blk, blk)]
+            return (wo if source_is_input else target), target
+        return get
+
+    def wide_block(source_is_input):
+        def get(m):
+            target = wide.at[:, pl.ds(m * zcol, zcol)]
+            return (wq if source_is_input else target), target
+        return get
+
+    def line(store, step, block_of, key):
+        lead = (key, step)
+        store[("r",) + lead] = copies.step(block_of, mp - (step - 1), mp - step, 1,
+                                           (mp >= step - 1) & (mp < 3), mp >= step)
+        store[("l",) + lead] = copies.step(block_of, mp + (step - 1), mp + step, -1,
+                                           (mp <= 3 - (step - 1)) & (mp > 0), mp <= 3 - step)
+
+    store = {}
+    core = []
+
+    def spread_core(piece):
+        core.append(copies.swap(piece, piece, CORE))
+
+    def arrive(key, step):
+        copies.got(store[("r", key, step)])
+        copies.got(store[("l", key, step)])
+
+    dy = flip(dp, DEEP // 4)
+    dx = flip(dp, SIDE // 4)
+    dxy = flip(dy, SIDE // 4)
+    own_piece = [weight.at[pl.ds(side * half, half), :] for weight, _ in mats]
+    zhop = [[], [], []]
+    yhop = [[], [], []]
+
+    def send_z(i, source, d):
+        zhop[i].append(copies.swap(source, tile(mats[i][1], high, d), Z_HIGH))
+
+    def send_y(i, source, z, d):
+        yhop[i].append((copies.swap(source, tile(mats[i][1], z, d), DEEP), z, flip(d, DEEP // 4)))
+
+    line(store, 1, out_block(True), "o")
+    send_z(0, own_piece[0], dp)
+    xhop = [copies.swap(weight.at[pl.ds((1 - side) * half, half), :], tile(whole, high, dp), SIDE)
+            for weight, whole in mats]
+    wq_y = copies.swap(wq, query.at[pl.ds(dp * blk, blk), :], DEEP)
+    for i in range(3):
+        send_y(i, own_piece[i], high, dp)
+    wq_x = [copies.swap(wq, query.at[pl.ds(dp * blk, blk), :], SIDE)]
+    for i in range(3):
+        core.append(copies.swap(own_piece[i], tile(mats[i][1], high, dp), CORE))
+    spread_wq = [copies.swap(wq, query.at[pl.ds(dp * blk, blk), :], CORE)]
+    copies.got(wq_y)
+    piece = query.at[pl.ds(dy * blk, blk), :]
+    wq_x.append(copies.swap(piece, piece, SIDE))
+    spread_core(piece)
+    cot_x = copies.swap(cot, cots.at[share:2 * share, :], SIDE)
+    arrive("o", 1)
+    line(store, 2, out_block(False), "o")
+    send_z(1, own_piece[1], dp)
+    arrive("o", 2)
+    line(store, 3, out_block(False), "o")
+    send_z(2, own_piece[2], dp)
+    for c in range(nchunk):
+        line(store, 1, row_block(c, True), c)
+    for i in range(3):
+        copies.got(xhop[i])
+        piece = tile(mats[i][1], high, dx)
+        send_y(i, piece, high, dx)
+        send_z(i, piece, dx)
+        spread_core(piece)
+    for item, d in zip(wq_x, (dx, dxy)):
+        copies.got(item)
+        spread_core(query.at[pl.ds(d * blk, blk), :])
+    arrive("o", 3)
+    for copy in locals_:
+        copy.wait()
+
+    def columns(d):
+        return out.at[:, pl.ds(d * blk, blk)]
+
+    out_y = copies.swap(columns(dp), columns(dp), DEEP)
+    out_x = [copies.swap(columns(dp), columns(dp), SIDE)]
+    spread_core(columns(dp))
+    for i in range(3):
+        copies.got(zhop[i][0])
+        piece = tile(mats[i][1], 1 - high, dp)
+        send_y(i, piece, 1 - high, dp)
+        spread_core(piece)
+    line(store, 1, wide_block(True), "w")
+    for c in range(nchunk):
+        arrive(c, 1)
+        line(store, 2, row_block(c, False), c)
+    copies.got(out_y)
+    out_x.append(copies.swap(columns(dy), columns(dy), SIDE))
+    spread_core(columns(dy))
+    cot_z = copies.swap(cot, cots.at[2 * share:3 * share, :], Z_LOW)
+    for i in range(3):
+        copies.got(zhop[i][1])
+        piece = tile(mats[i][1], 1 - high, dx)
+        send_y(i, piece, 1 - high, dx)
+        spread_core(piece)
+    arrive("w", 1)
+    line(store, 2, wide_block(False), "w")
+    for c in range(nchunk):
+        arrive(c, 2)
+        line(store, 3, row_block(c, False), c)
+    arrive("w", 2)
+    line(store, 3, wide_block(False), "w")
+    copies.got(out_x[0])
+    spread_core(columns(dx))
+    copies.got(cot_z)
+    cot_xz = copies.swap(cots.at[2 * share:3 * share, :], cots.at[3 * share:4 * share, :], SIDE)
+    for j in range(4):
+        for i in range(3):
+            item, z, d = yhop[i][j]
+            copies.got(item)
+            spread_core(tile(mats[i][1], z, d))
+    copies.got(out_x[1])
+    spread_core(columns(dxy))
+    copies.finish()
+
+
+def gather_call(first, cot, wq, wo, wg, wu, wd):
+    share, width = first.shape
+    hidden = wd.shape[0]
+    shapes = (
+        (share * 4, width), (share * 4, width), (width, wq.shape[1]), (wq.shape[0], width), (width, width),
+        (hidden, width), (hidden, width), (hidden, width),
+    )
+    return pl.pallas_call(
+        gather_kernel,
+        out_shape=tuple(jax.ShapeDtypeStruct(s, bf16) for s in shapes),
+        in_specs=[VM] * 7,
+        out_specs=(ANY,) * 8,
+        scratch_shapes=[pltpu.SemaphoreType.DMA((110,)), pltpu.SemaphoreType.DMA((110,)),
+                        pltpu.SemaphoreType.DMA((9,))],
+        compiler_params=pltpu.CompilerParams(collective_id=1, has_side_effects=True, vmem_limit_bytes=16 << 20),
+        name="gather_all",
+    )(first, cot, wq, wo, wg, wu, wd)
+
+DMA = pltpu.SemaphoreType.DMA
+
+
+def params(ident, vmem=32 << 20):
+    return pltpu.CompilerParams(collective_id=ident, has_side_effects=True, vmem_limit_bytes=vmem)
+
+
+def tokens_kernel(heads, query_y, query_0, query_x, own, whole, send_sems, recv_sems, local_sems):
+    place = Place()
+    mp, dp = place.mp, place.dp
+    share, local = own.shape[0], heads.shape[1]
+    blk = query_0.shape[0]
+    copies = Copies(place, send_sems, recv_sems, local_sems)
+    dy = place.flip(dp, 4)
+    dx = place.flip(dp, 2)
+    dxy = place.flip(dy, 2)
+
+    def rows(d):
+        return whole.at[pl.ds(d * blk, blk), :]
+
+    greet(place, (1, 2, 3, SIDE, CORE))
+    across = copies.swap(query_y, rows(dy), SIDE)
+    for mask in (2, 3, 1):
+        other = place.partner(mask)[1]
+        copies.swap(heads.at[pl.ds(other * share, share), :], own.at[:, pl.ds(mp * local, local)], mask)
+    held = [copies.local(query_0, rows(dp)), copies.local(query_y, rows(dy)), copies.local(query_x, rows(dx))]
+    copies.swap(query_0, rows(dp), CORE)
+    copies.swap(query_y, rows(dy), CORE)
+    copies.swap(query_x, rows(dx), CORE)
+    own[:, pl.ds(mp * local, local)] = heads[pl.ds(mp * share, share), :]
+    for copy in held:
+        copy.wait()
+    copies.got(across)
+    copies.swap(rows(dxy), rows(dxy), CORE)
+    copies.finish()
+
+
+def tokens_hop_kernel(heads, block, own, hopped, send_sems, recv_sems):
+    place = Place()
+    mp = place.mp
+    share, local = own.shape[0], heads.shape[1]
+    greet(place, (1, 2, 3, DEEP))
+    copies = Copies(place, send_sems, recv_sems)
+    for mask in (2, 3, 1):
+        other = place.partner(mask)[1]
+        copies.swap(heads.at[pl.ds(other * share, share), :], own.at[:, pl.ds(mp * local, local)], mask)
+    copies.swap(block, hopped, DEEP)
+    own[:, pl.ds(mp * local, local)] = heads[pl.ds(mp * share, share), :]
+    copies.finish()
+
+
+def heads_hop_kernel(own, block, heads, hopped, send_sems, recv_sems):
+    place = Place()
+    mp = place.mp
+    share, local = own.shape[0], heads.shape[1]
+    greet(place, (1, 2, 3, SIDE))
+    copies = Copies(place, send_sems, recv_sems)
+    for mask in (2, 3, 1):
+        other = place.partner(mask)[1]
+        copies.swap(own.at[:, pl.ds(other * local, local)], heads.at[pl.ds(mp * share, share), :], mask)
+    copies.swap(block, hopped, SIDE)
+    heads[pl.ds(mp * share, share), :] = own[:, pl.ds(mp * local, local)]
+    copies.finish()
+
+
+def to_tokens(heads, block, ident):
+    shape = (heads.shape[0] // 4, heads.shape[1] * 4)
+    return pl.pallas_call(
+        tokens_hop_kernel,
+        out_shape=(jax.ShapeDtypeStruct(shape, bf16), jax.ShapeDtypeStruct(block.shape, bf16)),
+        in_specs=[VM, VM], out_specs=(VM, VM),
+        scratch_shapes=[DMA((4,)), DMA((4,))], compiler_params=params(ident), name="to_tokens")(heads, block)
+
+
+def to_tokens_last(heads, query_y, query_0, query_x, ident):
+    shape = (heads.shape[0] // 4, heads.shape[1] * 4)
+    width = query_0.shape[1]
+    return pl.pallas_call(
+        tokens_kernel,
+        out_shape=(jax.ShapeDtypeStruct(shape, bf16), jax.ShapeDtypeStruct((width, width), bf16)),
+        in_specs=[VM] * 4, out_specs=(VM, ANY),
+        scratch_shapes=[DMA((8,)), DMA((8,)), DMA((3,))], compiler_params=params(ident),
+        name="to_tokens_last")(heads, query_y, query_0, query_x)
+
+
+def to_heads(own, block, ident):
+    shape = (own.shape[0] * 4, own.shape[1] // 4)
+    return pl.pallas_call(
+        heads_hop_kernel,
+        out_shape=(jax.ShapeDtypeStruct(shape, bf16), jax.ShapeDtypeStruct(block.shape, bf16)),
+        in_specs=[VM, VM], out_specs=(VM, VM),
+        scratch_shapes=[DMA((4,)), DMA((4,))], compiler_params=params(ident), name="to_heads")(own, block)
+
+
+def quad_gather_kernel(own, rows, send_sems, recv_sems):
+    place = Place()
+    share = own.shape[0]
+    half = share // 2
+    greet(place, (Z_LOW, SIDE))
+    copies = Copies(place, send_sems, recv_sems)
+    a, b = pl.ds(0, half), pl.ds(half, half)
+
+    def at(quarter, part):
+        return rows.at[pl.ds(quarter * share + part * half, half), :]
+
+    low_a = copies.swap(own.at[a, :], at(2, 0), Z_LOW)
+    side_b = copies.swap(own.at[b, :], at(1, 1), SIDE)
+    low_b = copies.swap(own.at[b, :], at(2, 1), Z_LOW)
+    side_a = copies.swap(own.at[a, :], at(1, 0), SIDE)
+    rows[0:share, :] = own[...]
+    copies.got(low_a)
+    copies.swap(at(2, 0), at(3, 0), SIDE)
+    copies.got(side_b)
+    copies.swap(at(1, 1), at(3, 1), Z_LOW)
+    copies.finish()
+
+
+def quad_gather(own, ident):
+    return pl.pallas_call(
+        quad_gather_kernel, out_shape=jax.ShapeDtypeStruct((own.shape[0] * 4, own.shape[1]), bf16),
+        in_specs=[VM], out_specs=VM, scratch_shapes=[DMA((6,)), DMA((6,))],
+        compiler_params=params(ident), name="quad_gather")(own)
+
+
+def add_into(target, rows, *others, step=32):
+    start, count = rows
+    pieces = count // step
+
+    def one(i, carry):
+        total = target[pl.ds(start + i * step, step), :].astype(f32)
+        for other in others:
+            total = total + other[pl.ds(i * step, step), :].astype(f32)
+        target[pl.ds(start + i * step, step), :] = total.astype(target.dtype)
+        return carry
+
+    lax.fori_loop(0, pieces, one, 0)
+
+
+class QuadReduce:
+    def __init__(self, copies, parts, relay, landed):
+        self.copies, self.parts, self.relay, self.landed = copies, parts, relay, landed
+        self.share = parts.shape[0] // 4
+        self.half = self.share // 2
+
+    def start(self):
+        share, half = self.share, self.half
+        self.first = self.copies.swap(self.parts.at[pl.ds(3 * share, half), :], self.relay.at[0], SIDE)
+        self.second = self.copies.swap(self.parts.at[pl.ds(3 * share + half, half), :], self.relay.at[1], Z_LOW)
+        self.side = [self.copies.swap(self.parts.at[pl.ds(share, half), :], self.landed.at[0, pl.ds(0, half), :], SIDE)]
+        self.low = [self.copies.swap(self.parts.at[pl.ds(2 * share + half, half), :], self.landed.at[1, pl.ds(half, half), :], Z_LOW)]
+
+    def relayed(self):
+        share, half = self.share, self.half
+        self.copies.got(self.first)
+        add_into(self.parts, (2 * share, half), self.relay.at[0])
+        self.low.append(self.copies.swap(self.parts.at[pl.ds(2 * share, half), :], self.landed.at[1, pl.ds(0, half), :], Z_LOW))
+        self.copies.got(self.second)
+        add_into(self.parts, (share + half, half), self.relay.at[1])
+        self.side.append(self.copies.swap(self.parts.at[pl.ds(share + half, half), :], self.landed.at[0, pl.ds(half, half), :], SIDE))
+
+    def arrived(self):
+        for item in self.side + self.low:
+            self.copies.got(item)
+
+
+def quad_reduce_kernel(parts_in, total, parts, relay, landed, send_sems, recv_sems, local_sem):
+    place = Place()
+    load = pltpu.make_async_copy(parts_in, parts, local_sem)
+    load.start()
+    greet(place, (Z_LOW, SIDE))
+    copies = Copies(place, send_sems, recv_sems)
+    load.wait()
+    reduce = QuadReduce(copies, parts, relay, landed)
+    reduce.start()
+    reduce.relayed()
+    reduce.arrived()
+    share = total.shape[0]
+
+    def one(i, carry):
+        here = pl.ds(i * 32, 32)
+        total[here, :] = (parts[here, :].astype(f32) + landed[0, here, :].astype(f32)
+                          + landed[1, here, :].astype(f32))
+        return carry
+
+    lax.fori_loop(0, share // 32, one, 0)
+    copies.finish()
+
+
+def quad_reduce(parts, ident):
+    share, width = parts.shape[0] // 4, parts.shape[1]
+    return pl.pallas_call(
+        quad_reduce_kernel, out_shape=jax.ShapeDtypeStruct((share, width), f32),
+        in_specs=[ANY], out_specs=VM,
+        scratch_shapes=[pltpu.VMEM((share * 4, width), bf16), pltpu.VMEM((2, share // 2, width), bf16),
+                        pltpu.VMEM((2, share, width), bf16), DMA((6,)), DMA((6,)), DMA],
+        compiler_params=params(ident), name="quad_reduce")(parts)
+
+
+def reduce_kernel(gd, gg, gu, go, gq, parts_in, gains_in, down, gate, up, out, query, total, gains,
+                  own_f, core_f, deep_f, high_f, side_f, own_o, core_o, side_o, deep_o, z_o,
+                  own_q, core_q, side_q, deep_q, parts, relay, landed, gains_got,
+                  send_sems, recv_sems, local_sems):
+    place = Place()
+    dp, mp = place.dp, place.mp
+    flip = place.flip
+    high = place.bit(Z_HIGH)
+    side = place.bit(SIDE)
+    blk = down.shape[1]
+    hidden = down.shape[0]
+    half = hidden // 2
+    share = total.shape[0]
+    zrow = out.shape[0]
+    spots = ((0, 0), (0, 1), (1, 0), (1, 1))
+    copies = Copies(place, send_sems, recv_sems, local_sems)
+    mats = (gd, gg, gu)
+
+    def place_of(spot, core):
+        return flip(flip(flip(dp, 4 * spot[0]), 2 * spot[1]), core)
+
+    def cols(array, d):
+        return array.at[:, pl.ds(d * blk, blk)]
+
+    def brows(array, d):
+        return array.at[pl.ds(d * blk, blk), :]
+
+    loads_f = [[copies.local(cols(m, place_of(s, 0)), own_f.at[i, j]) for j, s in enumerate(spots)]
+               for i, m in enumerate(mats)]
+    loads_o = [copies.local(cols(go, place_of(s, 0)), own_o.at[j]) for j, s in enumerate(spots)]
+    loads_q = [copies.local(brows(gq, place_of(s, 0)), own_q.at[j]) for j, s in enumerate(spots)]
+    load_p = copies.local(parts_in, parts)
+    greet(place, (1, 2, 3, CORE, SIDE, DEEP))
+    gains[...] = gains_in[...]
+    gain_masks = [1, 2, CORE, SIDE, DEEP]
+    gain_state = {"item": None, "at": 0}
+
+    def gain_hop():
+        if gain_state["item"] is not None:
+            copies.got(gain_state["item"])
+            copies_wait_send(gain_state["item"])
+            gains[...] = gains[...] + gains_got[gain_state["at"] - 1]
+            gain_state["item"] = None
+        if gain_state["at"] < len(gain_masks):
+            gain_state["item"] = copies.swap(gains, gains_got.at[gain_state["at"]], gain_masks[gain_state["at"]])
+            gain_state["at"] += 1
+
+    def copies_wait_send(item):
+        item["copy"].wait_send()
+        item["sent"] = True
+
+    order = ((1, 0), (1, 1), (0, 0), (0, 1))
+    index = {s: j for j, s in enumerate(spots)}
+    core_in = []
+    for i, m in enumerate(mats):
+        core_in.append({s: copies.swap(cols(m, place_of(s, 1)), core_f.at[i, index[s]], CORE) for s in order})
+    order_o = ((0, 1), (1, 1), (0, 0), (1, 0))
+    core_in_o = {s: copies.swap(cols(go, place_of(s, 1)), core_o.at[index[s]], CORE) for s in order_o}
+    core_in_q = {s: copies.swap(brows(gq, place_of(s, 1)), core_q.at[index[s]], CORE) for s in order_o}
+    gain_hop()
+    load_p.wait()
+    reduce = QuadReduce(copies, parts, relay, landed)
+    deep_in = []
+    for i in range(3):
+        sent = {}
+        for s in order:
+            j = index[s]
+            copies.got(core_in[i][s])
+            loads_f[i][j].wait()
+            add_into(own_f.at[i, j], (0, hidden), core_f.at[i, j])
+            if s[0]:
+                sent[s[1]] = copies.swap(own_f.at[i, j], deep_f.at[i, s[1]], DEEP)
+        deep_in.append(sent)
+        if i == 0:
+            reduce.start()
+        gain_hop()
+    side_in_o, side_in_q = {}, {}
+    for s in order_o:
+        j = index[s]
+        copies.got(core_in_q[s])
+        loads_q[j].wait()
+        add_into(own_q.at[j], (0, blk), core_q.at[j])
+        if s[1]:
+            side_in_q[s[0]] = copies.swap(own_q.at[j], side_q.at[s[0]], SIDE)
+    for s in order_o:
+        j = index[s]
+        copies.got(core_in_o[s])
+        loads_o[j].wait()
+        add_into(own_o.at[j], (0, own_o.shape[1]), core_o.at[j])
+        if s[1]:
+            side_in_o[s[0]] = copies.swap(own_o.at[j], side_o.at[s[0]], SIDE)
+    gain_hop()
+    reduce.relayed()
+    gain_hop()
+    high_in = []
+    for i in range(3):
+        sent = {}
+        for x in (1, 0):
+            j = index[(0, x)]
+            copies.got(deep_in[i][x])
+            add_into(own_f.at[i, j], ((1 - high) * half, half), deep_f.at[i, x, pl.ds((1 - high) * half, half), :], step=16)
+            sent[x] = copies.swap(own_f.at[i, j, pl.ds((1 - high) * half, half), :], high_f.at[i, x], Z_HIGH)
+            add_into(own_f.at[i, j], (high * half, half), deep_f.at[i, x, pl.ds(high * half, half), :], step=16)
+        high_in.append(sent)
+    gain_hop()
+    deep_in_q = None
+    deep_in_o = None
+    for y in (1, 0):
+        j = index[(y, 0)]
+        copies.got(side_in_q[y])
+        add_into(own_q.at[j], (0, blk), side_q.at[y])
+        if y:
+            deep_in_q = copies.swap(own_q.at[j], deep_q, DEEP)
+    for y in (1, 0):
+        j = index[(y, 0)]
+        copies.got(side_in_o[y])
+        add_into(own_o.at[j], (0, own_o.shape[1]), side_o.at[y])
+        if y:
+            deep_in_o = copies.swap(own_o.at[j], deep_o, DEEP)
+    copies.got(deep_in_o)
+    add_into(own_o.at[0], (0, own_o.shape[1]), deep_o)
+    z_in = []
+    for n, mask in enumerate((2, 3, 1)):
+        other = place.partner(mask)[1]
+        z_in.append(copies.swap(own_o.at[0, pl.ds(other * zrow, zrow), :], z_o.at[n], mask))
+    side_in = []
+    outs = (down, gate, up)
+    for i in range(3):
+        for x in (1, 0):
+            j = index[(0, x)]
+            copies.got(high_in[i][x])
+            add_into(own_f.at[i, j], (high * half, half), high_f.at[i, x], step=16)
+            if x:
+                side_in.append(copies.swap(own_f.at[i, j, pl.ds(high * half, half), :], side_f.at[i], SIDE))
+    copies.got(deep_in_q)
+    query[...] = own_q[0].astype(f32) + deep_q[...].astype(f32)
+    reduce.arrived()
+
+    def one(i, carry):
+        here = pl.ds(i * 32, 32)
+        total[here, :] = (parts[here, :].astype(f32) + landed[0, here, :].astype(f32)
+                          + landed[1, here, :].astype(f32))
+        return carry
+
+    lax.fori_loop(0, share // 32, one, 0)
+    for item in z_in:
+        copies.got(item)
+
+    def add_z(i, carry):
+        here = pl.ds(i * 32, 32)
+        sum_ = own_o[0, pl.ds(mp * zrow + i * 32, 32), :].astype(f32)
+        for n in range(3):
+            sum_ = sum_ + z_o[n, here, :].astype(f32)
+        out[here, :] = sum_
+        return carry
+
+    lax.fori_loop(0, zrow // 32, add_z, 0)
+    for i in range(3):
+        copies.got(side_in[i])
+
+        def write(n, carry, i=i):
+            here = pl.ds(side * half + n * 16, 16)
+            there = pl.ds((1 - side) * half + n * 16, 16)
+            outs[i][here, :] = own_f[i, 0, pl.ds(high * half + n * 16, 16), :].astype(f32)
+            outs[i][there, :] = side_f[i, pl.ds(n * 16, 16), :].astype(f32)
+            return carry
+
+        lax.fori_loop(0, half // 16, write, 0)
+    copies.finish()
+
+
+def reduce_call(gd, gg, gu, go, gq, parts, gains, ident):
+    hidden, width = gd.shape
+    blk = width // 8
+    half = hidden // 2
+    local = gq.shape[1]
+    share = parts.shape[0] // 4
+    V = pltpu.VMEM
+    return pl.pallas_call(
+        reduce_kernel,
+        out_shape=(jax.ShapeDtypeStruct((hidden, blk), f32),) * 3
+        + (jax.ShapeDtypeStruct((width // 4, blk), f32), jax.ShapeDtypeStruct((blk, local), f32),
+           jax.ShapeDtypeStruct((share, width), f32), jax.ShapeDtypeStruct(gains.shape, f32)),
+        in_specs=[ANY] * 6 + [VM],
+        out_specs=(VM,) * 7,
+        scratch_shapes=[
+            V((3, 4, hidden, blk), bf16), V((3, 4, hidden, blk), bf16), V((3, 2, hidden, blk), bf16),
+            V((3, 2, half, blk), bf16), V((3, half, blk), bf16),
+            V((4, width, blk), bf16), V((4, width, blk), bf16), V((2, width, blk), bf16), V((width, blk), bf16),
+            V((3, width // 4, blk), bf16),
+            V((4, blk, local), bf16), V((4, blk, local), bf16), V((2, blk, local), bf16), V((blk, local), bf16),
+            V((share * 4, width), bf16), V((2, share // 2, width), bf16), V((2, share, width), bf16),
+            V((5,) + gains.shape, f32),
+            DMA((60,)), DMA((60,)), DMA((24,))],
+        compiler_params=params(ident, 63 << 20), name="reduce_all",
+    )(gd, gg, gu, go, gq, parts, gains)
+ROWS=256
+DOC_MOST=512
+
+
+def dot(left, right, left_dim, right_dim):
+    return lax.dot_general(left, right, (((left_dim,), (right_dim,)), ((), ())), preferred_element_type=f32)
+
+
+def key_range(block, seq_len):
+    low = max(0, block * ROWS - DOC_MOST + 1) // ROWS * ROWS
+    return low, min(seq_len, (block + 1) * ROWS)
+
+
+def scores_turned(q, k, starts, low, first, scale):
+    s = dot(k, q, 1, 1) * scale
+    key_pos = low + lax.broadcasted_iota(jnp.int32, s.shape, 0)
+    query_pos = first + lax.broadcasted_iota(jnp.int32, s.shape, 1)
+    return jnp.where((key_pos >= starts) & (key_pos <= query_pos), s, -1e30)
+
+
+def forward_kernel(starts_ref, q_ref, k_ref, v_ref, ctx_ref, lse_ref):
+    seq_len = q_ref.shape[0]
+    scale = HEAD_DIM ** -0.5
+    for block in range(seq_len // ROWS):
+        low, high = key_range(block, seq_len)
+        here = pl.ds(block * ROWS, ROWS)
+        k = k_ref[low:high, :]
+        v = v_ref[low:high, :]
+        s = scores_turned(q_ref[here, :], k, starts_ref[:, here], low, block * ROWS, scale)
+        top = jnp.max(s, axis=0, keepdims=True)
+        raised = jnp.exp(s - top)
+        total = jnp.sum(raised, axis=0, keepdims=True)
+        low_probs = (raised * (1.0 / total)).astype(bf16)
+        ctx_ref[here, :] = dot(low_probs, v, 0, 0).astype(bf16)
+        lse_ref[0, :, here] = top + jnp.log(total)
+
+
+def backward_kernel(starts_ref, q_ref, k_ref, v_ref, grad_ref, lse_ref, dq_ref, dk_ref, dv_ref):
+    seq_len = q_ref.shape[0]
+    scale = HEAD_DIM ** -0.5
+    for block in range(seq_len // ROWS):
+        low, high = key_range(block, seq_len)
+        here = pl.ds(block * ROWS, ROWS)
+        k = k_ref[low:high, :]
+        v = v_ref[low:high, :]
+        q = q_ref[here, :]
+        grad = grad_ref[here, :]
+        s = scores_turned(q, k, starts_ref[:, here], low, block * ROWS, scale)
+        probs = jnp.exp(s - lse_ref[0, :, here])
+        grad_probs = dot(v, grad, 1, 1)
+        spread = jnp.sum(probs * grad_probs, axis=0, keepdims=True)
+        grad_s = (probs * (grad_probs - spread)).astype(bf16)
+        dq_ref[here, :] = (dot(grad_s, k, 0, 0) * scale).astype(bf16)
+        dk = dot(grad_s, q, 1, 0) * scale
+        dv = dot(probs.astype(bf16), grad, 1, 0)
+        old = max(low, min(high, block * ROWS))
+        if low == 0 and block == 0:
+            dk_ref[low:high, :] = dk
+            dv_ref[low:high, :] = dv
+        else:
+            n = old - low
+            dk_ref[low:old, :] += dk[:n]
+            dv_ref[low:old, :] += dv[:n]
+            dk_ref[old:high, :] = dk[n:]
+            dv_ref[old:high, :] = dv[n:]
+
+
+def specs(seq_len):
+    row = pl.BlockSpec((1, seq_len), lambda h: (0, 0))
+    head = pl.BlockSpec((seq_len, HEAD_DIM), lambda h: (0, h))
+    lse = pl.BlockSpec((1, 1, seq_len), lambda h: (h, 0, 0))
+    return row, head, lse
+
+
+def attend(starts, q, k, v):
+    seq_len, width = q.shape
+    heads = width // HEAD_DIM
+    row, head, lse = specs(seq_len)
+    flops = heads * seq_len * seq_len * HEAD_DIM * 3
+    return pl.pallas_call(
+        forward_kernel, grid=(heads,),
+        in_specs=[row, head, head, head], out_specs=(head, lse),
+        out_shape=(jax.ShapeDtypeStruct(q.shape, bf16), jax.ShapeDtypeStruct((heads, 1, seq_len), f32)),
+        cost_estimate=pl.CostEstimate(flops=flops, bytes_accessed=4 * q.size * 2, transcendentals=heads * seq_len * seq_len // 2),
+        name="attend",
+    )(starts, q, k, v)
+
+
+def attend_back(starts, q, k, v, grad, lse_array):
+    seq_len, width = q.shape
+    heads = width // HEAD_DIM
+    row, head, lse = specs(seq_len)
+    flops = heads * seq_len * seq_len * HEAD_DIM * 7
+    wide = jax.ShapeDtypeStruct(q.shape, f32)
+    return pl.pallas_call(
+        backward_kernel, grid=(heads,),
+        in_specs=[row, head, head, head, head, lse], out_specs=(head, head, head),
+        out_shape=(jax.ShapeDtypeStruct(q.shape, bf16), wide, wide),
+        cost_estimate=pl.CostEstimate(flops=flops, bytes_accessed=9 * q.size * 2, transcendentals=heads * seq_len * seq_len // 2),
+        name="attend_back",
+    )(starts, q, k, v, grad, lse_array)
+
+
+def starts_of(segments):
+    return jnp.sum((segments[0][None, :] < segments[0][:, None]).astype(jnp.int32), axis=1)[None, :]
 
 
 def contract(left, right, left_dim, right_dim):
@@ -27,7 +808,7 @@
     return (grad_values, jnp.sum(grad_normed * scaled, axis=0))
 
 
-def body(
+def plain_body(
     inputs,
     keys_values,
     segment_ids,
@@ -224,6 +1005,72 @@
     )
 
 
+def fast_body(inputs, keys_values, segment_ids, gain_first, gain_second, w_query, w_out, w_gate,
+              w_up, w_down, cotangent):
+    tokens = inputs.astype(f32)
+    inverse_first = root_inverse(tokens)
+    scaled_first = tokens * inverse_first
+    normed_first = (scaled_first * gain_first).astype(bf16)
+    share = inputs.shape[0]
+
+    rows_first, cots, query_part, query_0, out_whole, gate_here, up_here, down_here = gather_call(
+        normed_first, cotangent, w_query, w_out, w_gate.T, w_up.T, w_down)
+
+    queries = contract(rows_first, query_part, 1, 0).astype(bf16)
+    starts = starts_of(segment_ids)
+    keys = keys_values[:, 0, :]
+    values = keys_values[:, 1, :]
+    context, log_totals = attend(starts, queries, keys, values)
+    context_own, query_y = to_tokens(context, query_0, 2)
+    residual = tokens + contract(context_own, out_whole, 1, 0)
+    inverse_second = root_inverse(residual)
+    scaled_second = residual * inverse_second
+    normed_second = (scaled_second * gain_second).astype(bf16)
+    rows = quad_gather(normed_second, 3)
+
+    gate_proj = contract(rows, gate_here, 1, 1)
+    up_proj = contract(rows, up_here, 1, 1)
+    sigmoid_gate = jax.nn.sigmoid(gate_proj)
+    silu_gate = gate_proj * sigmoid_gate
+    hidden = (silu_gate * up_proj).astype(bf16)
+    ffn_parts = contract(hidden, down_here, 1, 0).astype(bf16)
+    grad_hidden = contract(cots, down_here, 1, 1)
+    grad_gate_act = (
+        grad_hidden * up_proj * sigmoid_gate * (1.0 + gate_proj * (1.0 - sigmoid_gate))
+    ).astype(bf16)
+    grad_up_act = (grad_hidden * silu_gate).astype(bf16)
+    grad_parts = (contract(grad_gate_act, gate_here, 1, 0) + contract(grad_up_act, up_here, 1, 0)).astype(bf16)
+    grad_normed_second = quad_reduce(grad_parts, 4)
+    grad_down = contract(hidden, cots, 0, 0).astype(bf16)
+    grad_gate = contract(grad_gate_act, rows, 0, 0).astype(bf16)
+    grad_up = contract(grad_up_act, rows, 0, 0).astype(bf16)
+
+    grad_from_norm, gain_second_part = norm_back(
+        grad_normed_second, scaled_second, inverse_second, gain_second
+    )
+    grad_residual = cotangent.astype(f32) + grad_from_norm
+    grad_low = grad_residual.astype(bf16)
+    grad_context, query_x = to_heads(contract(grad_low, out_whole, 1, 1).astype(bf16), query_0, 5)
+    grad_out = contract(context_own, grad_low, 0, 0).astype(bf16)
+    grad_queries, grad_keys, grad_values = attend_back(
+        starts, queries, keys, values, grad_context, log_totals)
+    grad_kv = jnp.stack([grad_keys, grad_values], axis=1)
+    grad_query = contract(rows_first, grad_queries, 0, 0).astype(bf16)
+    grad_queries_own, query_whole = to_tokens_last(grad_queries, query_y, query_0, query_x, 6)
+    grad_normed_first = contract(grad_queries_own, query_whole, 1, 1)
+    grad_from_first, gain_first_part = norm_back(
+        grad_normed_first, scaled_first, inverse_first, gain_first
+    )
+    grad_input = grad_residual + grad_from_first
+    gains = jnp.stack([gain_first_part, gain_second_part]).reshape(-1, 256)
+    down_shard, gate_shard, up_shard, out_shard, query_shard, ffn_sum, gain_sums = reduce_call(
+        grad_down, grad_gate, grad_up, grad_out, grad_query, ffn_parts, gains, 7)
+    output = (residual + ffn_sum).astype(bf16)
+    gain_sums = gain_sums.reshape(2, -1)
+    return (output, grad_input, grad_kv, gain_sums[0], gain_sums[1], query_shard, out_shard,
+            gate_shard.T, up_shard.T, down_shard)
+
+
 def solution(mesh):
     in_specs = (
         P(("dp", "mp"), None),
@@ -250,4 +1097,6 @@
         P("dp", "mp"),
         P("mp", "dp"),
     )
+    fast = mesh.shape["dp"] == 8 and mesh.shape["mp"] == 4
+    body = fast_body if fast else plain_body
     return jax.shard_map(body, mesh=mesh, in_specs=in_specs, out_specs=out_specs, check_vma=False)

time: 1330 us -> 763 us (0.57)
  waiting for transfers between devices: 981 us -> 0 us
  Pallas kernels: 0 us -> 592 us
  matrix products: 175 us -> 112 us
  blocking collectives: 43 us -> 0 us
  other arithmetic: 49.8 us -> 12.6 us
  between operations: 15.1 us -> 1.61 us
  local copies, waits for them, and re-layouts: 46.3 us -> 32.9 us
    pallas_call x0 -> x9, Pallas kernels: none -> 592 us  [the longest x1 227 us: reduce_call(): pl.pallas_call(reduce_kernel, out_shape=(jax.ShapeDtypeStruct((hidden, bl...]
    reduce_scatter x9 -> x0, waiting for transfers between devices: 562 us -> none  [the longest x1 145 us: body(): lax.psum_scatter(contract(grad_gate_act, gate_full, 1, 1) + contract(grad...]
    all_gather x9 -> x0, waiting for transfers between devices: 415 us -> none  [the longest x1 82.9 us: body(): rows_first = lax.all_gather(normed_first, 'mp', axis=0, tiled=True)]
    psum x1 -> x0, blocking collectives: 43 us -> none  [body(): lax.psum((gain_first_part, gain_second_part), ('dp', 'mp'))]
    dot_general x14 -> x0, matrix products: 38.3 us -> none  [the longest x2 9.33 us: backward_block(): jnp.einsum('hqk,qhd->khd', weights.astype(jnp.bfloat16), grad_block, pref...]
    dot_general x15, matrix products: 136 us -> 112 us  [contract(): lax.dot_general(left, right, (((left_dim,), (right_dim,)), ((), ())), pre...]
    convert_element_type x10 -> x3, other arithmetic: 20.8 us -> 5.37 us  [the longest x1 3.61 us: fast_body(): output = (residual + ffn_sum).astype(bf16)]
    unnamed x56 -> x107, local copies, waits for them, and re-layouts: 13 us -> 27.4 us
  transfers between devices with their start and end apart: 18 -> 0, of which waited for: 16 -> 0; matrix products, arithmetic and copies ran while one was open for 16% -> 0% of each run, Pallas kernels for 0% -> 0%
where the time goes in v1:
time: 763 us; the launch traced here: 751 us
  Pallas kernels  592 us (78%)
  matrix products  112 us (15%)
  local copies, waits for them, and re-layouts  32.9 us (4%)
  other arithmetic  12.6 us (2%)
    pallas_call x1, Pallas kernels, reduce_call(): pl.pallas_call(reduce_kernel, out_shape=(jax.ShapeDtypeStruct((hidden, bl...  227 us
    pallas_call x1, Pallas kernels, gather_call(): pl.pallas_call(gather_kernel, out_shape=tuple((jax.ShapeDtypeStruct(s, bf...  201 us
    dot_general x15, matrix products, contract(): lax.dot_general(left, right, (((left_dim,), (right_dim,)), ((), ())), pre...  112 us
    pallas_call x1, Pallas kernels, quad_gather(): pl.pallas_call(quad_gather_kernel, out_shape=jax.ShapeDtypeStruct((own.sh...  35.2 us
    pallas_call x1, Pallas kernels, quad_reduce(): pl.pallas_call(quad_reduce_kernel, out_shape=jax.ShapeDtypeStruct((share,...  32.1 us
    pallas_call x1, Pallas kernels, to_tokens_last(): pl.pallas_call(tokens_kernel, out_shape=(jax.ShapeDtypeStruct(shape, bf16...  27.5 us
    unnamed x107, local copies, waits for them, and re-layouts  27.4 us
    pallas_call x1, Pallas kernels, to_tokens(): pl.pallas_call(tokens_hop_kernel, out_shape=(jax.ShapeDtypeStruct(shape,...  26.3 us

profile of v1, /device:TPU:0, one launch (start us, length us, event | category | flops | bytes accessed | tf_op | source)
XLA Modules:
  0.0 751.0 jit_solution(9356354880110982744)
XLA Ops:
  5.8 3.0 fusion.14
  8.8 1.9 copy_bitcast_fusion
  11.5 200.9 %gather_all.1 = (bf16[1024,2048]{1,0:T(8,128)(2,1)S(1)}, bf16[1024,2048]{1,0:T(8,128)(2,1)S(1)}, bf16[2048,512]{1,0:T(8,128)(2,1)S(1)}, bf16[256,2048]{1,0:T(8,1...) custom-call(bf16[256,2048]{1,0:T(8,128)(2,1)S(1)} %fusion.5.first, ...), custom_call_target="tpu_custom_call" | custom-call | tf_op jit(solution)/shard_map/gather_all/pallas_call | solution.py:281
  212.4 2.4 copy-done.14
  214.8 2.4 copy-done.15
  217.2 2.5 copy-done.16
  219.6 2.0 copy-done.18
  223.6 3.3 convolution_convert_fusion.7.q_ref
  226.9 8.8 %attend.1 = (bf16[1024,512]{1,0:T(8,128)(2,1)}, f32[4,1,1024]{2,1,0:T(1,128)}) custom-call(s32[1,1024]{1,0:T(1,128)} %bitcast.65, bf16[1024,512]{1,0:T(8,128)(2,1)} %convolution_convert_fusion.7.q_ref, bf16[1024,512]{1,0:T(8,128)(2,1)} %get-tuple-element.97.k_ref, bf16[1024,512]{1,0:T(8,128)(2,1)} %get-tuple-element.96.v_ref), custom_call_target="tpu_custom_call" | custom-call | flops 1610612736 | bytes 4194304 | tf_op jit(solution)/shard_map/attend/pallas_call | solution.py:765
  236.9 26.3 %to_tokens.1 = (bf16[256,2048]{1,0:T(8,128)(2,1)S(1)}, bf16[256,2048]{1,0:T(8,128)(2,1)S(1)}) custom-call(bf16[1024,512]{1,0:T(8,128)(2,1)S(1)} %copy-done.3, bf16[256,2048]{1,0:T(8,128)(2,1)S(1)} %get-tuple-element.39.block.query_0), custom_call_target="tpu_custom_call" | custom-call | tf_op jit(solution)/shard_map/to_tokens/pallas_call | solution.py:359
  263.3 6.5 multiply_reduce_fusion.2
  270.0 35.2 %quad_gather.1 = bf16[1024,2048]{1,0:T(8,128)(2,1)S(1)} custom-call(bf16[256,2048]{1,0:T(8,128)(2,1)S(1)} %multiply_convert_fusion.3.own), custom_call_target="tpu_custom_call" | custom-call | tf_op jit(solution)/shard_map/quad_gather/pallas_call | solution.py:410
  305.3 7.8 %fusion.16 = f32[1024,1376]{0,1:T(8,128)} fusion(bf16[1024,2048]{1,0:T(8,128)(2,1)S(1)} %quad_gather.1, bf16[1376,2048]{1,0:T(8,128)(2,1)S(1)} %bitcast.51), kind=kOutput, calls=%fused_computation.49 | convolution fusion | flops 5771362304 | bytes 15466496 | tf_op jit(solution)/shard_map/dot_general | solution.py:794
  313.1 8.4 %fusion.15 = f32[1024,1376]{0,1:T(8,128)} fusion(bf16[1024,2048]{1,0:T(8,128)(2,1)S(1)} %quad_gather.1, bf16[1376,2048]{1,0:T(8,128)(2,1)S(1)} %bitcast.53), kind=kOutput, calls=%fused_computation.48 | convolution fusion | flops 5771362304 | bytes 15466496 | tf_op jit(solution)/shard_map/dot_general | solution.py:794
  321.5 14.2 %multiply_convert_fusion = (bf16[1024,1376]{0,1:T(8,128)(2,1)}, bf16[1024,1376]{0,1:T(8,128)(2,1)}, bf16[1024,1376]{0,1:T(8,128)(2,1)}) fusion(f32[1024,1376]{0,1:T(8,128)} %fusion.15, f32[1024,1376]{0,1:T(8,128)} %fusion.16, bf16[1024,2048]{1,0:T(8,128)(2,1)} %copy-done.18, bf16[1376,2048]{1,0:T(8,128)(2,1)S(1)} %bitcast.55), kind=kOutput, calls=%fused_computation.5 | convolution fusion | flops 5792497664 | bytes 29556736 | tf_op jit(solution)/shard_map/dot_general | solution.py:794
  335.7 10.4 %convolution_convert_fusion.4.parts_in = bf16[1024,2048]{1,0:T(8,128)(2,1)} fusion(bf16[1024,1376]{0,1:T(8,128)(2,1)} %get-tuple-element.88, bf16[1376,2048]{1,0:T(8,128)(2,1)S(1)} %bitcast.55), kind=kOutput, calls=%fused_computation.12 | convolution fusion | flops 5773459456 | bytes 12648448 | tf_op jit(solution)/shard_map/dot_general | solution.py:794
  346.1 7.9 %convolution_convert_fusion.3.gd = bf16[1376,2048]{1,0:T(8,128)(2,1)} fusion(bf16[1024,1376]{0,1:T(8,128)(2,1)S(1)} %copy-done.40, bf16[1024,2048]{1,0:T(8,128)(2,1)S(1)} %copy-done.19), kind=kOutput, calls=%fused_computation.4 | convolution fusion | flops 5774180352 | bytes 12648448 | tf_op jit(solution)/shard_map/dot_general | solution.py:794
  354.0 9.3 %fusion.17 = f32[1024,2048]{1,0:T(8,128)} fusion(bf16[1024,1376]{0,1:T(8,128)(2,1)S(1)} %copy-done.38, bf16[1376,2048]{1,0:T(8,128)(2,1)S(1)} %bitcast.53), kind=kOutput, calls=%fused_computation.50 | convolution fusion | flops 5771362304 | bytes 16842752 | tf_op jit(solution)/shard_map/dot_general | solution.py:794
  363.4 9.5 %add_convert_fusion.parts_in = bf16[1024,2048]{1,0:T(8,128)(2,1)S(1)} fusion(f32[1024,2048]{1,0:T(8,128)} %fusion.17, bf16[1024,1376]{0,1:T(8,128)(2,1)S(1)} %copy-done.36, bf16[1376,2048]{1,0:T(8,128)(2,1)S(1)} %bitcast.51), kind=kOutput, calls=%fused_computation | convolution fusion | flops 5775556608 | bytes 21037056 | tf_op jit(solution)/shard_map/dot_general | solution.py:794
  372.8 32.1 %quad_reduce.1 = f32[256,2048]{1,0:T(8,128)S(1)} custom-call(bf16[1024,2048]{1,0:T(8,128)(2,1)S(1)} %add_convert_fusion.parts_in), custom_call_target="tpu_custom_call" | custom-call | tf_op jit(solution)/shard_map/quad_reduce/pallas_call | solution.py:482
  407.1 2.4 convolution_convert_fusion.6.own
  409.6 21.0 %to_heads.1 = (bf16[1024,512]{1,0:T(8,128)(2,1)S(1)}, bf16[256,2048]{1,0:T(8,128)(2,1)S(1)}) custom-call(bf16[256,2048]{1,0:T(8,128)(2,1)S(1)} %convolution_convert_fusion.6.own, bf16[256,2048]{1,0:T(8,128)(2,1)S(1)} %get-tuple-element.39.block.query_0), custom_call_target="tpu_custom_call" | custom-call | tf_op jit(solution)/shard_map/to_heads/pallas_call | solution.py:379
  432.5 13.3 %attend_back.1 = (bf16[1024,512]{1,0:T(8,128)(2,1)}, f32[1024,512]{1,0:T(8,128)}, f32[1024,512]{1,0:T(8,128)}) custom-call(s32[1,1024]{1,0:T(1,128)} %bitcast.66, bf16[1024,512]{1,0:T(8,128)(2,1)} %convolution_convert_fusion.7.q_ref, bf16[1024,512]{1,0:T(8,128)(2,1)} %get-tuple-element.97.k_ref, bf16[1024,512]{1,0:T(8,128)(2,1)} %get-tuple-element.96.v_ref, ...), custom_call_target="tpu_custom_call" | custom-call | flops 3758096384 | bytes 9437184 | tf_op jit(solution)/shard_map/attend_back/pallas_call | solution.py:780
  445.8 6.3 convolution_convert_fusion.5.gq
  452.7 5.2 copy.26
  457.9 7.9 %convolution_convert_fusion.1.gu = bf16[1376,2048]{1,0:T(8,128)(2,1)} fusion(bf16[1024,1376]{0,1:T(8,128)(2,1)S(1)} %copy-done.37, bf16[1024,2048]{1,0:T(8,128)(2,1)S(1)} %copy-done.1), kind=kOutput, calls=%fused_computation.2 | convolution fusion | flops 5774180352 | bytes 12648448 | tf_op jit(solution)/shard_map/dot_general | solution.py:794
  465.8 8.2 %convolution_convert_fusion.2.gg = bf16[1376,2048]{1,0:T(8,128)(2,1)} fusion(bf16[1024,1376]{0,1:T(8,128)(2,1)S(1)} %copy-done.39, bf16[1024,2048]{1,0:T(8,128)(2,1)S(1)} %copy-done.1), kind=kOutput, calls=%fused_computation.3 | convolution fusion | flops 5774180352 | bytes 12648448 | tf_op jit(solution)/shard_map/dot_general | solution.py:794
  474.1 27.5 %to_tokens_last.1 = (bf16[256,2048]{1,0:T(8,128)(2,1)S(1)}, bf16[2048,2048]{1,0:T(8,128)(2,1)S(1)}) custom-call(bf16[1024,512]{1,0:T(8,128)(2,1)S(1)} %copy-done.8, bf16[256,2048]{1,0:T(8,128)(2,1)S(1)} %copy-done.5, bf16[256,2048]{1,0:T(8,128)(2,1)S(1)} %get-tuple-element.39.block.query_0, bf16[256,2048]{1,0:T(8,128)(2,1)S(1)} %copy-done.7), custom_call_target="tpu_custom_call" | custom-call | tf_op jit(solution)/shard_map/to_tokens_last/pallas_call | solution.py:369
  501.6 2.7 fusion.7
  506.9 7.3 convolution_convert_fusion.go
  514.1 226.7 %reduce_all.1 = (f32[1376,256]{1,0:T(8,128)}, f32[1376,256]{1,0:T(8,128)}, f32[1376,256]{1,0:T(8,128)}, f32[512,256]{1,0:T(8,128)}, f32[256,512]{1,0:T(8,128)}, /*index=5*/f32[256,2048]{1,0:T(8,128)}, f32[16,256]{1,0:T(8,128)}) custom-call(bf16[1376,2048]{1,0:T(8,128)(2,1)} %convolution_convert_fusion.3.gd, bf16[1376,2048]{1,0:T(8,128)(2,1)} %convolution_convert_fusion.2.gg, ...), custom_call_target="tpu_custom_call" | custom-call | tf_op jit(solution)/shard_map/reduce_all/pallas_call | solution.py:668
  740.8 3.6 add_convert_fusion.1
  (120 shorter events, 22.5 us)
Async XLA Ops:
  0.6 5.1 copy-start.25
  236.9 68.3 %slice-start = ((s8[5636096]{0:T(1024)(128)(4,1)}), s8[4194304]{0:T(1024)(128)(4,1)S(1)}, s32[]{:S(2)}) async-start(s8[5636096]{0:T(1024)(128)(4,1)} %bitcast.50), calls=%async_computation | async-start | bytes 8388608
  263.2 6.5 copy-start.4
  263.2 6.5 copy-start.33
  263.3 42.0 %slice-start.1 = ((s8[5636096]{0:T(1024)(128)(4,1)}), s8[1441792]{0:T(1024)(128)(4,1)S(1)}, s32[]{:S(2)}) async-start(s8[5636096]{0:T(1024)(128)(4,1)} %bitcast.50), calls=%async_computation.1 | async-start | bytes 2883584
  269.7 135.9 %copy-start.21 = (f32[256,2048]{1,0:T(8,128)}, f32[256,2048]{1,0:T(8,128)S(1)}, u32[]{:S(2)}) copy-start(f32[256,2048]{1,0:T(8,128)S(1)} %get-tuple-element.94) | copy-start | bytes 6291460
  270.0 43.1 %slice-start.2 = ((s8[5636096]{0:T(1024)(128)(4,1)}), s8[4194304]{0:T(1024)(128)(4,1)S(1)}, s32[]{:S(2)}) async-start(s8[5636096]{0:T(1024)(128)(4,1)} %bitcast.52), calls=%async_computation.2 | async-start | bytes 8388608
  305.3 7.8 %copy-start = (bf16[1024,2048]{1,0:T(8,128)(2,1)}, bf16[1024,2048]{1,0:T(8,128)(2,1)S(1)}, u32[]{:S(2)}) copy-start(bf16[1024,2048]{1,0:T(8,128)(2,1)S(1)} %quad_gather.1) | copy-start | bytes 12582916
  305.3 7.8 %slice-start.3 = ((s8[5636096]{0:T(1024)(128)(4,1)}), s8[1441792]{0:T(1024)(128)(4,1)S(1)}, s32[]{:S(2)}) async-start(s8[5636096]{0:T(1024)(128)(4,1)} %bitcast.52), calls=%async_computation.3 | async-start | bytes 2883584
  305.3 16.2 %slice-start.4 = ((s8[5636096]{0:T(1024)(128)(4,1)}), s8[4194304]{0:T(1024)(128)(4,1)S(1)}, s32[]{:S(2)}) async-start(s8[5636096]{0:T(1024)(128)(4,1)} %bitcast.54), calls=%async_computation.4 | async-start | bytes 8388608
  313.1 8.4 %slice-start.5 = ((s8[5636096]{0:T(1024)(128)(4,1)}), s8[1441792]{0:T(1024)(128)(4,1)S(1)}, s32[]{:S(2)}) async-start(s8[5636096]{0:T(1024)(128)(4,1)} %bitcast.54), calls=%async_computation.5 | async-start | bytes 2883584
  335.7 10.4 %copy-start.19 = (bf16[1024,2048]{1,0:T(8,128)(2,1)S(1)}, bf16[1024,2048]{1,0:T(8,128)(2,1)}, u32[]{:S(2)}) copy-start(bf16[1024,2048]{1,0:T(8,128)(2,1)} %copy-done.18) | copy-start | bytes 12582916
  335.7 10.4 %copy-start.40 = (bf16[1024,1376]{0,1:T(8,128)(2,1)S(1)}, bf16[1024,1376]{0,1:T(8,128)(2,1)}, u32[]{:S(2)}) copy-start(bf16[1024,1376]{0,1:T(8,128)(2,1)} %get-tuple-element.88) | copy-start | bytes 8454148
  346.1 7.9 %copy-start.38 = (bf16[1024,1376]{0,1:T(8,128)(2,1)S(1)}, bf16[1024,1376]{0,1:T(8,128)(2,1)}, u32[]{:S(2)}) copy-start(bf16[1024,1376]{0,1:T(8,128)(2,1)} %get-tuple-element.87) | copy-start | bytes 8454148
  354.0 9.3 %copy-start.36 = (bf16[1024,1376]{0,1:T(8,128)(2,1)S(1)}, bf16[1024,1376]{0,1:T(8,128)(2,1)}, u32[]{:S(2)}) copy-start(bf16[1024,1376]{0,1:T(8,128)(2,1)} %get-tuple-element.86) | copy-start | bytes 8454148
  372.8 33.4 %slice-start.6 = ((s8[8388608]{0:T(1024)(128)(4,1)}), s8[4194304]{0:T(1024)(128)(4,1)S(1)}, s32[]{:S(2)}) async-start(s8[8388608]{0:T(1024)(128)(4,1)} %bitcast.67), calls=%async_computation.6 | async-start | bytes 8388608
  445.8 6.3 copy-start.26
  445.8 6.3 copy-start.27
  452.6 5.3 copy-start.1
  452.6 5.3 copy-start.37
  457.9 7.9 %copy-start.39 = (bf16[1024,1376]{0,1:T(8,128)(2,1)S(1)}, bf16[1024,1376]{0,1:T(8,128)(2,1)}, u32[]{:S(2)}) copy-start(bf16[1024,1376]{0,1:T(8,128)(2,1)} %get-tuple-element.87) | copy-start | bytes 8454148
  465.8 8.2 %copy-start.5 = (bf16[256,2048]{1,0:T(8,128)(2,1)S(1)}, bf16[256,2048]{1,0:T(8,128)(2,1)}, u32[]{:S(2)}) copy-start(bf16[256,2048]{1,0:T(8,128)(2,1)} %copy-done.4) | copy-start | bytes 3145732
  465.8 8.2 %copy-start.7 = (bf16[256,2048]{1,0:T(8,128)(2,1)S(1)}, bf16[256,2048]{1,0:T(8,128)(2,1)}, u32[]{:S(2)}) copy-start(bf16[256,2048]{1,0:T(8,128)(2,1)} %copy-done.6) | copy-start | bytes 3145732
  465.8 8.2 %copy-start.8 = (bf16[1024,512]{1,0:T(8,128)(2,1)S(1)}, bf16[1024,512]{1,0:T(8,128)(2,1)}, u32[]{:S(2)}) copy-start(bf16[1024,512]{1,0:T(8,128)(2,1)} %get-tuple-element.48.heads) | copy-start | bytes 3145732
  474.1 27.5 %copy-start.24 = (bf16[256,2048]{1,0:T(8,128)(2,1)S(1)}, bf16[256,2048]{1,0:T(8,128)(2,1)}, u32[]{:S(2)}) copy-start(bf16[256,2048]{1,0:T(8,128)(2,1)} %param.11) | copy-start | bytes 3145732
  474.1 27.5 %copy-start.34 = (f32[2048]{0:T(1024)S(1)}, f32[2048]{0:T(1024)}, u32[]{:S(2)}) copy-start(f32[2048]{0:T(1024)} %param.14) | copy-start | bytes 24580
  501.6 2.7 copy-start.23
  740.8 3.7 copy-start.35
  740.8 4.9 copy-start.32
  740.8 5.6 copy-start.31
  740.8 6.4 copy-start.30
  744.5 3.9 copy-start.29
  (17 other events, 34.9 us)

commit v2 on v1

--- a/solution.py
+++ b/solution.py
@@ -8,7 +8,10 @@
 f32 = jnp.float32
 bf16 = jnp.bfloat16
 HEAD_DIM = 128
+MP = 4
 epsilon = 1e-06
+
+
 MESH = pl.DeviceIdType.MESH
 Z_LOW, Z_HIGH, CORE, SIDE, DEEP = 1, 2, 4, 8, 16
 ANY = pl.BlockSpec(memory_space=pl.ANY)
@@ -112,33 +115,29 @@
                   send_sems, recv_sems, local_sems):
     place = Place()
     dp, mp = place.dp, place.mp
-    side, high = place.bit(SIDE), place.bit(Z_HIGH)
+    side = place.bit(SIDE)
     locals_ = []
     copies = Copies(place, send_sems, recv_sems, local_sems)
-
     half = wd.shape[0] // 2
     blk = wd.shape[1]
     share = first.shape[0]
     zrow = wo.shape[0]
-    flip = place.flip
-    greet(place, (1, 2, 3, CORE, SIDE, DEEP))
-
-    locals_.append(copies.local(first, rows.at[pl.ds(mp * share, share), :]))
-    locals_.append(copies.local(cot, cots.at[0:share, :]))
-    locals_.append(copies.local(wq, query.at[pl.ds(dp * blk, blk), :]))
-    locals_.append(copies.local(wo, out.at[pl.ds(mp * zrow, zrow), pl.ds(dp * blk, blk)]))
-    mats = ((wg, gate), (wu, up), (wd, down))
-    for weight, whole in mats:
-        locals_.append(copies.local(weight.at[pl.ds(side * half, half), :],
-                                    whole.at[pl.ds(high * half, half), pl.ds(dp * blk, blk)]))
-
     zcol = wq.shape[1]
-    locals_.append(copies.local(wq, wide.at[:, pl.ds(mp * zcol, zcol)]))
-    def tile(whole, z, d):
-        return whole.at[pl.ds(z * half, half), pl.ds(d * blk, blk)]
-
     nchunk = 2
     chunk = share // nchunk
+    mats = ((wg, gate), (wu, up), (wd, down))
+    own, across = side, 1 - side
+    DEEPER, OTHER = 2, 4
+    greet(place, (1, 2, 3, CORE, SIDE, DEEP))
+
+    def tile(whole, z, spot):
+        return whole.at[pl.ds(z * half, half), pl.ds(spot * blk, blk)]
+
+    def qrows(spot):
+        return query.at[pl.ds(spot * blk, blk), :]
+
+    def columns(spot):
+        return out.at[:, pl.ds(spot * blk, blk)]
 
     def row_block(c, source_is_input):
         def get(m):
@@ -149,7 +148,7 @@
 
     def out_block(source_is_input):
         def get(m):
-            target = out.at[pl.ds(m * zrow, zrow), pl.ds(dp * blk, blk)]
+            target = out.at[pl.ds(m * zrow, zrow), pl.ds(own * blk, blk)]
             return (wo if source_is_input else target), target
         return get
 
@@ -159,115 +158,118 @@
             return (wq if source_is_input else target), target
         return get
 
-    def line(store, step, block_of, key):
-        lead = (key, step)
-        store[("r",) + lead] = copies.step(block_of, mp - (step - 1), mp - step, 1,
-                                           (mp >= step - 1) & (mp < 3), mp >= step)
-        store[("l",) + lead] = copies.step(block_of, mp + (step - 1), mp + step, -1,
-                                           (mp <= 3 - (step - 1)) & (mp > 0), mp <= 3 - step)
-
     store = {}
-    core = []
-
-    def spread_core(piece):
-        core.append(copies.swap(piece, piece, CORE))
+
+    def line(step, block_of, key):
+        store[("r", key, step)] = copies.step(block_of, mp - (step - 1), mp - step, 1,
+                                              (mp >= step - 1) & (mp < 3), mp >= step)
+        store[("l", key, step)] = copies.step(block_of, mp + (step - 1), mp + step, -1,
+                                              (mp <= 3 - (step - 1)) & (mp > 0), mp <= 3 - step)
 
     def arrive(key, step):
         copies.got(store[("r", key, step)])
         copies.got(store[("l", key, step)])
 
-    dy = flip(dp, DEEP // 4)
-    dx = flip(dp, SIDE // 4)
-    dxy = flip(dy, SIDE // 4)
     own_piece = [weight.at[pl.ds(side * half, half), :] for weight, _ in mats]
     zhop = [[], [], []]
     yhop = [[], [], []]
-
-    def send_z(i, source, d):
-        zhop[i].append(copies.swap(source, tile(mats[i][1], high, d), Z_HIGH))
-
-    def send_y(i, source, z, d):
-        yhop[i].append((copies.swap(source, tile(mats[i][1], z, d), DEEP), z, flip(d, DEEP // 4)))
-
-    line(store, 1, out_block(True), "o")
-    send_z(0, own_piece[0], dp)
-    xhop = [copies.swap(weight.at[pl.ds((1 - side) * half, half), :], tile(whole, high, dp), SIDE)
+    core = []
+
+    def send_z(i, source, spot):
+        zhop[i].append(copies.swap(source, tile(mats[i][1], 1, spot), Z_HIGH))
+
+    def send_y(i, source, z, spot):
+        yhop[i].append((copies.swap(source, tile(mats[i][1], z, spot + DEEPER), DEEP), z, spot + DEEPER))
+
+    def core_tile(i, z, spot, source=None):
+        piece = tile(mats[i][1], z, spot)
+        core.append(copies.swap(piece if source is None else source, tile(mats[i][1], z, spot + OTHER), CORE))
+
+    def core_query(spot, source=None):
+        core.append(copies.swap(qrows(spot) if source is None else source, qrows(spot + OTHER), CORE))
+
+    def core_out(spot):
+        core.append(copies.swap(columns(spot), columns(spot + OTHER), CORE))
+
+    line(1, out_block(True), "o")
+    send_z(0, own_piece[0], own)
+    xhop = [copies.swap(weight.at[pl.ds((1 - side) * half, half), :], tile(whole, 0, own), SIDE)
             for weight, whole in mats]
-    wq_y = copies.swap(wq, query.at[pl.ds(dp * blk, blk), :], DEEP)
+    wq_y = copies.swap(wq, qrows(own + DEEPER), DEEP)
     for i in range(3):
-        send_y(i, own_piece[i], high, dp)
-    wq_x = [copies.swap(wq, query.at[pl.ds(dp * blk, blk), :], SIDE)]
+        send_y(i, own_piece[i], 0, own)
+    wq_x = [copies.swap(wq, qrows(own), SIDE)]
+    locals_.append(copies.local(first, rows.at[pl.ds(mp * share, share), :]))
+    locals_.append(copies.local(cot, cots.at[0:share, :]))
+    locals_.append(copies.local(wq, qrows(own)))
+    locals_.append(copies.local(wo, out.at[pl.ds(mp * zrow, zrow), pl.ds(own * blk, blk)]))
     for i in range(3):
-        core.append(copies.swap(own_piece[i], tile(mats[i][1], high, dp), CORE))
-    spread_wq = [copies.swap(wq, query.at[pl.ds(dp * blk, blk), :], CORE)]
+        locals_.append(copies.local(own_piece[i], tile(mats[i][1], 0, own)))
+    locals_.append(copies.local(wq, wide.at[:, pl.ds(mp * zcol, zcol)]))
+    for i in range(3):
+        core_tile(i, 0, own, own_piece[i])
+    core_query(own, wq)
     copies.got(wq_y)
-    piece = query.at[pl.ds(dy * blk, blk), :]
-    wq_x.append(copies.swap(piece, piece, SIDE))
-    spread_core(piece)
+    wq_x.append(copies.swap(qrows(own + DEEPER), qrows(own + DEEPER), SIDE))
+    core_query(own + DEEPER)
     cot_x = copies.swap(cot, cots.at[share:2 * share, :], SIDE)
     arrive("o", 1)
-    line(store, 2, out_block(False), "o")
-    send_z(1, own_piece[1], dp)
+    line(2, out_block(False), "o")
+    send_z(1, own_piece[1], own)
     arrive("o", 2)
-    line(store, 3, out_block(False), "o")
-    send_z(2, own_piece[2], dp)
+    line(3, out_block(False), "o")
+    send_z(2, own_piece[2], own)
     for c in range(nchunk):
-        line(store, 1, row_block(c, True), c)
+        line(1, row_block(c, True), c)
     for i in range(3):
         copies.got(xhop[i])
-        piece = tile(mats[i][1], high, dx)
-        send_y(i, piece, high, dx)
-        send_z(i, piece, dx)
-        spread_core(piece)
-    for item, d in zip(wq_x, (dx, dxy)):
+        piece = tile(mats[i][1], 0, across)
+        send_y(i, piece, 0, across)
+        send_z(i, piece, across)
+        core_tile(i, 0, across)
+    for item, spot in zip(wq_x, (across, across + DEEPER)):
         copies.got(item)
-        spread_core(query.at[pl.ds(d * blk, blk), :])
+        core_query(spot)
     arrive("o", 3)
     for copy in locals_:
         copy.wait()
-
-    def columns(d):
-        return out.at[:, pl.ds(d * blk, blk)]
-
-    out_y = copies.swap(columns(dp), columns(dp), DEEP)
-    out_x = [copies.swap(columns(dp), columns(dp), SIDE)]
-    spread_core(columns(dp))
+    out_y = copies.swap(columns(own), columns(own + DEEPER), DEEP)
+    out_x = [copies.swap(columns(own), columns(own), SIDE)]
+    core_out(own)
     for i in range(3):
         copies.got(zhop[i][0])
-        piece = tile(mats[i][1], 1 - high, dp)
-        send_y(i, piece, 1 - high, dp)
-        spread_core(piece)
-    line(store, 1, wide_block(True), "w")
+        send_y(i, tile(mats[i][1], 1, own), 1, own)
+        core_tile(i, 1, own)
+    line(1, wide_block(True), "w")
     for c in range(nchunk):
         arrive(c, 1)
-        line(store, 2, row_block(c, False), c)
+        line(2, row_block(c, False), c)
     copies.got(out_y)
-    out_x.append(copies.swap(columns(dy), columns(dy), SIDE))
-    spread_core(columns(dy))
+    out_x.append(copies.swap(columns(own + DEEPER), columns(own + DEEPER), SIDE))
+    core_out(own + DEEPER)
     cot_z = copies.swap(cot, cots.at[2 * share:3 * share, :], Z_LOW)
     for i in range(3):
         copies.got(zhop[i][1])
-        piece = tile(mats[i][1], 1 - high, dx)
-        send_y(i, piece, 1 - high, dx)
-        spread_core(piece)
+        send_y(i, tile(mats[i][1], 1, across), 1, across)
+        core_tile(i, 1, across)
     arrive("w", 1)
-    line(store, 2, wide_block(False), "w")
+    line(2, wide_block(False), "w")
     for c in range(nchunk):
         arrive(c, 2)
-        line(store, 3, row_block(c, False), c)
+        line(3, row_block(c, False), c)
     arrive("w", 2)
-    line(store, 3, wide_block(False), "w")
+    line(3, wide_block(False), "w")
     copies.got(out_x[0])
-    spread_core(columns(dx))
+    core_out(across)
     copies.got(cot_z)
     cot_xz = copies.swap(cots.at[2 * share:3 * share, :], cots.at[3 * share:4 * share, :], SIDE)
     for j in range(4):
         for i in range(3):
-            item, z, d = yhop[i][j]
+            item, z, spot = yhop[i][j]
             copies.got(item)
-            spread_core(tile(mats[i][1], z, d))
+            core_tile(i, z, spot)
     copies.got(out_x[1])
-    spread_core(columns(dxy))
+    core_out(across + DEEPER)
     copies.finish()
 
 
@@ -289,7 +291,13 @@
         name="gather_all",
     )(first, cot, wq, wo, wg, wu, wd)
 
+
 DMA = pltpu.SemaphoreType.DMA
+
+
+def dot(left, right, left_dim, right_dim):
+    return lax.dot_general(
+        left, right, (((left_dim,), (right_dim,)), ((), ())), preferred_element_type=f32)
 
 
 def params(ident, vmem=32 << 20):
@@ -298,31 +306,30 @@
 
 def tokens_kernel(heads, query_y, query_0, query_x, own, whole, send_sems, recv_sems, local_sems):
     place = Place()
-    mp, dp = place.mp, place.dp
+    mp = place.mp
+    side = place.bit(SIDE)
     share, local = own.shape[0], heads.shape[1]
     blk = query_0.shape[0]
     copies = Copies(place, send_sems, recv_sems, local_sems)
-    dy = place.flip(dp, 4)
-    dx = place.flip(dp, 2)
-    dxy = place.flip(dy, 2)
-
-    def rows(d):
-        return whole.at[pl.ds(d * blk, blk), :]
+
+    def rows(spot):
+        return whole.at[pl.ds(spot * blk, blk), :]
 
     greet(place, (1, 2, 3, SIDE, CORE))
-    across = copies.swap(query_y, rows(dy), SIDE)
+    across = copies.swap(query_y, rows(side + 2), SIDE)
     for mask in (2, 3, 1):
         other = place.partner(mask)[1]
         copies.swap(heads.at[pl.ds(other * share, share), :], own.at[:, pl.ds(mp * local, local)], mask)
-    held = [copies.local(query_0, rows(dp)), copies.local(query_y, rows(dy)), copies.local(query_x, rows(dx))]
-    copies.swap(query_0, rows(dp), CORE)
-    copies.swap(query_y, rows(dy), CORE)
-    copies.swap(query_x, rows(dx), CORE)
+    held = [copies.local(query_0, rows(side)), copies.local(query_y, rows(side + 2)),
+            copies.local(query_x, rows(1 - side))]
+    copies.swap(query_0, rows(side + 4), CORE)
+    copies.swap(query_y, rows(side + 6), CORE)
+    copies.swap(query_x, rows(1 - side + 4), CORE)
     own[:, pl.ds(mp * local, local)] = heads[pl.ds(mp * share, share), :]
     for copy in held:
         copy.wait()
     copies.got(across)
-    copies.swap(rows(dxy), rows(dxy), CORE)
+    copies.swap(rows(1 - side + 2), rows(1 - side + 6), CORE)
     copies.finish()
 
 
@@ -487,208 +494,30 @@
         compiler_params=params(ident), name="quad_reduce")(parts)
 
 
-def reduce_kernel(gd, gg, gu, go, gq, parts_in, gains_in, down, gate, up, out, query, total, gains,
-                  own_f, core_f, deep_f, high_f, side_f, own_o, core_o, side_o, deep_o, z_o,
-                  own_q, core_q, side_q, deep_q, parts, relay, landed, gains_got,
-                  send_sems, recv_sems, local_sems):
+def all_sum_kernel(value, total, got, send_sems, recv_sems):
     place = Place()
-    dp, mp = place.dp, place.mp
-    flip = place.flip
-    high = place.bit(Z_HIGH)
-    side = place.bit(SIDE)
-    blk = down.shape[1]
-    hidden = down.shape[0]
-    half = hidden // 2
-    share = total.shape[0]
-    zrow = out.shape[0]
-    spots = ((0, 0), (0, 1), (1, 0), (1, 1))
-    copies = Copies(place, send_sems, recv_sems, local_sems)
-    mats = (gd, gg, gu)
-
-    def place_of(spot, core):
-        return flip(flip(flip(dp, 4 * spot[0]), 2 * spot[1]), core)
-
-    def cols(array, d):
-        return array.at[:, pl.ds(d * blk, blk)]
-
-    def brows(array, d):
-        return array.at[pl.ds(d * blk, blk), :]
-
-    loads_f = [[copies.local(cols(m, place_of(s, 0)), own_f.at[i, j]) for j, s in enumerate(spots)]
-               for i, m in enumerate(mats)]
-    loads_o = [copies.local(cols(go, place_of(s, 0)), own_o.at[j]) for j, s in enumerate(spots)]
-    loads_q = [copies.local(brows(gq, place_of(s, 0)), own_q.at[j]) for j, s in enumerate(spots)]
-    load_p = copies.local(parts_in, parts)
-    greet(place, (1, 2, 3, CORE, SIDE, DEEP))
-    gains[...] = gains_in[...]
-    gain_masks = [1, 2, CORE, SIDE, DEEP]
-    gain_state = {"item": None, "at": 0}
-
-    def gain_hop():
-        if gain_state["item"] is not None:
-            copies.got(gain_state["item"])
-            copies_wait_send(gain_state["item"])
-            gains[...] = gains[...] + gains_got[gain_state["at"] - 1]
-            gain_state["item"] = None
-        if gain_state["at"] < len(gain_masks):
-            gain_state["item"] = copies.swap(gains, gains_got.at[gain_state["at"]], gain_masks[gain_state["at"]])
-            gain_state["at"] += 1
-
-    def copies_wait_send(item):
+    masks = (1, 2, CORE, SIDE, DEEP)
+    greet(place, masks)
+    copies = Copies(place, send_sems, recv_sems)
+    total[...] = value[...]
+    for i, mask in enumerate(masks):
+        item = copies.swap(total, got.at[i], mask)
+        copies.got(item)
         item["copy"].wait_send()
         item["sent"] = True
-
-    order = ((1, 0), (1, 1), (0, 0), (0, 1))
-    index = {s: j for j, s in enumerate(spots)}
-    core_in = []
-    for i, m in enumerate(mats):
-        core_in.append({s: copies.swap(cols(m, place_of(s, 1)), core_f.at[i, index[s]], CORE) for s in order})
-    order_o = ((0, 1), (1, 1), (0, 0), (1, 0))
-    core_in_o = {s: copies.swap(cols(go, place_of(s, 1)), core_o.at[index[s]], CORE) for s in order_o}
-    core_in_q = {s: copies.swap(brows(gq, place_of(s, 1)), core_q.at[index[s]], CORE) for s in order_o}
-    gain_hop()
-    load_p.wait()
-    reduce = QuadReduce(copies, parts, relay, landed)
-    deep_in = []
-    for i in range(3):
-        sent = {}
-        for s in order:
-            j = index[s]
-            copies.got(core_in[i][s])
-            loads_f[i][j].wait()
-            add_into(own_f.at[i, j], (0, hidden), core_f.at[i, j])
-            if s[0]:
-                sent[s[1]] = copies.swap(own_f.at[i, j], deep_f.at[i, s[1]], DEEP)
-        deep_in.append(sent)
-        if i == 0:
-            reduce.start()
-        gain_hop()
-    side_in_o, side_in_q = {}, {}
-    for s in order_o:
-        j = index[s]
-        copies.got(core_in_q[s])
-        loads_q[j].wait()
-        add_into(own_q.at[j], (0, blk), core_q.at[j])
-        if s[1]:
-            side_in_q[s[0]] = copies.swap(own_q.at[j], side_q.at[s[0]], SIDE)
-    for s in order_o:
-        j = index[s]
-        copies.got(core_in_o[s])
-        loads_o[j].wait()
-        add_into(own_o.at[j], (0, own_o.shape[1]), core_o.at[j])
-        if s[1]:
-            side_in_o[s[0]] = copies.swap(own_o.at[j], side_o.at[s[0]], SIDE)
-    gain_hop()
-    reduce.relayed()
-    gain_hop()
-    high_in = []
-    for i in range(3):
-        sent = {}
-        for x in (1, 0):
-            j = index[(0, x)]
-            copies.got(deep_in[i][x])
-            add_into(own_f.at[i, j], ((1 - high) * half, half), deep_f.at[i, x, pl.ds((1 - high) * half, half), :], step=16)
-            sent[x] = copies.swap(own_f.at[i, j, pl.ds((1 - high) * half, half), :], high_f.at[i, x], Z_HIGH)
-            add_into(own_f.at[i, j], (high * half, half), deep_f.at[i, x, pl.ds(high * half, half), :], step=16)
-        high_in.append(sent)
-    gain_hop()
-    deep_in_q = None
-    deep_in_o = None
-    for y in (1, 0):
-        j = index[(y, 0)]
-        copies.got(side_in_q[y])
-        add_into(own_q.at[j], (0, blk), side_q.at[y])
-        if y:
-            deep_in_q = copies.swap(own_q.at[j], deep_q, DEEP)
-    for y in (1, 0):
-        j = index[(y, 0)]
-        copies.got(side_in_o[y])
-        add_into(own_o.at[j], (0, own_o.shape[1]), side_o.at[y])
-        if y:
-            deep_in_o = copies.swap(own_o.at[j], deep_o, DEEP)
-    copies.got(deep_in_o)
-    add_into(own_o.at[0], (0, own_o.shape[1]), deep_o)
-    z_in = []
-    for n, mask in enumerate((2, 3, 1)):
-        other = place.partner(mask)[1]
-        z_in.append(copies.swap(own_o.at[0, pl.ds(other * zrow, zrow), :], z_o.at[n], mask))
-    side_in = []
-    outs = (down, gate, up)
-    for i in range(3):
-        for x in (1, 0):
-            j = index[(0, x)]
-            copies.got(high_in[i][x])
-            add_into(own_f.at[i, j], (high * half, half), high_f.at[i, x], step=16)
-            if x:
-                side_in.append(copies.swap(own_f.at[i, j, pl.ds(high * half, half), :], side_f.at[i], SIDE))
-    copies.got(deep_in_q)
-    query[...] = own_q[0].astype(f32) + deep_q[...].astype(f32)
-    reduce.arrived()
-
-    def one(i, carry):
-        here = pl.ds(i * 32, 32)
-        total[here, :] = (parts[here, :].astype(f32) + landed[0, here, :].astype(f32)
-                          + landed[1, here, :].astype(f32))
-        return carry
-
-    lax.fori_loop(0, share // 32, one, 0)
-    for item in z_in:
-        copies.got(item)
-
-    def add_z(i, carry):
-        here = pl.ds(i * 32, 32)
-        sum_ = own_o[0, pl.ds(mp * zrow + i * 32, 32), :].astype(f32)
-        for n in range(3):
-            sum_ = sum_ + z_o[n, here, :].astype(f32)
-        out[here, :] = sum_
-        return carry
-
-    lax.fori_loop(0, zrow // 32, add_z, 0)
-    for i in range(3):
-        copies.got(side_in[i])
-
-        def write(n, carry, i=i):
-            here = pl.ds(side * half + n * 16, 16)
-            there = pl.ds((1 - side) * half + n * 16, 16)
-            outs[i][here, :] = own_f[i, 0, pl.ds(high * half + n * 16, 16), :].astype(f32)
-            outs[i][there, :] = side_f[i, pl.ds(n * 16, 16), :].astype(f32)
-            return carry
-
-        lax.fori_loop(0, half // 16, write, 0)
+        total[...] = total[...] + got[i]
     copies.finish()
 
 
-def reduce_call(gd, gg, gu, go, gq, parts, gains, ident):
-    hidden, width = gd.shape
-    blk = width // 8
-    half = hidden // 2
-    local = gq.shape[1]
-    share = parts.shape[0] // 4
-    V = pltpu.VMEM
+def all_sum(value, ident):
     return pl.pallas_call(
-        reduce_kernel,
-        out_shape=(jax.ShapeDtypeStruct((hidden, blk), f32),) * 3
-        + (jax.ShapeDtypeStruct((width // 4, blk), f32), jax.ShapeDtypeStruct((blk, local), f32),
-           jax.ShapeDtypeStruct((share, width), f32), jax.ShapeDtypeStruct(gains.shape, f32)),
-        in_specs=[ANY] * 6 + [VM],
-        out_specs=(VM,) * 7,
-        scratch_shapes=[
-            V((3, 4, hidden, blk), bf16), V((3, 4, hidden, blk), bf16), V((3, 2, hidden, blk), bf16),
-            V((3, 2, half, blk), bf16), V((3, half, blk), bf16),
-            V((4, width, blk), bf16), V((4, width, blk), bf16), V((2, width, blk), bf16), V((width, blk), bf16),
-            V((3, width // 4, blk), bf16),
-            V((4, blk, local), bf16), V((4, blk, local), bf16), V((2, blk, local), bf16), V((blk, local), bf16),
-            V((share * 4, width), bf16), V((2, share // 2, width), bf16), V((2, share, width), bf16),
-            V((5,) + gains.shape, f32),
-            DMA((60,)), DMA((60,)), DMA((24,))],
-        compiler_params=params(ident, 63 << 20), name="reduce_all",
-    )(gd, gg, gu, go, gq, parts, gains)
+        all_sum_kernel, out_shape=jax.ShapeDtypeStruct(value.shape, f32), in_specs=[VM], out_specs=VM,
+        scratch_shapes=[pltpu.VMEM((5,) + value.shape, f32), DMA((5,)), DMA((5,))],
+        compiler_params=params(ident), name="all_sum")(value)
+
+
 ROWS=256
 DOC_MOST=512
-
-
-def dot(left, right, left_dim, right_dim):
-    return lax.dot_general(left, right, (((left_dim,), (right_dim,)), ((), ())), preferred_element_type=f32)
 
 
 def key_range(block, seq_len):
@@ -788,6 +617,266 @@
 
 def starts_of(segments):
     return jnp.sum((segments[0][None, :] < segments[0][:, None]).astype(jnp.int32), axis=1)[None, :]
+
+
+def hidden_cuts(hidden):
+    cuts = []
+    start = 0
+    while start < hidden:
+        size = min(512, hidden - start)
+        cuts.append((start, size))
+        start += size
+    return cuts
+
+
+def ffn_kernel(normed, cots_in, down_in, gate_in, up_in, total, fparts_out, sums_out,
+               weights, tokens, acts, dparts, relay, landed, fparts,
+               send_sems, recv_sems, local_sems, free_sem):
+    place = Place()
+    share, width = normed.shape
+    hidden = down_in.shape[0]
+    half = share // 2
+    wide = width // 2
+    cuts = hidden_cuts(hidden)
+    copies = Copies(place, send_sems, recv_sems, local_sems)
+    load_cots = copies.local(cots_in, tokens.at[0])
+    load_w = [copies.local(w, weights.at[i]) for i, w in enumerate((down_in, gate_in, up_in))]
+    greet(place, (Z_LOW, SIDE, CORE))
+
+    def at(quarter, part):
+        return tokens.at[1, pl.ds(quarter * share + part * half, half), :]
+
+    a, b = pl.ds(0, half), pl.ds(half, half)
+    low_a = copies.swap(normed.at[a, :], at(2, 0), Z_LOW)
+    side_b = copies.swap(normed.at[b, :], at(1, 1), SIDE)
+    low_b = copies.swap(normed.at[b, :], at(2, 1), Z_LOW)
+    side_a = copies.swap(normed.at[a, :], at(1, 0), SIDE)
+    tokens[1, 0:share, :] = normed[...]
+
+    def block(r):
+        here = pl.ds(r * share, share)
+        for start, size in cuts:
+            rows = tokens[1, here, :]
+            gate = dot(rows, weights[1, start:start + size, :], 1, 1)
+            up = dot(rows, weights[2, start:start + size, :], 1, 1)
+            grad = dot(tokens[0, here, :], weights[0, start:start + size, :], 1, 1)
+            sigmoid = jax.nn.sigmoid(gate)
+            silu = gate * sigmoid
+            acts[0, here, start:start + size] = (silu * up).astype(bf16)
+            acts[1, here, start:start + size] = (
+                grad * up * sigmoid * (1.0 + gate * (1.0 - sigmoid))).astype(bf16)
+            acts[2, here, start:start + size] = (grad * silu).astype(bf16)
+
+        def columns(n, carry):
+            there = pl.ds(pl.multiple_of(n * 512, 512), 512)
+            dparts[here, there] = (dot(acts[1, here, :], weights[1, :, there], 1, 0)
+                                   + dot(acts[2, here, :], weights[2, :, there], 1, 0)).astype(bf16)
+            fparts[here, there] = dot(acts[0, here, :], weights[0, :, there], 1, 0).astype(bf16)
+            return carry
+
+        lax.fori_loop(0, width // 512, columns, 0)
+
+    for copy in load_w:
+        copy.wait()
+    load_cots.wait()
+    got = {"across": None}
+
+    def step(r, carry):
+        @pl.when(r == 1)
+        def _():
+            low_a["copy"].wait_recv()
+            side_b["copy"].wait_recv()
+            forward[0].start()
+            forward[1].start()
+            side_a["copy"].wait_recv()
+            low_b["copy"].wait_recv()
+
+        @pl.when(r == 3)
+        def _():
+            forward[0].wait_recv()
+            forward[1].wait_recv()
+        block(r)
+        return carry
+
+    forward = [copies.describe(at(2, 0), at(3, 0), place.partner(SIDE), copies.count),
+               copies.describe(at(1, 1), at(3, 1), place.partner(Z_LOW), copies.count + 1)]
+    copies.count += 2
+    lax.fori_loop(0, 4, step, 0)
+    for item in (low_a, side_b, low_b, side_a):
+        item["got"] = True
+    pl.semaphore_signal(free_sem, inc=1, device_id=place.partner(CORE), device_id_type=MESH)
+    reduce = QuadReduce(copies, dparts, relay, landed)
+    reduce.start()
+    save = copies.local(fparts, fparts_out)
+
+    base = copies.count
+    copies.count += 3
+
+    def give_copy(i):
+        return copies.describe(weights.at[i, :, pl.ds(0, wide)], weights.at[i, :, pl.ds(wide, wide)],
+                               place.partner(CORE), base + i)
+
+    def give(i, carry):
+        right = tokens[jnp.minimum(i, 1), :, wide:]
+        for start, size in cuts:
+            weights[i, start:start + size, 0:wide] = dot(
+                acts[i, :, start:start + size], right, 0, 0).astype(bf16)
+
+        @pl.when(i == 0)
+        def _():
+            pl.semaphore_wait(free_sem, 1)
+        give_copy(i).start()
+        return carry
+
+    lax.fori_loop(0, 3, give, 0)
+    reduce.relayed()
+
+    def keep(i, carry):
+        give_copy(i).wait_recv()
+        right = tokens[jnp.minimum(i, 1), :, 0:wide]
+        for start, size in cuts:
+            rows = slice(start, start + size)
+            weights[i, rows, wide:] = (dot(acts[i, :, rows], right, 0, 0)
+                                       + weights[i, rows, wide:].astype(f32)).astype(bf16)
+        pltpu.make_async_copy(weights.at[i, :, pl.ds(wide, wide)], sums_out.at[i], local_sems.at[5 + i]).start()
+        return carry
+
+    lax.fori_loop(0, 3, keep, 0)
+    reduce.arrived()
+
+    def one(i, carry):
+        here = pl.ds(i * 32, 32)
+        total[here, :] = (dparts[here, :].astype(f32) + landed[0, here, :].astype(f32)
+                          + landed[1, here, :].astype(f32))
+        return carry
+
+    lax.fori_loop(0, share // 32, one, 0)
+    for i in range(3):
+        give_copy(i).wait_send()
+        pltpu.make_async_copy(weights.at[i, :, pl.ds(wide, wide)], sums_out.at[i], local_sems.at[5 + i]).wait()
+    for copy in forward:
+        copy.wait_send()
+    save.wait()
+    copies.finish()
+
+
+def ffn_call(normed, cots, down, gate, up, ident):
+    share, width = normed.shape
+    hidden = down.shape[0]
+    V = pltpu.VMEM
+    flops = 2 * share * 4 * width * hidden * 9
+    return pl.pallas_call(
+        ffn_kernel,
+        out_shape=(jax.ShapeDtypeStruct((share, width), f32), jax.ShapeDtypeStruct((share * 4, width), bf16),
+                   jax.ShapeDtypeStruct((3, hidden, width // 2), bf16)),
+        in_specs=[VM] + [ANY] * 4,
+        out_specs=(VM, ANY, ANY),
+        scratch_shapes=[
+            V((3, hidden, width), bf16), V((2, share * 4, width), bf16), V((3, share * 4, hidden), bf16),
+            V((share * 4, width), bf16), V((2, share // 2, width), bf16), V((2, share, width), bf16),
+            V((share * 4, width), bf16),
+            DMA((16,)), DMA((16,)), DMA((8,)), pltpu.SemaphoreType.REGULAR],
+        compiler_params=params(ident, 63 << 20),
+        cost_estimate=pl.CostEstimate(flops=flops, bytes_accessed=40 << 20, transcendentals=share * 4 * hidden),
+        name="feed_forward",
+    )(normed, cots, down, gate, up)
+
+
+class Grid:
+    def __init__(self, dp):
+        self.dp = dp
+        self.size = dp * MP
+        self.rest = []
+        mask = 16
+        while mask < self.size:
+            self.rest.append(mask)
+            mask *= 2
+        self.relative = [CORE] + self.rest
+        self.me = lax.axis_index("dp") * MP + lax.axis_index("mp")
+        self.me_mp = lax.axis_index("mp")
+        self.me_dp = lax.axis_index("dp")
+
+    def swap(self, value, mask):
+        return lax.ppermute(value, ("dp", "mp"), [(i, i ^ mask) for i in range(self.size)])
+
+    def bit(self, mask):
+        return (self.me // mask) % 2
+
+    def spread(self, value):
+        block = value.shape[-1] // self.dp
+        pieces = []
+        for spot in range(self.dp):
+            flips = 0
+            digits = spot >> 1
+            for place, mask in enumerate(reversed(self.relative)):
+                if (digits >> place) & 1:
+                    flips |= mask // MP
+            source = ((self.me_dp ^ flips) & ~(SIDE // MP)) | ((spot & 1) * (SIDE // MP))
+            pieces.append(lax.dynamic_slice_in_dim(value, source * block, block, value.ndim - 1))
+        return jnp.concatenate(pieces, axis=-1)
+
+    def restore(self, value):
+        block = value.shape[-1] // self.dp
+        pieces = []
+        for target in range(self.dp):
+            flips = (self.me_dp ^ target) * MP
+            spot = 0
+            for mask in self.relative:
+                spot = spot * 2 + (flips // mask) % 2
+            spot = spot * 2 + (target * MP // SIDE) % 2
+            pieces.append(lax.dynamic_slice_in_dim(value, spot * block, block, value.ndim - 1))
+        return jnp.concatenate(pieces, axis=-1)
+
+    def ordered(self, mine, theirs, mask, axis):
+        high = self.bit(mask) == 1
+        return jnp.concatenate(
+            [jnp.where(high, theirs, mine), jnp.where(high, mine, theirs)], axis=axis
+        )
+
+    def line_gather(self, value):
+        right, left = {0: value}, {0: value}
+        for step in range(1, MP):
+            right[step] = lax.ppermute(
+                right[step - 1], "mp", [(j, j + 1) for j in range(step - 1, MP - 1)]
+            )
+            left[step] = lax.ppermute(
+                left[step - 1], "mp", [(j, j - 1) for j in range(1, MP - step + 1)]
+            )
+        return [value] + [left[d] + right[MP - d] for d in range(1, MP)]
+
+    def exchange_mp(self, value, split, join):
+        return lax.all_to_all(value, "mp", split, join, tiled=True)
+
+    def quad_gather(self, value):
+        half = value.shape[0] // 2
+        from_side = self.swap(value, SIDE)
+        from_low = self.swap(value, Z_LOW)
+        across = jnp.concatenate(
+            [self.swap(from_low[:half], SIDE), self.swap(from_side[half:], Z_LOW)], axis=0
+        )
+        return [value, from_side, from_low, across]
+
+    def quad_start(self, across):
+        half = across.shape[0] // 2
+        return self.swap(across[:half], SIDE), self.swap(across[half:], Z_LOW)
+
+    def quad_finish(self, relayed, for_side, for_low, own):
+        by_side, by_low = relayed
+        half = own.shape[0] // 2
+        low_sum = jnp.concatenate(
+            [(for_low[:half] + by_side.astype(f32)), for_low[half:]], axis=0
+        ).astype(bf16)
+        side_sum = jnp.concatenate(
+            [for_side[:half], for_side[half:] + by_low.astype(f32)], axis=0
+        ).astype(bf16)
+        return own + self.swap(side_sum, SIDE).astype(f32) + self.swap(low_sum, Z_LOW).astype(f32)
+
+    def all_sum(self, value):
+        mask = 1
+        while mask < self.size:
+            value = value + self.swap(value, mask)
+            mask *= 2
+        return value
 
 
 def contract(left, right, left_dim, right_dim):
@@ -1007,14 +1096,19 @@
 
 def fast_body(inputs, keys_values, segment_ids, gain_first, gain_second, w_query, w_out, w_gate,
               w_up, w_down, cotangent):
-    tokens = inputs.astype(f32)
+    grid = Grid(8)
+    share = inputs.shape[0]
+    hidden_half = w_down.shape[0] // 2
+    tokens = grid.spread(inputs).astype(f32)
+    gain_one = grid.spread(gain_first)
+    gain_two = grid.spread(gain_second)
+    cot_here = grid.spread(cotangent)
     inverse_first = root_inverse(tokens)
     scaled_first = tokens * inverse_first
-    normed_first = (scaled_first * gain_first).astype(bf16)
-    share = inputs.shape[0]
+    normed_first = (scaled_first * gain_one).astype(bf16)
 
     rows_first, cots, query_part, query_0, out_whole, gate_here, up_here, down_here = gather_call(
-        normed_first, cotangent, w_query, w_out, w_gate.T, w_up.T, w_down)
+        normed_first, cot_here, w_query, w_out, w_gate.T, w_up.T, w_down)
 
     queries = contract(rows_first, query_part, 1, 0).astype(bf16)
     starts = starts_of(segment_ids)
@@ -1025,50 +1119,71 @@
     residual = tokens + contract(context_own, out_whole, 1, 0)
     inverse_second = root_inverse(residual)
     scaled_second = residual * inverse_second
-    normed_second = (scaled_second * gain_second).astype(bf16)
-    rows = quad_gather(normed_second, 3)
-
-    gate_proj = contract(rows, gate_here, 1, 1)
-    up_proj = contract(rows, up_here, 1, 1)
-    sigmoid_gate = jax.nn.sigmoid(gate_proj)
-    silu_gate = gate_proj * sigmoid_gate
-    hidden = (silu_gate * up_proj).astype(bf16)
-    ffn_parts = contract(hidden, down_here, 1, 0).astype(bf16)
-    grad_hidden = contract(cots, down_here, 1, 1)
-    grad_gate_act = (
-        grad_hidden * up_proj * sigmoid_gate * (1.0 + gate_proj * (1.0 - sigmoid_gate))
-    ).astype(bf16)
-    grad_up_act = (grad_hidden * silu_gate).astype(bf16)
-    grad_parts = (contract(grad_gate_act, gate_here, 1, 0) + contract(grad_up_act, up_here, 1, 0)).astype(bf16)
-    grad_normed_second = quad_reduce(grad_parts, 4)
-    grad_down = contract(hidden, cots, 0, 0).astype(bf16)
-    grad_gate = contract(grad_gate_act, rows, 0, 0).astype(bf16)
-    grad_up = contract(grad_up_act, rows, 0, 0).astype(bf16)
+    normed_second = (scaled_second * gain_two).astype(bf16)
+    grad_normed_second, ffn_parts, ffn_sums = ffn_call(normed_second, cots, down_here, gate_here, up_here, 3)
+
+    def quad_sum(parts):
+        own, side_part, low_part, across = (parts[i * share:(i + 1) * share] for i in range(4))
+        relayed = grid.quad_start(across)
+        return grid.quad_finish(relayed, side_part.astype(f32), low_part.astype(f32), own.astype(f32))
+
+    ffn_sum = quad_sum(ffn_parts)
+    output = grid.restore((residual + ffn_sum).astype(bf16))
+
+    def halves_sum(keep, give, mask):
+        return keep.astype(f32) + grid.swap(give.astype(bf16), mask).astype(f32)
+
+    def ffn_grad(total):
+        for mask in grid.rest:
+            half = total.shape[1] // 2
+            total = halves_sum(total[:, :half], total[:, half:], mask)
+        total = halves_sum(total[:hidden_half], total[hidden_half:], Z_HIGH)
+        width = total.shape[1] // 2
+        side = grid.bit(SIDE)
+        keep = lax.dynamic_slice_in_dim(total, side * width, width, 1)
+        give = lax.dynamic_slice_in_dim(total, (1 - side) * width, width, 1)
+        theirs = grid.swap(give.astype(bf16), SIDE).astype(f32)
+        return grid.ordered(keep, theirs, SIDE, 0)
+
+    down_shard = ffn_grad(ffn_sums[0])
+    gate_shard = ffn_grad(ffn_sums[1]).T
+    up_shard = ffn_grad(ffn_sums[2]).T
 
     grad_from_norm, gain_second_part = norm_back(
-        grad_normed_second, scaled_second, inverse_second, gain_second
-    )
-    grad_residual = cotangent.astype(f32) + grad_from_norm
+        grad_normed_second, scaled_second, inverse_second, gain_two
+    )
+    grad_residual = cot_here.astype(f32) + grad_from_norm
     grad_low = grad_residual.astype(bf16)
     grad_context, query_x = to_heads(contract(grad_low, out_whole, 1, 1).astype(bf16), query_0, 5)
-    grad_out = contract(context_own, grad_low, 0, 0).astype(bf16)
+
+    def rows_reduce(total):
+        for mask in [CORE] + grid.rest:
+            half = total.shape[0] // 2
+            total = halves_sum(total[:half], total[half:], mask)
+        width = total.shape[0] // 2
+        side = grid.bit(SIDE)
+        keep = lax.dynamic_slice_in_dim(total, side * width, width, 0)
+        give = lax.dynamic_slice_in_dim(total, (1 - side) * width, width, 0)
+        return halves_sum(keep, give, SIDE)
+
+    grad_out_t = rows_reduce(contract(grad_low, context_own, 0, 0))
+    pieces = grid.exchange_mp(grad_out_t.astype(bf16), 1, 0).astype(f32)
+    out_shard = jnp.sum(pieces.reshape(4, -1, pieces.shape[1]), axis=0).T
+
     grad_queries, grad_keys, grad_values = attend_back(
         starts, queries, keys, values, grad_context, log_totals)
     grad_kv = jnp.stack([grad_keys, grad_values], axis=1)
-    grad_query = contract(rows_first, grad_queries, 0, 0).astype(bf16)
+    query_shard = rows_reduce(contract(rows_first, grad_queries, 0, 0))
     grad_queries_own, query_whole = to_tokens_last(grad_queries, query_y, query_0, query_x, 6)
     grad_normed_first = contract(grad_queries_own, query_whole, 1, 1)
     grad_from_first, gain_first_part = norm_back(
-        grad_normed_first, scaled_first, inverse_first, gain_first
-    )
-    grad_input = grad_residual + grad_from_first
-    gains = jnp.stack([gain_first_part, gain_second_part]).reshape(-1, 256)
-    down_shard, gate_shard, up_shard, out_shard, query_shard, ffn_sum, gain_sums = reduce_call(
-        grad_down, grad_gate, grad_up, grad_out, grad_query, ffn_parts, gains, 7)
-    output = (residual + ffn_sum).astype(bf16)
-    gain_sums = gain_sums.reshape(2, -1)
+        grad_normed_first, scaled_first, inverse_first, gain_one
+    )
+    grad_input = grid.restore(grad_residual + grad_from_first)
+    gains = jnp.stack([grid.restore(gain_first_part), grid.restore(gain_second_part)]).reshape(-1, 256)
+    gain_sums = all_sum(gains, 7).reshape(2, -1)
     return (output, grad_input, grad_kv, gain_sums[0], gain_sums[1], query_shard, out_shard,
-            gate_shard.T, up_shard.T, down_shard)
+            gate_shard, up_shard, down_shard)
 
 
 def solution(mesh):

time: 763 us -> 745 us (0.976)
  Pallas kernels: 592 us -> 449 us
  waiting for transfers between devices: 0 us -> 109 us
  matrix products: 112 us -> 32.3 us
  local copies, waits for them, and re-layouts: 32.9 us -> 76.8 us
  other arithmetic: 12.6 us -> 42.1 us
  starting transfers between devices: 0 us -> 24.9 us
    pallas_call x3 -> x2, Pallas kernels: 294 us -> 141 us  [the longest x1 99.3 us: ffn_call(): pl.pallas_call(ffn_kernel, out_shape=(jax.ShapeDtypeStruct((share, width)...]
    ppermute x0 -> x19, waiting for transfers between devices: none -> 107 us  [swap(): lax.ppermute(value, ('dp', 'mp'), [(i, i ^ mask) for i in range(self.size)])]
    dot_general x15 -> x6, matrix products: 112 us -> 32.3 us  [contract(): lax.dot_general(left, right, (((left_dim,), (right_dim,)), ((), ())), pre...]
    add x2 -> x13, other arithmetic: 2.5 us -> 25.3 us  [the longest x11 22.2 us: halves_sum(): return keep.astype(f32) + grid.swap(give.astype(bf16), mask).astype(f32)]
    ppermute x0 -> x19, starting transfers between devices: none -> 21.4 us  [swap(): lax.ppermute(value, ('dp', 'mp'), [(i, i ^ mask) for i in range(self.size)])]
    squeeze x0 -> x1, local copies, waits for them, and re-layouts: none -> 15.4 us  [fast_body(): down_shard = ffn_grad(ffn_sums[0])]
    slice x0 -> x11, local copies, waits for them, and re-layouts: none -> 13.6 us  [the longest x4 5.49 us: rows_reduce(): total = halves_sum(total[:half], total[half:], mask)]
    unnamed x107 -> x168, local copies, waits for them, and re-layouts: 27.4 us -> 38.9 us
  transfers between devices with their start and end apart: 0 -> 20, of which waited for: 0 -> 10; matrix products, arithmetic and copies ran while one was open for 0% -> 12% of each run, Pallas kernels for 0% -> 15%
where the time goes in v2:
time: 745 us; the launch traced here: 736 us
  Pallas kernels  449 us (60%)
  waiting for transfers between devices  109 us (15%)
  local copies, waits for them, and re-layouts  76.8 us (10%)
  other arithmetic  42.1 us (6%)
  matrix products  32.3 us (4%)
  starting transfers between devices  24.9 us (3%)
    pallas_call x1, Pallas kernels, gather_call(): pl.pallas_call(gather_kernel, out_shape=tuple((jax.ShapeDtypeStruct(s, bf...  201 us
    ppermute x19, waiting for transfers between devices, swap(): lax.ppermute(value, ('dp', 'mp'), [(i, i ^ mask) for i in range(self.size)])  107 us
    pallas_call x1, Pallas kernels, ffn_call(): pl.pallas_call(ffn_kernel, out_shape=(jax.ShapeDtypeStruct((share, width)...  99.3 us
    pallas_call x1, Pallas kernels, all_sum(): pl.pallas_call(all_sum_kernel, out_shape=jax.ShapeDtypeStruct(value.shape...  41.8 us
    unnamed x168, local copies, waits for them, and re-layouts  38.9 us
    dot_general x6, matrix products, contract(): lax.dot_general(left, right, (((left_dim,), (right_dim,)), ((), ())), pre...  32.3 us
    pallas_call x1, Pallas kernels, to_tokens_last(): pl.pallas_call(tokens_kernel, out_shape=(jax.ShapeDtypeStruct(shape, bf16...  29.9 us
    pallas_call x1, Pallas kernels, to_heads(): pl.pallas_call(heads_hop_kernel, out_shape=(jax.ShapeDtypeStruct(shape, b...  29 us
  transfers between devices with their start and end apart: 20, of which 10 were waited for; matrix products, arithmetic and copies ran while one was open for 12% of the time, Pallas kernels for 15%

profile of v2, /device:TPU:0, one launch (start us, length us, event | category | flops | bytes accessed | tf_op | source)
XLA Modules:
  0.0 736.1 jit_solution(14659803803181656945)
XLA Ops:
  9.7 3.0 fusion.15
  14.4 200.6 %gather_all.1 = (bf16[1024,2048]{1,0:T(8,128)(2,1)S(1)}, bf16[1024,2048]{1,0:T(8,128)(2,1)S(1)}, bf16[2048,512]{1,0:T(8,128)(2,1)S(1)}, bf16[256,2048]{1,0:T(8,1...) custom-call(bf16[256,2048]{1,0:T(8,128)(2,1)S(1)} %fusion.4.first, ...), custom_call_target="tpu_custom_call" | custom-call | tf_op jit(solution)/shard_map/gather_all/pallas_call | solution.py:283
  215.0 2.4 copy-done.17
  219.5 3.9 convolution_convert_fusion.1.q_ref
  227.1 8.8 %attend.1 = (bf16[1024,512]{1,0:T(8,128)(2,1)}, f32[4,1,1024]{2,1,0:T(1,128)}) custom-call(s32[1,1024]{1,0:T(1,128)} %bitcast.52, bf16[1024,512]{1,0:T(8,128)(2,1)} %convolution_convert_fusion.1.q_ref, bf16[1024,512]{1,0:T(8,128)(2,1)} %get-tuple-element.107.k_ref, bf16[1024,512]{1,0:T(8,128)(2,1)} %get-tuple-element.106.v_ref), custom_call_target="tpu_custom_call" | custom-call | flops 1610612736 | bytes 4194304 | tf_op jit(solution)/shard_map/attend/pallas_call | solution.py:594
  237.2 26.3 %to_tokens.1 = (bf16[256,2048]{1,0:T(8,128)(2,1)S(1)}, bf16[256,2048]{1,0:T(8,128)(2,1)S(1)}) custom-call(bf16[1024,512]{1,0:T(8,128)(2,1)S(1)} %copy-done.6, bf16[256,2048]{1,0:T(8,128)(2,1)S(1)} %get-tuple-element.35.block.query_0), custom_call_target="tpu_custom_call" | custom-call | tf_op jit(solution)/shard_map/to_tokens/pallas_call | solution.py:366
  263.5 6.6 multiply_reduce_fusion.2
  272.6 99.3 %feed_forward.1 = (f32[256,2048]{1,0:T(8,128)}, bf16[1024,2048]{1,0:T(8,128)(2,1)}, bf16[3,1376,1024]{2,1,0:T(8,128)(2,1)}) custom-call(bf16[256,2048]{1,0:T(8,128)(2,1)} %multiply_convert_fusion.normed, bf16[1024,2048]{1,0:T(8,128)(2,1)} %copy-done.19, bf16[1376,2048]{1,0:T(8,128)(2,1)} %copy-done.17, bf16[1376,2048]{1,0:T(8,128)(2,1)} %copy-done.15, ...), custom_call_target="tpu_custom_call" | custom-call | flops 51942260736 | bytes 41943040 | tf_op jit(solution)/shard_map/feed_forward/pallas_call | solution.py:768
  372.0 15.4 %slice_bitcast_fusion = (bf16[1376,1024]{1,0:T(8,128)(2,1)S(1)}, bf16[1376,1024]{1,0:T(8,128)(2,1)S(1)}, bf16[1376,1024]{1,0:T(8,128)(2,1)S(1)}) fusion(bf16[3,1376,1024]{2,1,0:T(8,128)(2,1)} %get-tuple-element.53), kind=kLoop, calls=%fused_computation.14 | loop fusion | bytes 16908288 | tf_op jit(solution)/shard_map/squeeze | solution.py:1148
  400.7 7.0 collective-permute-done
  412.0 11.0 %collective-permute-done.16 = bf16[1376,512]{1,0:T(8,128)(2,1)} collective-permute-done((bf16[1376,512]{1,0:T(8,128)(2,1)}, bf16[1376,512]{1,0:T(8,128)(2,1)}, u32[]{:S(2)}, u32[]{:S(2)}) %collective-permute-start.16) | collective-permute-done | bytes 1409056 | tf_op jit(solution)/shard_map/ppermute | solution.py:800
  428.2 25.1 %collective-permute-done.13 = bf16[1376,512]{1,0:T(8,128)(2,1)} collective-permute-done((bf16[1376,512]{1,0:T(8,128)(2,1)}, bf16[1376,512]{1,0:T(8,128)(2,1)}, u32[]{:S(2)}, u32[]{:S(2)}) %collective-permute-start.13) | collective-permute-done | bytes 1409056 | tf_op jit(solution)/shard_map/ppermute | solution.py:800
  458.4 22.6 %collective-permute-done.10 = bf16[1376,512]{1,0:T(8,128)(2,1)} collective-permute-done((bf16[1376,512]{1,0:T(8,128)(2,1)}, bf16[1376,512]{1,0:T(8,128)(2,1)}, u32[]{:S(2)}, u32[]{:S(2)}) %collective-permute-start.10) | collective-permute-done | bytes 1409056 | tf_op jit(solution)/shard_map/ppermute | solution.py:800
  485.4 2.6 multiply_add_fusion
  490.4 11.7 %convolution_convert_fusion.own = bf16[256,2048]{1,0:T(8,128)(2,1)S(1)} fusion(bf16[2048,2048]{1,0:T(8,128)(2,1)} %get-tuple-element.37, f32[256,2048]{1,0:T(8,128)S(1)} %get-tuple-element.87), kind=kOutput, calls=%fused_computation.19 | convolution fusion | flops 2148532224 | bytes 11534336 | tf_op jit(solution)/shard_map/dot_general | solution.py:883
  502.2 2.7 slice.211
  504.9 29.0 %to_heads.1 = (bf16[1024,512]{1,0:T(8,128)(2,1)S(1)}, bf16[256,2048]{1,0:T(8,128)(2,1)S(1)}) custom-call(bf16[256,2048]{1,0:T(8,128)(2,1)S(1)} %convolution_convert_fusion.own, bf16[256,2048]{1,0:T(8,128)(2,1)S(1)} %copy-done.1), custom_call_target="tpu_custom_call" | custom-call | tf_op jit(solution)/shard_map/to_heads/pallas_call | solution.py:386
  534.9 13.1 %attend_back.1 = (bf16[1024,512]{1,0:T(8,128)(2,1)}, f32[1024,512]{1,0:T(8,128)}, f32[1024,512]{1,0:T(8,128)}) custom-call(s32[1,1024]{1,0:T(1,128)} %bitcast.53, bf16[1024,512]{1,0:T(8,128)(2,1)} %convolution_convert_fusion.1.q_ref, bf16[1024,512]{1,0:T(8,128)(2,1)} %get-tuple-element.107.k_ref, bf16[1024,512]{1,0:T(8,128)(2,1)} %get-tuple-element.106.v_ref, ...), custom_call_target="tpu_custom_call" | custom-call | flops 3758096384 | bytes 9437184 | tf_op jit(solution)/shard_map/attend_back/pallas_call | solution.py:609
  548.0 4.9 fusion.16
  556.0 29.9 %to_tokens_last.1 = (bf16[256,2048]{1,0:T(8,128)(2,1)S(1)}, bf16[2048,2048]{1,0:T(8,128)(2,1)S(1)}) custom-call(bf16[1024,512]{1,0:T(8,128)(2,1)S(1)} %copy-done.9, bf16[256,2048]{1,0:T(8,128)(2,1)S(1)} %copy-done.8, bf16[256,2048]{1,0:T(8,128)(2,1)S(1)} %copy-done.1, bf16[256,2048]{1,0:T(8,128)(2,1)S(1)} %get-tuple-element.48.query_x), custom_call_target="tpu_custom_call" | custom-call | tf_op jit(solution)/shard_map/to_tokens_last/pallas_call | solution.py:376
  585.9 2.7 fusion.9
  595.4 5.9 slice_add_fusion
  606.6 2.4 pad_maximum_fusion
  609.7 41.8 %all_sum.1 = f32[16,256]{1,0:T(8,128)S(1)} custom-call(f32[16,256]{1,0:T(8,128)S(1)} %reshape.59.value), custom_call_target="tpu_custom_call" | custom-call | tf_op jit(solution)/shard_map/all_sum/pallas_call | solution.py:513
  654.1 7.6 %copy.26 = f32[1024,2,512]{2,1,0:T(2,128)} copy(f32[1024,2,512]{2,0,1:T(8,128)} %pad_maximum_fusion) | data formatting | bytes 8388608
  668.7 2.6 slice_add_fusion.1
  676.4 7.4 %collective-permute-done.15 = bf16[688,256]{1,0:T(8,128)(2,1)S(1)} collective-permute-done((bf16[688,256]{1,0:T(8,128)(2,1)S(1)}, bf16[688,256]{1,0:T(8,128)(2,1)S(1)}, u32[]{:S(2)}, u32[]{:S(2)}) %collective-permute-start.15) | collective-permute-done | bytes 352288 | tf_op jit(solution)/shard_map/ppermute | solution.py:800
  686.0 20.3 %collective-permute-done.9 = bf16[256,2048]{0,1:T(8,128)(2,1)S(1)} collective-permute-done((bf16[256,2048]{0,1:T(8,128)(2,1)S(1)}, bf16[256,2048]{0,1:T(8,128)(2,1)S(1)}, u32[]{:S(2)}, u32[]{:S(2)}) %collective-permute-start.9) | collective-permute-done | bytes 1048608 | tf_op jit(solution)/shard_map/ppermute | solution.py:800
  707.7 3.5 all-to-all-start
  716.2 8.6 %collective-permute-done.5 = bf16[512,512]{1,0:T(8,128)(2,1)S(1)} collective-permute-done((bf16[512,512]{1,0:T(8,128)(2,1)S(1)}, bf16[512,512]{1,0:T(8,128)(2,1)S(1)}, u32[]{:S(2)}, u32[]{:S(2)}) %collective-permute-start.5) | collective-permute-done | bytes 524320 | tf_op jit(solution)/shard_map/ppermute | solution.py:800
  727.7 3.8 collective-permute-done.6
  732.4 2.4 all-to-all-done
  (258 shorter events, 98.7 us)
Async XLA Ops:
  8.5 255.0 %copy-start.33 = (bf16[256,2048]{1,0:T(8,128)(2,1)}, bf16[256,2048]{1,0:T(8,128)(2,1)S(1)}, u32[]{:S(2)}) copy-start(bf16[256,2048]{1,0:T(8,128)(2,1)S(1)} %dynamic-slice_dynamic-update-slice_fusion.24) | copy-start | bytes 3145732
  219.4 16.5 %copy-start = (bf16[256,2048]{1,0:T(8,128)(2,1)}, bf16[256,2048]{1,0:T(8,128)(2,1)S(1)}, u32[]{:S(2)}) copy-start(bf16[256,2048]{1,0:T(8,128)(2,1)S(1)} %get-tuple-element.35.block.query_0) | copy-start | bytes 3145732
  388.9 34.1 %collective-permute-start.16 = (bf16[1376,512]{1,0:T(8,128)(2,1)}, bf16[1376,512]{1,0:T(8,128)(2,1)}, u32[]{:S(2)}, u32[]{:S(2)}) collective-permute-start(bf16[1376,512]{1,0:T(8,128)(2,1)} %slice.181), channel_id=1, source_target_pairs={{0,16},{1,17},{2,18},{3,19},{4,20},{5,21},{6,22},{7,23},{8,24},{9,... | collective-permute-start | bytes 4227080 | tf_op jit(solution)/shard_map/ppermute | solution.py:800
  391.4 61.8 %collective-permute-start.13 = (bf16[1376,512]{1,0:T(8,128)(2,1)}, bf16[1376,512]{1,0:T(8,128)(2,1)}, u32[]{:S(2)}, u32[]{:S(2)}) collective-permute-start(bf16[1376,512]{1,0:T(8,128)(2,1)} %slice.177), channel_id=1, source_target_pairs={{0,16},{1,17},{2,18},{3,19},{4,20},{5,21},{6,22},{7,23},{8,24},{9,... | collective-permute-start | bytes 4227080 | tf_op jit(solution)/shard_map/ppermute | solution.py:800
  393.4 87.5 %collective-permute-start.10 = (bf16[1376,512]{1,0:T(8,128)(2,1)}, bf16[1376,512]{1,0:T(8,128)(2,1)}, u32[]{:S(2)}, u32[]{:S(2)}) collective-permute-start(bf16[1376,512]{1,0:T(8,128)(2,1)} %slice.173), channel_id=1, source_target_pairs={{0,16},{1,17},{2,18},{3,19},{4,20},{5,21},{6,22},{7,23},{8,24},{9,... | collective-permute-start | bytes 4227080 | tf_op jit(solution)/shard_map/ppermute | solution.py:800
  395.8 11.9 %collective-permute-start = (bf16[128,2048]{1,0:T(8,128)(2,1)}, bf16[128,2048]{1,0:T(8,128)(2,1)}, u32[]{:S(2)}, u32[]{:S(2)}) collective-permute-start(bf16[128,2048]{1,0:T(8,128)(2,1)} %get-tuple-element.84), channel_id=1, source_target_pairs={{0,1},{1,0},{2,3},{3,2},{4,5},{5,4},{6,7},{7,6},{8,9},{9,8},{10,11... | collective-permute-start | bytes 1572872 | tf_op jit(solution)/shard_map/ppermute | solution.py:800
  395.8 11.9 %collective-permute-start.2 = (bf16[128,2048]{1,0:T(8,128)(2,1)}, bf16[128,2048]{1,0:T(8,128)(2,1)}, u32[]{:S(2)}, u32[]{:S(2)}) collective-permute-start(bf16[128,2048]{1,0:T(8,128)(2,1)} %get-tuple-element.83), channel_id=1, source_target_pairs={{0,8},{1,9},{2,10},{3,11},{4,12},{5,13},{6,14},{7,15},{8,0},{9,1},... | collective-permute-start | bytes 1572872 | tf_op jit(solution)/shard_map/ppermute | solution.py:800
  409.7 13.4 %copy-start.32 = (bf16[1376,1024]{1,0:T(8,128)(2,1)S(1)}, bf16[1376,1024]{1,0:T(8,128)(2,1)}, u32[]{:S(2)}) copy-start(bf16[1376,1024]{1,0:T(8,128)(2,1)} %copy-done.31) | copy-start | bytes 8454148
  409.8 75.6 %collective-permute-start.1 = (bf16[256,2048]{1,0:T(8,128)(2,1)S(1)}, bf16[256,2048]{1,0:T(8,128)(2,1)S(1)}, u32[]{:S(2)}, u32[]{:S(2)}) collective-permute-start(bf16[256,2048]{1,0:T(8,128)(2,1)S(1)} %pad_maximum_fusion.2), channel_id=1, source_target_pairs={{0,8},{1,9},{2,10},{3,11},{4,12},{5,13},{6,14},{7,15},{8,0},{9,1},... | collective-permute-start | bytes 3145736 | tf_op jit(solution)/shard_map/ppermute | solution.py:800
  411.6 73.8 %collective-permute-start.3 = (bf16[256,2048]{1,0:T(8,128)(2,1)S(1)}, bf16[256,2048]{1,0:T(8,128)(2,1)S(1)}, u32[]{:S(2)}, u32[]{:S(2)}) collective-permute-start(bf16[256,2048]{1,0:T(8,128)(2,1)S(1)} %pad_maximum_fusion.3), channel_id=1, source_target_pairs={{0,1},{1,0},{2,3},{3,2},{4,5},{5,4},{6,7},{7,6},{8,9},{9,8},{10,11... | collective-permute-start | bytes 3145736 | tf_op jit(solution)/shard_map/ppermute | solution.py:800
  423.0 30.2 %copy-start.30 = (bf16[1376,1024]{1,0:T(8,128)(2,1)S(1)}, bf16[1376,1024]{1,0:T(8,128)(2,1)}, u32[]{:S(2)}) copy-start(bf16[1376,1024]{1,0:T(8,128)(2,1)} %copy-done.29) | copy-start | bytes 8454148
  425.0 30.2 %copy-start.37 = (f32[1376,512]{1,0:T(8,128)}, f32[1376,512]{1,0:T(8,128)S(1)}, u32[]{:S(2)}) copy-start(f32[1376,512]{1,0:T(8,128)S(1)} %convert_add_fusion.1) | copy-start | bytes 8454148
  426.1 237.0 %collective-permute-start.17 = (bf16[688,512]{1,0:T(8,128)(2,1)}, bf16[688,512]{1,0:T(8,128)(2,1)}, u32[]{:S(2)}, u32[]{:S(2)}) collective-permute-start(bf16[688,512]{1,0:T(8,128)(2,1)} %slice.214), channel_id=1, source_target_pairs={{0,2},{1,3},{2,0},{3,1},{4,6},{5,7},{6,4},{7,5},{8,10},{9,11},{10,... | collective-permute-start | bytes 2113544 | tf_op jit(solution)/shard_map/ppermute | solution.py:800
  453.2 27.7 %copy-start.28 = (bf16[1376,1024]{1,0:T(8,128)(2,1)S(1)}, bf16[1376,1024]{1,0:T(8,128)(2,1)}, u32[]{:S(2)}) copy-start(bf16[1376,1024]{1,0:T(8,128)(2,1)} %copy-done.27) | copy-start | bytes 8454148
  455.3 27.7 %copy-start.39 = (f32[1376,512]{1,0:T(8,128)}, f32[1376,512]{1,0:T(8,128)S(1)}, u32[]{:S(2)}) copy-start(f32[1376,512]{1,0:T(8,128)S(1)} %convert_add_fusion.2) | copy-start | bytes 8454148
  456.3 210.1 %collective-permute-start.14 = (bf16[688,512]{1,0:T(8,128)(2,1)}, bf16[688,512]{1,0:T(8,128)(2,1)}, u32[]{:S(2)}, u32[]{:S(2)}) collective-permute-start(bf16[688,512]{1,0:T(8,128)(2,1)} %slice.215), channel_id=1, source_target_pairs={{0,2},{1,3},{2,0},{3,1},{4,6},{5,7},{6,4},{7,5},{8,10},{9,11},{10,... | collective-permute-start | bytes 2113544 | tf_op jit(solution)/shard_map/ppermute | solution.py:800
  483.9 188.9 %collective-permute-start.11 = (bf16[688,512]{1,0:T(8,128)(2,1)}, bf16[688,512]{1,0:T(8,128)(2,1)}, u32[]{:S(2)}, u32[]{:S(2)}) collective-permute-start(bf16[688,512]{1,0:T(8,128)(2,1)} %slice.216), channel_id=1, source_target_pairs={{0,2},{1,3},{2,0},{3,1},{4,6},{5,7},{6,4},{7,5},{8,10},{9,11},{10,... | collective-permute-start | bytes 2113544 | tf_op jit(solution)/shard_map/ppermute | solution.py:800
  490.4 11.7 %copy-start.21 = (f32[2048,2048]{0,1:T(8,128)}, f32[2048,2048]{0,1:T(8,128)S(1)}, u32[]{:S(2)}) copy-start(f32[2048,2048]{0,1:T(8,128)S(1)} %fusion.11) | copy-start | bytes 50331652
  504.9 90.5 %collective-permute-start.7 = (bf16[1024,2048]{0,1:T(8,128)(2,1)}, bf16[1024,2048]{0,1:T(8,128)(2,1)}, u32[]{:S(2)}, u32[]{:S(2)}) collective-permute-start(bf16[1024,2048]{0,1:T(8,128)(2,1)} %slice.211), channel_id=1, source_target_pairs={{0,4},{1,5},{2,6},{3,7},{4,0},{5,1},{6,2},{7,3},{8,12},{9,13},{10,... | collective-permute-start | bytes 12582920 | tf_op jit(solution)/shard_map/ppermute | solution.py:800
  554.0 157.2 %collective-permute-start.4 = (bf16[1024,512]{1,0:T(8,128)(2,1)}, bf16[1024,512]{1,0:T(8,128)(2,1)}, u32[]{:S(2)}, u32[]{:S(2)}) collective-permute-start(bf16[1024,512]{1,0:T(8,128)(2,1)} %slice.213), channel_id=1, source_target_pairs={{0,4},{1,5},{2,6},{3,7},{4,0},{5,1},{6,2},{7,3},{8,12},{9,13},{10,... | collective-permute-start | bytes 3145736 | tf_op jit(solution)/shard_map/ppermute | solution.py:800
  556.0 29.9 %copy-start.34 = (bf16[256,2048]{1,0:T(8,128)(2,1)S(1)}, bf16[256,2048]{1,0:T(8,128)(2,1)}, u32[]{:S(2)}) copy-start(bf16[256,2048]{1,0:T(8,128)(2,1)} %copy-done.33) | copy-start | bytes 3145732
  602.9 65.7 %collective-permute-start.8 = (bf16[512,2048]{0,1:T(8,128)(2,1)}, bf16[512,2048]{0,1:T(8,128)(2,1)}, u32[]{:S(2)}, u32[]{:S(2)}) collective-permute-start(bf16[512,2048]{0,1:T(8,128)(2,1)} %slice.212), channel_id=1, source_target_pairs={{0,16},{1,17},{2,18},{3,19},{4,20},{5,21},{6,22},{7,23},{8,24},{9,... | collective-permute-start | bytes 6291464 | tf_op jit(solution)/shard_map/ppermute | solution.py:800
  654.1 9.0 %copy-start.38 = (f32[1376,512]{1,0:T(8,128)S(1)}, f32[1376,512]{1,0:T(8,128)}, u32[]{:S(2)}) copy-start(f32[1376,512]{1,0:T(8,128)} %copy-done.37) | copy-start | bytes 8454148
  654.1 12.3 %copy-start.40 = (f32[1376,512]{1,0:T(8,128)S(1)}, f32[1376,512]{1,0:T(8,128)}, u32[]{:S(2)}) copy-start(f32[1376,512]{1,0:T(8,128)} %copy-done.39) | copy-start | bytes 8454148
  654.1 14.5 %slice-start = ((s8[8388608]{0:T(1024)(128)(4,1)}), s8[4194304]{0:T(1024)(128)(4,1)S(1)}, s32[]{:S(2)}) async-start(s8[8388608]{0:T(1024)(128)(4,1)} %bitcast.42), calls=%async_computation.1 | async-start | bytes 8388608
  665.1 11.2 %collective-permute-start.18 = (bf16[688,256]{1,0:T(8,128)(2,1)S(1)}, bf16[688,256]{1,0:T(8,128)(2,1)S(1)}, u32[]{:S(2)}, u32[]{:S(2)}) collective-permute-start(bf16[688,256]{1,0:T(8,128)(2,1)S(1)} %dynamic-slice_convert_fusion.1), channel_id=1, source_target_pairs={{0,8},{1,9},{2,10},{3,11},{4,12},{5,13},{6,14},{7,15},{8,0},{9,1},... | collective-permute-start | bytes 1056776 | tf_op jit(solution)/shard_map/ppermute | solution.py:800
  667.9 15.9 %collective-permute-start.15 = (bf16[688,256]{1,0:T(8,128)(2,1)S(1)}, bf16[688,256]{1,0:T(8,128)(2,1)S(1)}, u32[]{:S(2)}, u32[]{:S(2)}) collective-permute-start(bf16[688,256]{1,0:T(8,128)(2,1)S(1)} %dynamic-slice_convert_fusion.2), channel_id=1, source_target_pairs={{0,8},{1,9},{2,10},{3,11},{4,12},{5,13},{6,14},{7,15},{8,0},{9,1},... | collective-permute-start | bytes 1056776 | tf_op jit(solution)/shard_map/ppermute | solution.py:800
  671.4 34.9 %collective-permute-start.9 = (bf16[256,2048]{0,1:T(8,128)(2,1)S(1)}, bf16[256,2048]{0,1:T(8,128)(2,1)S(1)}, u32[]{:S(2)}, u32[]{:S(2)}) collective-permute-start(bf16[256,2048]{0,1:T(8,128)(2,1)S(1)} %dynamic-slice_convert_fusion), channel_id=1, source_target_pairs={{0,8},{1,9},{2,10},{3,11},{4,12},{5,13},{6,14},{7,15},{8,0},{9,1},... | collective-permute-start | bytes 3145736 | tf_op jit(solution)/shard_map/ppermute | solution.py:800
  675.0 39.9 %collective-permute-start.12 = (bf16[688,256]{1,0:T(8,128)(2,1)}, bf16[688,256]{1,0:T(8,128)(2,1)S(1)}, u32[]{:S(2)}, u32[]{:S(2)}) collective-permute-start(bf16[688,256]{1,0:T(8,128)(2,1)} %dynamic-slice_convert_fusion.3), channel_id=1, source_target_pairs={{0,8},{1,9},{2,10},{3,11},{4,12},{5,13},{6,14},{7,15},{8,0},{9,1},... | collective-permute-start | bytes 1056776 | tf_op jit(solution)/shard_map/ppermute | solution.py:800
  707.7 27.1 %all-to-all-start = ((bf16[256,4,512]{0,2,1:T(8,128)(2,1)}), bf16[256,4,512]{0,2,1:T(8,128)(2,1)S(1)}, u32[]{:S(2)}, u32[]{:S(2)}) async-start(bf16[256,4,512]{0,2,1:T(8,128)(2,1)} %bitcast.10), calls=%async_computation | async-start | bytes 2097152 | tf_op jit(solution)/shard_map/all_to_all | solution.py:848
  713.5 11.3 %collective-permute-start.5 = (bf16[512,512]{1,0:T(8,128)(2,1)S(1)}, bf16[512,512]{1,0:T(8,128)(2,1)S(1)}, u32[]{:S(2)}, u32[]{:S(2)}) collective-permute-start(bf16[512,512]{1,0:T(8,128)(2,1)S(1)} %slice.217), channel_id=1, source_target_pairs={{0,16},{1,17},{2,18},{3,19},{4,20},{5,21},{6,22},{7,23},{8,24},{9,... | collective-permute-start | bytes 1572872 | tf_op jit(solution)/shard_map/ppermute | solution.py:800
  725.1 6.4 collective-permute-start.6
  (43 other events, 172.6 us)

commit v3 on v2

--- a/solution.py
+++ b/solution.py
@@ -782,6 +782,362 @@
     )(normed, cots, down, gate, up)
 
 
+def absolute(place, spot):
+    core, deep, side = spot // 4, (spot // 2) % 2, spot % 2
+    return place.flip(place.dp, core + 4 * deep) - 2 * place.bit(SIDE) + 2 * side
+
+
+def back_first_kernel(dn2, residual, cot, gain, context, out_whole, sums, query_0,
+                      dres, heads, gain_part, query_x, down_sums, out_sums,
+                      keep_d, deep_d, grad_low, wout, dctx, give_o, core_o,
+                      send_sems, recv_sems, local_sems):
+    place = Place()
+    mp = place.mp
+    share, width = dn2.shape
+    hidden = keep_d.shape[0]
+    local = heads.shape[1]
+    wide = width // 2
+    copies = Copies(place, send_sems, recv_sems, local_sems)
+    loads = [copies.local(out_whole.at[pl.ds(z * local, local), :], wout.at[z]) for z in range(4)]
+    load_d = copies.local(sums.at[0, :, pl.ds(0, wide // 2)], keep_d)
+    greet(place, (1, 2, 3, CORE, SIDE, DEEP))
+    in_d = copies.swap(sums.at[0, :, pl.ds(wide // 2, wide // 2)], deep_d, DEEP)
+    copies.swap(query_0, query_x, SIDE)
+    gain_part[...] = jnp.zeros_like(gain_part)
+
+    def norm(i, carry):
+        here = pl.ds(i * 32, 32)
+        value = residual[here, :]
+        inverse = lax.rsqrt(jnp.mean(value * value, axis=-1, keepdims=True) + epsilon)
+        scaled = value * inverse
+        grad = dn2[here, :]
+        grad_scaled = grad * gain[...]
+        back = inverse * (grad_scaled - scaled * jnp.mean(grad_scaled * scaled, axis=-1, keepdims=True))
+        total = cot[here, :].astype(f32) + back
+        dres[here, :] = total
+        grad_low[here, :] = total.astype(bf16)
+        gain_part[...] += jnp.sum(grad * scaled, axis=0, keepdims=True)
+        return carry
+
+    lax.fori_loop(0, share // 32, norm, 0)
+    for copy in loads:
+        copy.wait()
+    for mask in (2, 3, 1, 0):
+        other = place.partner(mask)[1]
+        there = pl.ds(pl.multiple_of(other * local, local), local)
+        piece = dot(grad_low[...], wout[other], 1, 1).astype(bf16)
+        if mask:
+            dctx[:, there] = piece
+            copies.swap(dctx.at[:, there], heads.at[pl.ds(mp * share, share), :], mask)
+        else:
+            heads[pl.ds(mp * share, share), :] = piece
+    chunks = width // 512
+    base = copies.count
+    copies.count += chunks
+
+    def core_copy(n):
+        rows = pl.ds(pl.multiple_of(n * 512, 512), 512)
+        return copies.describe(give_o.at[rows, :], core_o.at[rows, :], place.partner(CORE), base + n)
+
+    def give(n, carry):
+        rows = pl.ds(pl.multiple_of(n * 512, 512), 512)
+        give_o[rows, :] = dot(context[:, rows], grad_low[:, wide:], 0, 0).astype(bf16)
+        core_copy(n).start()
+        return carry
+
+    lax.fori_loop(0, chunks, give, 0)
+
+    def keep(n, carry):
+        rows = pl.ds(pl.multiple_of(n * 512, 512), 512)
+        core_copy(n).wait_recv()
+        out_sums[rows, :] = (dot(context[:, rows], grad_low[:, :wide], 0, 0)
+                             + core_o[rows, :].astype(f32)).astype(bf16)
+        return carry
+
+    lax.fori_loop(0, chunks, keep, 0)
+    load_d.wait()
+    copies.got(in_d)
+
+    def add_d(n, carry):
+        rows = pl.ds(n * 32, 32)
+        down_sums[rows, :] = (keep_d[rows, :].astype(f32) + deep_d[rows, :].astype(f32)).astype(bf16)
+        return carry
+
+    lax.fori_loop(0, hidden // 32, add_d, 0)
+    copies.finish()
+
+    def sent(n, carry):
+        core_copy(n).wait_send()
+        return carry
+
+    lax.fori_loop(0, chunks, sent, 0)
+
+
+def back_first(dn2, residual, cot, gain, context, out_whole, sums, query_0, ident):
+    share, width = dn2.shape
+    hidden = sums.shape[1]
+    V = pltpu.VMEM
+    S = jax.ShapeDtypeStruct
+    return pl.pallas_call(
+        back_first_kernel,
+        out_shape=(S((share, width), f32), S((share * 4, width // 4), bf16), S((1, width), f32),
+                   S(query_0.shape, bf16), S((hidden, width // 4), bf16), S((width, width // 2), bf16)),
+        in_specs=[VM] * 5 + [ANY, ANY, VM],
+        out_specs=(VM,) * 6,
+        scratch_shapes=[
+            V((hidden, width // 4), bf16), V((hidden, width // 4), bf16), V((share, width), bf16),
+            V((4, width // 4, width), bf16), V((share, width), bf16), V((width, width // 2), bf16),
+            V((width, width // 2), bf16), DMA((12,)), DMA((12,)), DMA((5,))],
+        compiler_params=params(ident, 60 << 20), name="back_first",
+    )(dn2, residual, cot, gain, context, out_whole, sums, query_0)
+
+
+def back_last_kernel(grad_q, rows_first, dres, inputs, gain, query_y, query_0, query_x,
+                     sums, down_sums, out_sums, fparts, residual, gain_part,
+                     down, gate, up, out, query, grad_input, output, gains, query_whole,
+                     keep_f, deep_f, high_f, side_f, own_o, side_o, deep_o, z_o,
+                     give_q, own_q, core_q, side_q, deep_q, parts, relay, landed,
+                     grad_own, stream, dn1, gain_rows, gains_got,
+                     send_sems, recv_sems, local_sems):
+    place = Place()
+    mp = place.mp
+    side = place.bit(SIDE)
+    share, width = dres.shape
+    hidden, blk = down.shape
+    half = hidden // 2
+    local = grad_q.shape[1]
+    zrow = out.shape[0]
+    quarter = 2 * blk
+    copies = Copies(place, send_sems, recv_sems, local_sems)
+    load_rows = copies.local(rows_first, stream.at[pl.ds(0, share * 4), :])
+    load_d = copies.local(down_sums, keep_f.at[0])
+    load_p = copies.local(fparts, parts)
+    load_f = [copies.local(sums.at[i, :, pl.ds(0, quarter)], keep_f.at[i]) for i in (1, 2)]
+    load_o = copies.local(out_sums, own_o)
+
+    def qrows(spot):
+        return query_whole.at[pl.ds(spot * blk, blk), :]
+
+    greet(place, (1, 2, 3, CORE, SIDE, DEEP))
+    tokens_in = []
+    for mask in (2, 3, 1):
+        other = place.partner(mask)[1]
+        tokens_in.append(copies.swap(grad_q.at[pl.ds(other * share, share), :],
+                                     grad_own.at[:, pl.ds(mp * local, local)], mask))
+    wq_across = copies.swap(query_y, qrows(side + 2), SIDE)
+    deep_in = [None]
+    for i in (1, 2):
+        deep_in.append([copies.swap(sums.at[i, :, pl.ds(quarter + x * blk, blk)], deep_f.at[i - 1, :, pl.ds(x * blk, blk)], DEEP)
+                        for x in (0, 1)])
+    held = [copies.local(query_0, qrows(side)), copies.local(query_y, qrows(side + 2)),
+            copies.local(query_x, qrows(1 - side))]
+    wq_core = [copies.swap(query_0, qrows(side + 4), CORE), copies.swap(query_y, qrows(side + 6), CORE),
+               copies.swap(query_x, qrows(1 - side + 4), CORE)]
+    load_d.wait()
+    give_rows = pl.ds(half, half)
+    high_in = [[copies.swap(keep_f.at[0, give_rows, pl.ds(x * blk, blk)], high_f.at[0, :, pl.ds(x * blk, blk)], Z_HIGH)
+                for x in (0, 1)]]
+    grad_own[:, pl.ds(mp * local, local)] = grad_q[pl.ds(mp * share, share), :]
+    load_rows.wait()
+    wide = width // 2
+
+    def product(first):
+        return dot(stream[0:share * 4, first:first + wide], grad_q[...], 0, 0)
+
+    give_q[...] = product(wide).astype(bf16)
+    core_in_q = copies.swap(give_q, core_q, CORE)
+    load_p.wait()
+    reduce = QuadReduce(copies, parts, relay, landed)
+    reduce.start()
+    load_o.wait()
+
+    def block_o(spot):
+        return own_o.at[:, pl.ds(spot * blk, blk)]
+
+    side_in_o = {y: copies.swap(block_o(2 * y + 1 - side), side_o.at[y], SIDE) for y in (1, 0)}
+    keep_q = product(0)
+    copies.got(core_in_q)
+    own_q[...] = (keep_q + core_q[...].astype(f32)).astype(bf16)
+    side_in_q = {y: copies.swap(own_q.at[pl.ds((2 * y + 1 - side) * blk, blk), :], side_q.at[y], SIDE) for y in (1, 0)}
+    reduce.relayed()
+    for copy in held:
+        copy.wait()
+    for item in tokens_in:
+        copies.got(item)
+    copies.got(wq_across)
+    wq_core.append(copies.swap(qrows(1 - side + 2), qrows(1 - side + 6), CORE))
+    for item in wq_core:
+        copies.got(item)
+    load_wq = copies.local(query_whole, stream)
+    load_wq.wait()
+
+    def first_back(n, carry):
+        there = pl.ds(pl.multiple_of(n * 512, 512), 512)
+        dn1[:, there] = dot(grad_own[...], stream[there, :], 1, 1)
+        return carry
+
+    lax.fori_loop(0, width // 512, first_back, 0)
+    gain_rows[0:1, :] = jnp.zeros((1, width), f32)
+    gain_rows[1:2, :] = gain_part[...]
+
+    def norm(i, carry):
+        here = pl.ds(i * 32, 32)
+        value = inputs[here, :].astype(f32)
+        inverse = lax.rsqrt(jnp.mean(value * value, axis=-1, keepdims=True) + epsilon)
+        scaled = value * inverse
+        grad = dn1[here, :]
+        grad_scaled = grad * gain[...]
+        back = inverse * (grad_scaled - scaled * jnp.mean(grad_scaled * scaled, axis=-1, keepdims=True))
+        total = dres[here, :] + back
+        for spot in range(8):
+            there = pl.ds(pl.multiple_of(absolute(place, spot) * blk, blk), blk)
+            grad_input[here, there] = total[:, spot * blk:(spot + 1) * blk]
+        gain_rows[0:1, :] += jnp.sum(grad * scaled, axis=0, keepdims=True)
+        return carry
+
+    lax.fori_loop(0, share // 32, norm, 0)
+    for spot in range(8):
+        there = pl.ds(pl.multiple_of(absolute(place, spot) * blk, blk), blk)
+        gains[:, there] = gain_rows[:, spot * blk:(spot + 1) * blk]
+    gain_masks = (1, 2, CORE, SIDE, DEEP)
+    gain_state = {"item": None, "at": 0}
+
+    def gain_hop():
+        if gain_state["item"] is not None:
+            item = gain_state["item"]
+            copies.got(item)
+            item["copy"].wait_send()
+            item["sent"] = True
+            gains[...] = gains[...] + gains_got[gain_state["at"] - 1]
+            gain_state["item"] = None
+        if gain_state["at"] < len(gain_masks):
+            gain_state["item"] = copies.swap(gains, gains_got.at[gain_state["at"]], gain_masks[gain_state["at"]])
+            gain_state["at"] += 1
+
+    def deep_sum(i):
+        sent = []
+        for x in (0, 1):
+            copies.got(deep_in[i][x])
+            there = pl.ds(x * blk, blk)
+            add_into(keep_f.at[i, :, there], (half, half), deep_f.at[i - 1, give_rows, there], step=16)
+            sent.append(copies.swap(keep_f.at[i, give_rows, there], high_f.at[i, :, there], Z_HIGH))
+        for x in (0, 1):
+            there = pl.ds(x * blk, blk)
+            add_into(keep_f.at[i, :, there], (0, half), deep_f.at[i - 1, :, there], step=16)
+        high_in.append(sent)
+
+    def high_sum(i):
+        for x in (0, 1):
+            copies.got(high_in[i][x])
+            add_into(keep_f.at[i, :, pl.ds(x * blk, blk)], (0, half), high_f.at[i, :, pl.ds(x * blk, blk)], step=16)
+        there = pl.ds(pl.multiple_of((1 - side) * blk, blk), blk)
+        return copies.swap(keep_f.at[i, pl.ds(0, half), there], side_f.at[i], SIDE)
+
+    gain_hop()
+    load_f[0].wait()
+    deep_sum(1)
+    gain_hop()
+    side_in = [high_sum(0)]
+    gain_hop()
+    deep_in_q = None
+    for y in (1, 0):
+        copies.got(side_in_q[y])
+        spot = 2 * y + side
+        rows = pl.ds(pl.multiple_of(spot * blk, blk), blk)
+        own_q[rows, :] = (own_q[rows, :].astype(f32) + side_q[y].astype(f32)).astype(bf16)
+        if y:
+            deep_in_q = copies.swap(own_q.at[rows, :], deep_q, DEEP)
+    gain_hop()
+    load_f[1].wait()
+    deep_sum(2)
+    gain_hop()
+    deep_in_o = None
+    for y in (1, 0):
+        copies.got(side_in_o[y])
+        there = pl.ds(pl.multiple_of((2 * y + side) * blk, blk), blk)
+        add_into(own_o.at[:, there], (0, width), side_o.at[y])
+        if y:
+            deep_in_o = copies.swap(own_o.at[:, there], deep_o, DEEP)
+    gain_hop()
+    reduce.arrived()
+
+    def finish_output(i, carry):
+        here = pl.ds(i * 32, 32)
+        total = (residual[here, :] + parts[here, :].astype(f32) + landed[0, here, :].astype(f32)
+                 + landed[1, here, :].astype(f32)).astype(bf16)
+        for spot in range(8):
+            there = pl.ds(pl.multiple_of(absolute(place, spot) * blk, blk), blk)
+            output[here, there] = total[:, spot * blk:(spot + 1) * blk]
+        return carry
+
+    lax.fori_loop(0, share // 32, finish_output, 0)
+    mine = pl.ds(pl.multiple_of(side * blk, blk), blk)
+    copies.got(deep_in_o)
+    add_into(own_o.at[:, mine], (0, width), deep_o)
+    z_in = []
+    for n, mask in enumerate((2, 3, 1)):
+        other = place.partner(mask)[1]
+        z_in.append(copies.swap(own_o.at[pl.ds(other * zrow, zrow), mine], z_o.at[n], mask))
+    copies.got(deep_in_q)
+    query[...] = own_q[pl.ds(pl.multiple_of(side * blk, blk), blk), :].astype(f32) + deep_q[...].astype(f32)
+    side_in.append(high_sum(1))
+    side_in.append(high_sum(2))
+    for item in z_in:
+        copies.got(item)
+
+    def add_z(i, carry):
+        here = pl.ds(i * 32, 32)
+        sum_ = own_o[pl.ds(mp * zrow + i * 32, 32), mine].astype(f32)
+        for n in range(3):
+            sum_ = sum_ + z_o[n, here, :].astype(f32)
+        out[here, :] = sum_
+        return carry
+
+    lax.fori_loop(0, zrow // 32, add_z, 0)
+    for i, target in enumerate((down, gate, up)):
+        copies.got(side_in[i])
+
+        def write(n, carry, i=i, target=target):
+            target[pl.ds(side * half + n * 16, 16), :] = keep_f[i, pl.ds(n * 16, 16), mine].astype(f32)
+            target[pl.ds((1 - side) * half + n * 16, 16), :] = side_f[i, pl.ds(n * 16, 16), :].astype(f32)
+            return carry
+
+        lax.fori_loop(0, half // 16, write, 0)
+    copies.finish()
+
+
+def back_last(grad_q, rows_first, dres, inputs, gain, query_y, query_0, query_x,
+              sums, down_sums, out_sums, fparts, residual, gain_part, ident):
+    share, width = dres.shape
+    hidden = sums.shape[1]
+    blk = width // 8
+    half = hidden // 2
+    local = grad_q.shape[1]
+    V = pltpu.VMEM
+    S = jax.ShapeDtypeStruct
+    return pl.pallas_call(
+        back_last_kernel,
+        out_shape=(S((hidden, blk), f32),) * 3
+        + (S((width // 4, blk), f32), S((blk, local), f32), S((share, width), f32), S((share, width), bf16),
+           S((2, width), f32), S((width, width), bf16)),
+        in_specs=[VM, ANY] + [VM] * 6 + [ANY] * 4 + [VM] * 2,
+        out_specs=(VM,) * 8 + (ANY,),
+        scratch_shapes=[
+            V((3, hidden, 2 * blk), bf16), V((2, hidden, 2 * blk), bf16), V((3, half, 2 * blk), bf16),
+            V((3, half, blk), bf16),
+            V((width, width // 2), bf16), V((2, width, blk), bf16), V((width, blk), bf16),
+            V((3, width // 4, blk), bf16),
+            V((width // 2, local), bf16), V((width // 2, local), bf16), V((width // 2, local), bf16),
+            V((2, blk, local), bf16), V((blk, local), bf16),
+            V((share * 4, width), bf16), V((2, share // 2, width), bf16), V((2, share, width), bf16),
+            V((share, width), bf16), V((width, width), bf16), V((share, width), f32),
+            V((2, width), f32), V((5, 2, width), f32),
+            DMA((48,)), DMA((48,)), DMA((12,))],
+        compiler_params=params(ident, 63 << 20), name="back_last",
+    )(grad_q, rows_first, dres, inputs, gain, query_y, query_0, query_x,
+      sums, down_sums, out_sums, fparts, residual, gain_part)
+
+
 class Grid:
     def __init__(self, dp):
         self.dp = dp
@@ -1099,7 +1455,8 @@
     grid = Grid(8)
     share = inputs.shape[0]
     hidden_half = w_down.shape[0] // 2
-    tokens = grid.spread(inputs).astype(f32)
+    inputs_here = grid.spread(inputs)
+    tokens = inputs_here.astype(f32)
     gain_one = grid.spread(gain_first)
     gain_two = grid.spread(gain_second)
     cot_here = grid.spread(cotangent)
@@ -1122,68 +1479,16 @@
     normed_second = (scaled_second * gain_two).astype(bf16)
     grad_normed_second, ffn_parts, ffn_sums = ffn_call(normed_second, cots, down_here, gate_here, up_here, 3)
 
-    def quad_sum(parts):
-        own, side_part, low_part, across = (parts[i * share:(i + 1) * share] for i in range(4))
-        relayed = grid.quad_start(across)
-        return grid.quad_finish(relayed, side_part.astype(f32), low_part.astype(f32), own.astype(f32))
-
-    ffn_sum = quad_sum(ffn_parts)
-    output = grid.restore((residual + ffn_sum).astype(bf16))
-
-    def halves_sum(keep, give, mask):
-        return keep.astype(f32) + grid.swap(give.astype(bf16), mask).astype(f32)
-
-    def ffn_grad(total):
-        for mask in grid.rest:
-            half = total.shape[1] // 2
-            total = halves_sum(total[:, :half], total[:, half:], mask)
-        total = halves_sum(total[:hidden_half], total[hidden_half:], Z_HIGH)
-        width = total.shape[1] // 2
-        side = grid.bit(SIDE)
-        keep = lax.dynamic_slice_in_dim(total, side * width, width, 1)
-        give = lax.dynamic_slice_in_dim(total, (1 - side) * width, width, 1)
-        theirs = grid.swap(give.astype(bf16), SIDE).astype(f32)
-        return grid.ordered(keep, theirs, SIDE, 0)
-
-    down_shard = ffn_grad(ffn_sums[0])
-    gate_shard = ffn_grad(ffn_sums[1]).T
-    up_shard = ffn_grad(ffn_sums[2]).T
-
-    grad_from_norm, gain_second_part = norm_back(
-        grad_normed_second, scaled_second, inverse_second, gain_two
-    )
-    grad_residual = cot_here.astype(f32) + grad_from_norm
-    grad_low = grad_residual.astype(bf16)
-    grad_context, query_x = to_heads(contract(grad_low, out_whole, 1, 1).astype(bf16), query_0, 5)
-
-    def rows_reduce(total):
-        for mask in [CORE] + grid.rest:
-            half = total.shape[0] // 2
-            total = halves_sum(total[:half], total[half:], mask)
-        width = total.shape[0] // 2
-        side = grid.bit(SIDE)
-        keep = lax.dynamic_slice_in_dim(total, side * width, width, 0)
-        give = lax.dynamic_slice_in_dim(total, (1 - side) * width, width, 0)
-        return halves_sum(keep, give, SIDE)
-
-    grad_out_t = rows_reduce(contract(grad_low, context_own, 0, 0))
-    pieces = grid.exchange_mp(grad_out_t.astype(bf16), 1, 0).astype(f32)
-    out_shard = jnp.sum(pieces.reshape(4, -1, pieces.shape[1]), axis=0).T
-
+    grad_residual, grad_context, gain_second_part, query_x, down_sums, out_sums = back_first(
+        grad_normed_second, residual, cot_here, gain_two[None], context_own, out_whole, ffn_sums, query_0, 5)
     grad_queries, grad_keys, grad_values = attend_back(
         starts, queries, keys, values, grad_context, log_totals)
     grad_kv = jnp.stack([grad_keys, grad_values], axis=1)
-    query_shard = rows_reduce(contract(rows_first, grad_queries, 0, 0))
-    grad_queries_own, query_whole = to_tokens_last(grad_queries, query_y, query_0, query_x, 6)
-    grad_normed_first = contract(grad_queries_own, query_whole, 1, 1)
-    grad_from_first, gain_first_part = norm_back(
-        grad_normed_first, scaled_first, inverse_first, gain_one
-    )
-    grad_input = grid.restore(grad_residual + grad_from_first)
-    gains = jnp.stack([grid.restore(gain_first_part), grid.restore(gain_second_part)]).reshape(-1, 256)
-    gain_sums = all_sum(gains, 7).reshape(2, -1)
-    return (output, grad_input, grad_kv, gain_sums[0], gain_sums[1], query_shard, out_shard,
-            gate_shard, up_shard, down_shard)
+    down_shard, gate_shard, up_shard, out_shard, query_shard, grad_input, output, gains, _ = back_last(
+        grad_queries, rows_first, grad_residual, inputs_here, gain_one[None], query_y, query_0, query_x,
+        ffn_sums, down_sums, out_sums, ffn_parts, residual, gain_second_part, 6)
+    return (output, grad_input, grad_kv, gains[0], gains[1], query_shard, out_shard,
+            gate_shard.T, up_shard.T, down_shard)
 
 
 def solution(mesh):

time: 745 us -> 636 us (0.85)
  Pallas kernels: 449 us -> 564 us
  waiting for transfers between devices: 109 us -> 0 us
  other arithmetic: 42.1 us -> 6.57 us
  local copies, waits for them, and re-layouts: 76.8 us -> 51.2 us
  starting transfers between devices: 24.9 us -> 0 us
  matrix products: 32.3 us -> 11.2 us
    pallas_call x3 -> x2, Pallas kernels: 101 us -> 216 us  [the longest x1 175 us: back_last(): pl.pallas_call(back_last_kernel, out_shape=(S((hidden, blk), f32),) * 3 +...]
    ppermute x19 -> x0, waiting for transfers between devices: 107 us -> none  [swap(): lax.ppermute(value, ('dp', 'mp'), [(i, i ^ mask) for i in range(self.size)])]
    add x13 -> x0, other arithmetic: 25.3 us -> none  [the longest x11 22.2 us: halves_sum(): return keep.astype(f32) + grid.swap(give.astype(bf16), mask).astype(f32)]
    ppermute x19 -> x0, starting transfers between devices: 21.4 us -> none  [swap(): lax.ppermute(value, ('dp', 'mp'), [(i, i ^ mask) for i in range(self.size)])]
    dot_general x6 -> x2, matrix products: 32.3 us -> 11.2 us  [contract(): lax.dot_general(left, right, (((left_dim,), (right_dim,)), ((), ())), pre...]
    squeeze x1 -> x0, local copies, waits for them, and re-layouts: 15.4 us -> none  [fast_body(): down_shard = ffn_grad(ffn_sums[0])]
    slice x11 -> x1, local copies, waits for them, and re-layouts: 13.6 us -> 0.62 us  [fast_body(): gains[1]]
    unnamed x168 -> x92, local copies, waits for them, and re-layouts: 38.9 us -> 44.1 us
  transfers between devices with their start and end apart: 20 -> 0, of which waited for: 10 -> 0; matrix products, arithmetic and copies ran while one was open for 12% -> 0% of each run, Pallas kernels for 15% -> 0%
where the time goes in v3:
time: 636 us; the launch traced here: 634 us
  Pallas kernels  564 us (89%)
  local copies, waits for them, and re-layouts  51.2 us (8%)
  matrix products  11.2 us (2%)
  other arithmetic  6.57 us (1%)
    pallas_call x1, Pallas kernels, gather_call(): pl.pallas_call(gather_kernel, out_shape=tuple((jax.ShapeDtypeStruct(s, bf...  201 us
    pallas_call x1, Pallas kernels, back_last(): pl.pallas_call(back_last_kernel, out_shape=(S((hidden, blk), f32),) * 3 +...  175 us
    pallas_call x1, Pallas kernels, ffn_call(): pl.pallas_call(ffn_kernel, out_shape=(jax.ShapeDtypeStruct((share, width)...  99.4 us
    unnamed x92, local copies, waits for them, and re-layouts  44.1 us
    pallas_call x1, Pallas kernels, back_first(): pl.pallas_call(back_first_kernel, out_shape=(S((share, width), f32), S((s...  40.7 us
    pallas_call x1, Pallas kernels, to_tokens(): pl.pallas_call(tokens_hop_kernel, out_shape=(jax.ShapeDtypeStruct(shape,...  26.3 us
    pallas_call x1, Pallas kernels, attend_back(): pl.pallas_call(backward_kernel, grid=(heads,), in_specs=[row, head, head,...  13.2 us

profile of v3, /device:TPU:0, one launch (start us, length us, event | category | flops | bytes accessed | tf_op | source)
XLA Modules:
  0.0 634.4 jit_solution(8604046494767947420)
XLA Ops:
  0.7 2.0 convert_reduce_fusion
  14.2 1.0 dynamic-slice_dynamic-update-slice_fusion.7
  15.2 0.9 dynamic-slice_dynamic-update-slice_fusion.6
  16.1 0.9 dynamic-slice_dynamic-update-slice_fusion.14
  17.0 0.9 dynamic-slice_dynamic-update-slice_fusion.13
  18.0 0.9 dynamic-slice_dynamic-update-slice_fusion.5
  21.7 1.6 copy-done.16
  23.2 3.0 fusion.8
  26.3 1.9 copy_bitcast_fusion
  28.2 200.6 %gather_all.1 = (bf16[1024,2048]{1,0:T(8,128)(2,1)S(1)}, bf16[1024,2048]{1,0:T(8,128)(2,1)S(1)}, bf16[2048,512]{1,0:T(8,128)(2,1)S(1)}, bf16[256,2048]{1,0:T(8,1...) custom-call(bf16[256,2048]{1,0:T(8,128)(2,1)S(1)} %fusion.7.first, ...), custom_call_target="tpu_custom_call" | custom-call | tf_op jit(solution)/shard_map/gather_all/pallas_call | solution.py:283
  228.8 2.5 copy-done.11
  231.3 2.4 copy-done.12
  233.7 2.5 copy-done.13
  236.2 2.0 copy-done.14
  238.2 2.1 copy-done.2
  240.2 3.3 convolution_convert_fusion.q_ref
  243.5 8.8 %attend.1 = (bf16[1024,512]{1,0:T(8,128)(2,1)}, f32[4,1,1024]{2,1,0:T(1,128)}) custom-call(s32[1,1024]{1,0:T(1,128)} %bitcast.31, bf16[1024,512]{1,0:T(8,128)(2,1)} %convolution_convert_fusion.q_ref, bf16[1024,512]{1,0:T(8,128)(2,1)} %get-tuple-element.106.k_ref, bf16[1024,512]{1,0:T(8,128)(2,1)} %get-tuple-element.105.v_ref), custom_call_target="tpu_custom_call" | custom-call | flops 1610612736 | bytes 4194304 | tf_op jit(solution)/shard_map/attend/pallas_call | solution.py:594
  252.4 1.2 copy-done.5
  253.6 26.3 %to_tokens.1 = (bf16[256,2048]{1,0:T(8,128)(2,1)S(1)}, bf16[256,2048]{1,0:T(8,128)(2,1)S(1)}) custom-call(bf16[1024,512]{1,0:T(8,128)(2,1)S(1)} %copy-done.5, bf16[256,2048]{1,0:T(8,128)(2,1)S(1)} %get-tuple-element.45.block.query_0), custom_call_target="tpu_custom_call" | custom-call | tf_op jit(solution)/shard_map/to_tokens/pallas_call | solution.py:366
  280.0 7.9 %convert_add_fusion = (f32[256,2048]{1,0:T(8,128)}, f32[256]{0:T(256)S(1)}, f32[256,2048]{1,0:T(8,128)S(1)}) fusion(bf16[256,2048]{1,0:T(8,128)(2,1)S(1)} %dynamic-slice_dynamic-update-slice_fusion.8.inputs, bf16[256,2048]{1,0:T(8,128)(2,1)S(1)} %get-tuple-element.46.context, bf16[2048,2048]{1,0:T(8,128)(2,1)} %get-tuple-element.47.out_whole), kind=kOutput, calls=%fused_computation.2 | convolution fusion | flops 2149580544 | bytes 14681088 | tf_op jit(solution)/shard_map/dot_general | solution.py:1239
  287.9 1.3 fusion.4.normed
  289.2 99.4 %feed_forward.1 = (f32[256,2048]{1,0:T(8,128)}, bf16[1024,2048]{1,0:T(8,128)(2,1)}, bf16[3,1376,1024]{2,1,0:T(8,128)(2,1)}) custom-call(bf16[256,2048]{1,0:T(8,128)(2,1)} %fusion.4.normed, bf16[1024,2048]{1,0:T(8,128)(2,1)} %copy-done.14, bf16[1376,2048]{1,0:T(8,128)(2,1)} %copy-done.13, bf16[1376,2048]{1,0:T(8,128)(2,1)} %copy-done.11, ...), custom_call_target="tpu_custom_call" | custom-call | flops 51942260736 | bytes 41943040 | tf_op jit(solution)/shard_map/feed_forward/pallas_call | solution.py:768
  388.6 40.7 %back_first.1 = (f32[256,2048]{1,0:T(8,128)}, bf16[1024,512]{1,0:T(8,128)(2,1)}, f32[1,2048]{1,0:T(1,128)}, bf16[256,2048]{1,0:T(8,128)(2,1)}, bf16[1376,512]{1,0:T(8,128)(2,1)}, /*index=5*/bf16[2048,1024]{1,0:T(8,128)(2,1)}) custom-call(f32[256,2048]{1,0:T(8,128)} %get-tuple-element.52.dn2, f32[256,2048]{1,0:T(8,128)} %get-tuple-element.94.residual, ...), custom_call_target="tpu_custom_call" | custom-call | tf_op jit(solution)/shard_map/back_first/pallas_call | solution.py:881
  429.3 13.2 %attend_back.1 = (bf16[1024,512]{1,0:T(8,128)(2,1)}, f32[1024,512]{1,0:T(8,128)}, f32[1024,512]{1,0:T(8,128)}) custom-call(s32[1,1024]{1,0:T(1,128)} %bitcast.32, bf16[1024,512]{1,0:T(8,128)(2,1)} %convolution_convert_fusion.q_ref, bf16[1024,512]{1,0:T(8,128)(2,1)} %get-tuple-element.106.k_ref, bf16[1024,512]{1,0:T(8,128)(2,1)} %get-tuple-element.105.v_ref, ...), custom_call_target="tpu_custom_call" | custom-call | flops 3758096384 | bytes 9437184 | tf_op jit(solution)/shard_map/attend_back/pallas_call | solution.py:609
  442.5 175.4 %back_last.1 = (f32[1376,256]{1,0:T(8,128)}, f32[1376,256]{1,0:T(8,128)}, f32[1376,256]{1,0:T(8,128)}, f32[512,256]{1,0:T(8,128)}, f32[256,512]{1,0:T(8,128)}, /...) custom-call(bf16[1024,512]{1,0:T(8,128)(2,1)} %get-tuple-element.56.grad_q, ...), custom_call_target="tpu_custom_call" | custom-call | tf_op jit(solution)/shard_map/back_last/pallas_call | solution.py:1118
  617.9 2.7 pad_maximum_fusion
  620.6 5.2 copy.26
  626.4 1.0 copy.68
  627.4 1.3 copy.69
  630.4 1.1 copy.72
  631.5 1.1 copy.73
  633.4 1.1 copy.74
  (85 shorter events, 17.3 us)
Async XLA Ops:
  0.6 20.1 %copy-start.22 = (bf16[256,2048]{1,0:T(8,128)(2,1)S(1)}, bf16[256,2048]{1,0:T(8,128)(2,1)}, u32[]{:S(2)}) copy-start(bf16[256,2048]{1,0:T(8,128)(2,1)} %param.21) | copy-start | bytes 3145732
  0.7 20.1 %copy-start.21 = (bf16[256,2048]{1,0:T(8,128)(2,1)S(1)}, bf16[256,2048]{1,0:T(8,128)(2,1)}, u32[]{:S(2)}) copy-start(bf16[256,2048]{1,0:T(8,128)(2,1)} %param.11) | copy-start | bytes 3145732
  8.8 12.5 %copy-start.26 = (f32[2048]{0:T(1024)}, f32[2048]{0:T(1024)S(1)}, u32[]{:S(2)}) copy-start(f32[2048]{0:T(1024)S(1)} %constant_dynamic-update-slice_fusion.2) | copy-start | bytes 24580
  14.2 273.6 %copy-start.27 = (f32[2048]{0:T(1024)}, f32[2048]{0:T(1024)S(1)}, u32[]{:S(2)}) copy-start(f32[2048]{0:T(1024)S(1)} %constant_dynamic-update-slice_fusion.3) | copy-start | bytes 24580
  20.9 2.4 copy-start.16
  21.0 266.8 %copy-start.15 = (bf16[256,2048]{1,0:T(8,128)(2,1)}, bf16[256,2048]{1,0:T(8,128)(2,1)S(1)}, u32[]{:S(2)}) copy-start(bf16[256,2048]{1,0:T(8,128)(2,1)S(1)} %dynamic-slice_dynamic-update-slice_fusion.8.inputs) | copy-start | bytes 3145732
  21.1 7.1 %copy-start.1 = (bf16[256,2048]{1,0:T(8,128)(2,1)}, bf16[256,2048]{1,0:T(8,128)(2,1)S(1)}, u32[]{:S(2)}) copy-start(bf16[256,2048]{1,0:T(8,128)(2,1)S(1)} %dynamic-slice_dynamic-update-slice_fusion.cot) | copy-start | bytes 3145732
  26.2 2.0 copy-start.6
  26.2 2.0 copy-start.7
  26.2 2.0 copy-start.8
  26.2 2.0 copy-start.9
  26.3 2.0 copy-start.10
  228.8 2.5 copy-start.11
  231.3 2.4 copy-start.12
  233.7 2.5 copy-start.13
  236.2 2.0 copy-start.14
  238.2 2.1 copy-start.2
  238.2 14.2 %copy-start = (bf16[256,2048]{1,0:T(8,128)(2,1)}, bf16[256,2048]{1,0:T(8,128)(2,1)S(1)}, u32[]{:S(2)}) copy-start(bf16[256,2048]{1,0:T(8,128)(2,1)S(1)} %get-tuple-element.45.block.query_0) | copy-start | bytes 3145732
  252.4 1.2 copy-start.5
  279.9 7.9 %copy-start.3 = (bf16[256,2048]{1,0:T(8,128)(2,1)}, bf16[256,2048]{1,0:T(8,128)(2,1)S(1)}, u32[]{:S(2)}) copy-start(bf16[256,2048]{1,0:T(8,128)(2,1)S(1)} %get-tuple-element.58.query_y) | copy-start | bytes 3145732
  279.9 7.9 %copy-start.4 = (bf16[256,2048]{1,0:T(8,128)(2,1)}, bf16[256,2048]{1,0:T(8,128)(2,1)S(1)}, u32[]{:S(2)}) copy-start(bf16[256,2048]{1,0:T(8,128)(2,1)S(1)} %get-tuple-element.46.context) | copy-start | bytes 3145732
  620.6 5.3 copy-start.28
  620.6 5.9 copy-start.23
  625.8 1.6 copy-start.17
  627.4 1.4 copy-start.25
  627.4 2.2 copy-start.24
  628.8 1.6 copy-start.20
  629.6 1.9 copy-start.19
  631.5 1.9 copy-start.18

commit v4 on v3

--- a/solution.py
+++ b/solution.py
@@ -69,22 +69,45 @@
             else:
                 item["copy"].wait_recv()
 
-    def step(self, block, mp_send, mp_get, direction, send_if, get_if):
+    def prepare(self, source, target, mask):
+        slot = self.count
+        self.count += 1
+        item = {"copy": self.describe(source, target, self.place.partner(mask), slot), "got": False}
+        self.pending.append(item)
+        return item
+
+    def prepare_step(self, block, mp_send, mp_get, direction, send_if, get_if):
         slot = self.count
         self.count += 1
         place = self.place
-        other = jnp.clip(place.mp + direction, 0, 3)
-        sent, target = block(mp_send)
-        copy = self.describe(sent, target, (place.dp, other), slot)
-
-        @pl.when(send_if)
-        def _():
-            copy.start()
-        sent2, target2 = block(mp_get)
-        get = self.describe(sent2, target2, (place.dp, other), slot)
+        device = (place.dp, jnp.clip(place.mp + direction, 0, 3))
+        copy = self.describe(*block(jnp.clip(mp_send, 0, 3)), device, slot)
+        get = self.describe(*block(jnp.clip(mp_get, 0, 3)), device, slot)
         item = {"copy": copy, "got": False, "send_if": send_if, "get_if": get_if, "get": get}
         self.pending.append(item)
         return item
+
+    def start(self, item):
+        if "send_if" in item:
+            @pl.when(item["send_if"])
+            def _():
+                item["copy"].start()
+        else:
+            item["copy"].start()
+
+    def step(self, *arguments):
+        item = self.prepare_step(*arguments)
+        self.start(item)
+        return item
+
+    def received(self, item):
+        item["got"] = True
+        if "get_if" in item:
+            @pl.when(item["get_if"])
+            def _():
+                item["get"].wait_recv()
+        else:
+            item["copy"].wait_recv()
 
     def local(self, source, target):
         copy = pltpu.make_async_copy(source, target, self.local_sems.at[self.local_count])
@@ -111,185 +134,9 @@
     pl.semaphore_wait(barrier, len(masks))
 
 
-def gather_kernel(first, cot, wq, wo, wg, wu, wd, rows, cots, query, wide, out, gate, up, down,
-                  send_sems, recv_sems, local_sems):
-    place = Place()
-    dp, mp = place.dp, place.mp
-    side = place.bit(SIDE)
-    locals_ = []
-    copies = Copies(place, send_sems, recv_sems, local_sems)
-    half = wd.shape[0] // 2
-    blk = wd.shape[1]
-    share = first.shape[0]
-    zrow = wo.shape[0]
-    zcol = wq.shape[1]
-    nchunk = 2
-    chunk = share // nchunk
-    mats = ((wg, gate), (wu, up), (wd, down))
-    own, across = side, 1 - side
-    DEEPER, OTHER = 2, 4
-    greet(place, (1, 2, 3, CORE, SIDE, DEEP))
-
-    def tile(whole, z, spot):
-        return whole.at[pl.ds(z * half, half), pl.ds(spot * blk, blk)]
-
-    def qrows(spot):
-        return query.at[pl.ds(spot * blk, blk), :]
-
-    def columns(spot):
-        return out.at[:, pl.ds(spot * blk, blk)]
-
-    def row_block(c, source_is_input):
-        def get(m):
-            target = rows.at[pl.ds(m * share + c * chunk, chunk), :]
-            source = first.at[pl.ds(c * chunk, chunk), :] if source_is_input else target
-            return source, target
-        return get
-
-    def out_block(source_is_input):
-        def get(m):
-            target = out.at[pl.ds(m * zrow, zrow), pl.ds(own * blk, blk)]
-            return (wo if source_is_input else target), target
-        return get
-
-    def wide_block(source_is_input):
-        def get(m):
-            target = wide.at[:, pl.ds(m * zcol, zcol)]
-            return (wq if source_is_input else target), target
-        return get
-
-    store = {}
-
-    def line(step, block_of, key):
-        store[("r", key, step)] = copies.step(block_of, mp - (step - 1), mp - step, 1,
-                                              (mp >= step - 1) & (mp < 3), mp >= step)
-        store[("l", key, step)] = copies.step(block_of, mp + (step - 1), mp + step, -1,
-                                              (mp <= 3 - (step - 1)) & (mp > 0), mp <= 3 - step)
-
-    def arrive(key, step):
-        copies.got(store[("r", key, step)])
-        copies.got(store[("l", key, step)])
-
-    own_piece = [weight.at[pl.ds(side * half, half), :] for weight, _ in mats]
-    zhop = [[], [], []]
-    yhop = [[], [], []]
-    core = []
-
-    def send_z(i, source, spot):
-        zhop[i].append(copies.swap(source, tile(mats[i][1], 1, spot), Z_HIGH))
-
-    def send_y(i, source, z, spot):
-        yhop[i].append((copies.swap(source, tile(mats[i][1], z, spot + DEEPER), DEEP), z, spot + DEEPER))
-
-    def core_tile(i, z, spot, source=None):
-        piece = tile(mats[i][1], z, spot)
-        core.append(copies.swap(piece if source is None else source, tile(mats[i][1], z, spot + OTHER), CORE))
-
-    def core_query(spot, source=None):
-        core.append(copies.swap(qrows(spot) if source is None else source, qrows(spot + OTHER), CORE))
-
-    def core_out(spot):
-        core.append(copies.swap(columns(spot), columns(spot + OTHER), CORE))
-
-    line(1, out_block(True), "o")
-    send_z(0, own_piece[0], own)
-    xhop = [copies.swap(weight.at[pl.ds((1 - side) * half, half), :], tile(whole, 0, own), SIDE)
-            for weight, whole in mats]
-    wq_y = copies.swap(wq, qrows(own + DEEPER), DEEP)
-    for i in range(3):
-        send_y(i, own_piece[i], 0, own)
-    wq_x = [copies.swap(wq, qrows(own), SIDE)]
-    locals_.append(copies.local(first, rows.at[pl.ds(mp * share, share), :]))
-    locals_.append(copies.local(cot, cots.at[0:share, :]))
-    locals_.append(copies.local(wq, qrows(own)))
-    locals_.append(copies.local(wo, out.at[pl.ds(mp * zrow, zrow), pl.ds(own * blk, blk)]))
-    for i in range(3):
-        locals_.append(copies.local(own_piece[i], tile(mats[i][1], 0, own)))
-    locals_.append(copies.local(wq, wide.at[:, pl.ds(mp * zcol, zcol)]))
-    for i in range(3):
-        core_tile(i, 0, own, own_piece[i])
-    core_query(own, wq)
-    copies.got(wq_y)
-    wq_x.append(copies.swap(qrows(own + DEEPER), qrows(own + DEEPER), SIDE))
-    core_query(own + DEEPER)
-    cot_x = copies.swap(cot, cots.at[share:2 * share, :], SIDE)
-    arrive("o", 1)
-    line(2, out_block(False), "o")
-    send_z(1, own_piece[1], own)
-    arrive("o", 2)
-    line(3, out_block(False), "o")
-    send_z(2, own_piece[2], own)
-    for c in range(nchunk):
-        line(1, row_block(c, True), c)
-    for i in range(3):
-        copies.got(xhop[i])
-        piece = tile(mats[i][1], 0, across)
-        send_y(i, piece, 0, across)
-        send_z(i, piece, across)
-        core_tile(i, 0, across)
-    for item, spot in zip(wq_x, (across, across + DEEPER)):
-        copies.got(item)
-        core_query(spot)
-    arrive("o", 3)
-    for copy in locals_:
-        copy.wait()
-    out_y = copies.swap(columns(own), columns(own + DEEPER), DEEP)
-    out_x = [copies.swap(columns(own), columns(own), SIDE)]
-    core_out(own)
-    for i in range(3):
-        copies.got(zhop[i][0])
-        send_y(i, tile(mats[i][1], 1, own), 1, own)
-        core_tile(i, 1, own)
-    line(1, wide_block(True), "w")
-    for c in range(nchunk):
-        arrive(c, 1)
-        line(2, row_block(c, False), c)
-    copies.got(out_y)
-    out_x.append(copies.swap(columns(own + DEEPER), columns(own + DEEPER), SIDE))
-    core_out(own + DEEPER)
-    cot_z = copies.swap(cot, cots.at[2 * share:3 * share, :], Z_LOW)
-    for i in range(3):
-        copies.got(zhop[i][1])
-        send_y(i, tile(mats[i][1], 1, across), 1, across)
-        core_tile(i, 1, across)
-    arrive("w", 1)
-    line(2, wide_block(False), "w")
-    for c in range(nchunk):
-        arrive(c, 2)
-        line(3, row_block(c, False), c)
-    arrive("w", 2)
-    line(3, wide_block(False), "w")
-    copies.got(out_x[0])
-    core_out(across)
-    copies.got(cot_z)
-    cot_xz = copies.swap(cots.at[2 * share:3 * share, :], cots.at[3 * share:4 * share, :], SIDE)
-    for j in range(4):
-        for i in range(3):
-            item, z, spot = yhop[i][j]
-            copies.got(item)
-            core_tile(i, z, spot)
-    copies.got(out_x[1])
-    core_out(across + DEEPER)
-    copies.finish()
-
-
-def gather_call(first, cot, wq, wo, wg, wu, wd):
-    share, width = first.shape
-    hidden = wd.shape[0]
-    shapes = (
-        (share * 4, width), (share * 4, width), (width, wq.shape[1]), (wq.shape[0], width), (width, width),
-        (hidden, width), (hidden, width), (hidden, width),
-    )
-    return pl.pallas_call(
-        gather_kernel,
-        out_shape=tuple(jax.ShapeDtypeStruct(s, bf16) for s in shapes),
-        in_specs=[VM] * 7,
-        out_specs=(ANY,) * 8,
-        scratch_shapes=[pltpu.SemaphoreType.DMA((110,)), pltpu.SemaphoreType.DMA((110,)),
-                        pltpu.SemaphoreType.DMA((9,))],
-        compiler_params=pltpu.CompilerParams(collective_id=1, has_side_effects=True, vmem_limit_bytes=16 << 20),
-        name="gather_all",
-    )(first, cot, wq, wo, wg, wu, wd)
+def absolute(place, spot):
+    core, deep, side = spot // 4, (spot // 2) % 2, spot % 2
+    return place.flip(place.dp, core + 4 * deep) - 2 * place.bit(SIDE) + 2 * side
 
 
 DMA = pltpu.SemaphoreType.DMA
@@ -302,122 +149,6 @@
 
 def params(ident, vmem=32 << 20):
     return pltpu.CompilerParams(collective_id=ident, has_side_effects=True, vmem_limit_bytes=vmem)
-
-
-def tokens_kernel(heads, query_y, query_0, query_x, own, whole, send_sems, recv_sems, local_sems):
-    place = Place()
-    mp = place.mp
-    side = place.bit(SIDE)
-    share, local = own.shape[0], heads.shape[1]
-    blk = query_0.shape[0]
-    copies = Copies(place, send_sems, recv_sems, local_sems)
-
-    def rows(spot):
-        return whole.at[pl.ds(spot * blk, blk), :]
-
-    greet(place, (1, 2, 3, SIDE, CORE))
-    across = copies.swap(query_y, rows(side + 2), SIDE)
-    for mask in (2, 3, 1):
-        other = place.partner(mask)[1]
-        copies.swap(heads.at[pl.ds(other * share, share), :], own.at[:, pl.ds(mp * local, local)], mask)
-    held = [copies.local(query_0, rows(side)), copies.local(query_y, rows(side + 2)),
-            copies.local(query_x, rows(1 - side))]
-    copies.swap(query_0, rows(side + 4), CORE)
-    copies.swap(query_y, rows(side + 6), CORE)
-    copies.swap(query_x, rows(1 - side + 4), CORE)
-    own[:, pl.ds(mp * local, local)] = heads[pl.ds(mp * share, share), :]
-    for copy in held:
-        copy.wait()
-    copies.got(across)
-    copies.swap(rows(1 - side + 2), rows(1 - side + 6), CORE)
-    copies.finish()
-
-
-def tokens_hop_kernel(heads, block, own, hopped, send_sems, recv_sems):
-    place = Place()
-    mp = place.mp
-    share, local = own.shape[0], heads.shape[1]
-    greet(place, (1, 2, 3, DEEP))
-    copies = Copies(place, send_sems, recv_sems)
-    for mask in (2, 3, 1):
-        other = place.partner(mask)[1]
-        copies.swap(heads.at[pl.ds(other * share, share), :], own.at[:, pl.ds(mp * local, local)], mask)
-    copies.swap(block, hopped, DEEP)
-    own[:, pl.ds(mp * local, local)] = heads[pl.ds(mp * share, share), :]
-    copies.finish()
-
-
-def heads_hop_kernel(own, block, heads, hopped, send_sems, recv_sems):
-    place = Place()
-    mp = place.mp
-    share, local = own.shape[0], heads.shape[1]
-    greet(place, (1, 2, 3, SIDE))
-    copies = Copies(place, send_sems, recv_sems)
-    for mask in (2, 3, 1):
-        other = place.partner(mask)[1]
-        copies.swap(own.at[:, pl.ds(other * local, local)], heads.at[pl.ds(mp * share, share), :], mask)
-    copies.swap(block, hopped, SIDE)
-    heads[pl.ds(mp * share, share), :] = own[:, pl.ds(mp * local, local)]
-    copies.finish()
-
-
-def to_tokens(heads, block, ident):
-    shape = (heads.shape[0] // 4, heads.shape[1] * 4)
-    return pl.pallas_call(
-        tokens_hop_kernel,
-        out_shape=(jax.ShapeDtypeStruct(shape, bf16), jax.ShapeDtypeStruct(block.shape, bf16)),
-        in_specs=[VM, VM], out_specs=(VM, VM),
-        scratch_shapes=[DMA((4,)), DMA((4,))], compiler_params=params(ident), name="to_tokens")(heads, block)
-
-
-def to_tokens_last(heads, query_y, query_0, query_x, ident):
-    shape = (heads.shape[0] // 4, heads.shape[1] * 4)
-    width = query_0.shape[1]
-    return pl.pallas_call(
-        tokens_kernel,
-        out_shape=(jax.ShapeDtypeStruct(shape, bf16), jax.ShapeDtypeStruct((width, width), bf16)),
-        in_specs=[VM] * 4, out_specs=(VM, ANY),
-        scratch_shapes=[DMA((8,)), DMA((8,)), DMA((3,))], compiler_params=params(ident),
-        name="to_tokens_last")(heads, query_y, query_0, query_x)
-
-
-def to_heads(own, block, ident):
-    shape = (own.shape[0] * 4, own.shape[1] // 4)
-    return pl.pallas_call(
-        heads_hop_kernel,
-        out_shape=(jax.ShapeDtypeStruct(shape, bf16), jax.ShapeDtypeStruct(block.shape, bf16)),
-        in_specs=[VM, VM], out_specs=(VM, VM),
-        scratch_shapes=[DMA((4,)), DMA((4,))], compiler_params=params(ident), name="to_heads")(own, block)
-
-
-def quad_gather_kernel(own, rows, send_sems, recv_sems):
-    place = Place()
-    share = own.shape[0]
-    half = share // 2
-    greet(place, (Z_LOW, SIDE))
-    copies = Copies(place, send_sems, recv_sems)
-    a, b = pl.ds(0, half), pl.ds(half, half)
-
-    def at(quarter, part):
-        return rows.at[pl.ds(quarter * share + part * half, half), :]
-
-    low_a = copies.swap(own.at[a, :], at(2, 0), Z_LOW)
-    side_b = copies.swap(own.at[b, :], at(1, 1), SIDE)
-    low_b = copies.swap(own.at[b, :], at(2, 1), Z_LOW)
-    side_a = copies.swap(own.at[a, :], at(1, 0), SIDE)
-    rows[0:share, :] = own[...]
-    copies.got(low_a)
-    copies.swap(at(2, 0), at(3, 0), SIDE)
-    copies.got(side_b)
-    copies.swap(at(1, 1), at(3, 1), Z_LOW)
-    copies.finish()
-
-
-def quad_gather(own, ident):
-    return pl.pallas_call(
-        quad_gather_kernel, out_shape=jax.ShapeDtypeStruct((own.shape[0] * 4, own.shape[1]), bf16),
-        in_specs=[VM], out_specs=VM, scratch_shapes=[DMA((6,)), DMA((6,))],
-        compiler_params=params(ident), name="quad_gather")(own)
 
 
 def add_into(target, rows, *others, step=32):
@@ -461,61 +192,6 @@
             self.copies.got(item)
 
 
-def quad_reduce_kernel(parts_in, total, parts, relay, landed, send_sems, recv_sems, local_sem):
-    place = Place()
-    load = pltpu.make_async_copy(parts_in, parts, local_sem)
-    load.start()
-    greet(place, (Z_LOW, SIDE))
-    copies = Copies(place, send_sems, recv_sems)
-    load.wait()
-    reduce = QuadReduce(copies, parts, relay, landed)
-    reduce.start()
-    reduce.relayed()
-    reduce.arrived()
-    share = total.shape[0]
-
-    def one(i, carry):
-        here = pl.ds(i * 32, 32)
-        total[here, :] = (parts[here, :].astype(f32) + landed[0, here, :].astype(f32)
-                          + landed[1, here, :].astype(f32))
-        return carry
-
-    lax.fori_loop(0, share // 32, one, 0)
-    copies.finish()
-
-
-def quad_reduce(parts, ident):
-    share, width = parts.shape[0] // 4, parts.shape[1]
-    return pl.pallas_call(
-        quad_reduce_kernel, out_shape=jax.ShapeDtypeStruct((share, width), f32),
-        in_specs=[ANY], out_specs=VM,
-        scratch_shapes=[pltpu.VMEM((share * 4, width), bf16), pltpu.VMEM((2, share // 2, width), bf16),
-                        pltpu.VMEM((2, share, width), bf16), DMA((6,)), DMA((6,)), DMA],
-        compiler_params=params(ident), name="quad_reduce")(parts)
-
-
-def all_sum_kernel(value, total, got, send_sems, recv_sems):
-    place = Place()
-    masks = (1, 2, CORE, SIDE, DEEP)
-    greet(place, masks)
-    copies = Copies(place, send_sems, recv_sems)
-    total[...] = value[...]
-    for i, mask in enumerate(masks):
-        item = copies.swap(total, got.at[i], mask)
-        copies.got(item)
-        item["copy"].wait_send()
-        item["sent"] = True
-        total[...] = total[...] + got[i]
-    copies.finish()
-
-
-def all_sum(value, ident):
-    return pl.pallas_call(
-        all_sum_kernel, out_shape=jax.ShapeDtypeStruct(value.shape, f32), in_specs=[VM], out_specs=VM,
-        scratch_shapes=[pltpu.VMEM((5,) + value.shape, f32), DMA((5,)), DMA((5,))],
-        compiler_params=params(ident), name="all_sum")(value)
-
-
 ROWS=256
 DOC_MOST=512
 
@@ -532,21 +208,21 @@
     return jnp.where((key_pos >= starts) & (key_pos <= query_pos), s, -1e30)
 
 
-def forward_kernel(starts_ref, q_ref, k_ref, v_ref, ctx_ref, lse_ref):
+def attend_head(h, starts_ref, q_ref, k_ref, v_ref, ctx_ref, lse_ref):
     seq_len = q_ref.shape[0]
     scale = HEAD_DIM ** -0.5
+    lanes = pl.ds(pl.multiple_of(h * HEAD_DIM, HEAD_DIM), HEAD_DIM)
     for block in range(seq_len // ROWS):
         low, high = key_range(block, seq_len)
         here = pl.ds(block * ROWS, ROWS)
-        k = k_ref[low:high, :]
-        v = v_ref[low:high, :]
-        s = scores_turned(q_ref[here, :], k, starts_ref[:, here], low, block * ROWS, scale)
+        keys_here = pl.ds(low, high - low)
+        s = scores_turned(q_ref[here, lanes], k_ref[keys_here, lanes], starts_ref[:, here], low, block * ROWS, scale)
         top = jnp.max(s, axis=0, keepdims=True)
         raised = jnp.exp(s - top)
         total = jnp.sum(raised, axis=0, keepdims=True)
         low_probs = (raised * (1.0 / total)).astype(bf16)
-        ctx_ref[here, :] = dot(low_probs, v, 0, 0).astype(bf16)
-        lse_ref[0, :, here] = top + jnp.log(total)
+        ctx_ref[here, lanes] = dot(low_probs, v_ref[keys_here, lanes], 0, 0).astype(bf16)
+        lse_ref[h, :, here] = top + jnp.log(total)
 
 
 def backward_kernel(starts_ref, q_ref, k_ref, v_ref, grad_ref, lse_ref, dq_ref, dk_ref, dv_ref):
@@ -586,20 +262,6 @@
     return row, head, lse
 
 
-def attend(starts, q, k, v):
-    seq_len, width = q.shape
-    heads = width // HEAD_DIM
-    row, head, lse = specs(seq_len)
-    flops = heads * seq_len * seq_len * HEAD_DIM * 3
-    return pl.pallas_call(
-        forward_kernel, grid=(heads,),
-        in_specs=[row, head, head, head], out_specs=(head, lse),
-        out_shape=(jax.ShapeDtypeStruct(q.shape, bf16), jax.ShapeDtypeStruct((heads, 1, seq_len), f32)),
-        cost_estimate=pl.CostEstimate(flops=flops, bytes_accessed=4 * q.size * 2, transcendentals=heads * seq_len * seq_len // 2),
-        name="attend",
-    )(starts, q, k, v)
-
-
 def attend_back(starts, q, k, v, grad, lse_array):
     seq_len, width = q.shape
     heads = width // HEAD_DIM
@@ -619,6 +281,252 @@
     return jnp.sum((segments[0][None, :] < segments[0][:, None]).astype(jnp.int32), axis=1)[None, :]
 
 
+def front_kernel(x, cot, gain_one_in, gain_two_in, wq, wo, wg, wu, wd, keys, values, starts,
+                 rows_out, cots, gate, up, down, out_out, queries, context_own, lse, residual, normed,
+                 x_here, cot_here, gain_one, gain_two,
+                 first, rows, query, out, context,
+                 send_sems, recv_sems, local_sems):
+    place = Place()
+    dp, mp = place.dp, place.mp
+    side = place.bit(SIDE)
+    copies = Copies(place, send_sems, recv_sems, local_sems)
+    half = wd.shape[0] // 2
+    blk = wd.shape[1]
+    share, width = first.shape
+    zrow = wo.shape[0]
+    local = wq.shape[1]
+    chunk = share // 2
+    mats = ((wg, gate), (wu, up), (wd, down))
+    own, across = side, 1 - side
+    DEEPER, OTHER = 2, 4
+    locals_ = []
+
+    def tile(whole, z, spot):
+        return whole.at[pl.ds(z * half, half), pl.ds(spot * blk, blk)]
+
+    def qrows(spot):
+        return query.at[pl.ds(spot * blk, blk), :]
+
+    def columns(spot):
+        return out.at[:, pl.ds(spot * blk, blk)]
+
+    def row_block(c, source_is_input):
+        def get(m):
+            target = rows.at[pl.ds(m * share + c * chunk, chunk), :]
+            source = first.at[pl.ds(c * chunk, chunk), :] if source_is_input else target
+            return source, target
+        return get
+
+    def out_block(source_is_input):
+        def get(m):
+            target = out.at[pl.ds(m * zrow, zrow), pl.ds(own * blk, blk)]
+            return (wo if source_is_input else target), target
+        return get
+
+    store = {}
+
+    def line(step, block_of, key):
+        store[("r", key, step)] = copies.step(block_of, mp - (step - 1), mp - step, 1,
+                                              (mp >= step - 1) & (mp < 3), mp >= step)
+        store[("l", key, step)] = copies.step(block_of, mp + (step - 1), mp + step, -1,
+                                              (mp <= 3 - (step - 1)) & (mp > 0), mp <= 3 - step)
+
+    def arrive(key, step):
+        copies.got(store[("r", key, step)])
+        copies.got(store[("l", key, step)])
+
+    own_piece = [weight.at[pl.ds(side * half, half), :] for weight, _ in mats]
+    zhop = [[], [], []]
+    yhop = [[], [], []]
+
+    def send_z(i, source, spot):
+        zhop[i].append(copies.swap(source, tile(mats[i][1], 1, spot), Z_HIGH))
+
+    def send_y(i, source, z, spot):
+        yhop[i].append((copies.swap(source, tile(mats[i][1], z, spot + DEEPER), DEEP), z, spot + DEEPER))
+
+    def core_tile(i, z, spot, source=None):
+        piece = tile(mats[i][1], z, spot)
+        copies.swap(piece if source is None else source, tile(mats[i][1], z, spot + OTHER), CORE)
+
+    def core_query(spot, source=None):
+        return copies.swap(qrows(spot) if source is None else source, qrows(spot + OTHER), CORE)
+
+    def core_out(spot):
+        return copies.swap(columns(spot), columns(spot + OTHER), CORE)
+
+    greet(place, (1, 2, 3, CORE, SIDE, DEEP))
+    line(1, out_block(True), "o")
+    xhop = [copies.swap(weight.at[pl.ds((1 - side) * half, half), :], tile(whole, 0, own), SIDE)
+            for weight, whole in mats]
+    wq_y = copies.swap(wq, qrows(own + DEEPER), DEEP)
+    for i in range(3):
+        send_y(i, own_piece[i], 0, own)
+    wq_x = [copies.swap(wq, qrows(own), SIDE)]
+    wq_core = [core_query(own, wq)]
+    send_z(0, own_piece[0], own)
+
+    spots = [pl.ds(pl.multiple_of(absolute(place, s) * blk, blk), blk) for s in range(8)]
+    for s in range(8):
+        gain_one[:, s * blk:(s + 1) * blk] = gain_one_in[:, spots[s]]
+        gain_two[:, s * blk:(s + 1) * blk] = gain_two_in[:, spots[s]]
+
+    def norm_first(i, carry):
+        here = pl.ds(i * 32, 32)
+        for s in range(8):
+            x_here[here, s * blk:(s + 1) * blk] = x[here, spots[s]]
+            cot_here[here, s * blk:(s + 1) * blk] = cot[here, spots[s]]
+        value = x_here[here, :].astype(f32)
+        inverse = lax.rsqrt(jnp.mean(value * value, axis=-1, keepdims=True) + epsilon)
+        first[here, :] = (value * inverse * gain_one[...]).astype(bf16)
+        return carry
+
+    lax.fori_loop(0, share // 32, norm_first, 0)
+    for c in range(2):
+        line(1, row_block(c, True), c)
+    rows[pl.ds(mp * share, share), :] = first[...]
+    query[pl.ds(own * blk, blk), :] = wq[...]
+    out[pl.ds(mp * zrow, zrow), pl.ds(pl.multiple_of(own * blk, blk), blk)] = wo[...]
+    locals_.append(copies.local(cot_here, cots.at[0:share, :]))
+    for i in range(3):
+        locals_.append(copies.local(own_piece[i], tile(mats[i][1], 0, own)))
+        core_tile(i, 0, own, own_piece[i])
+    copies.got(wq_y)
+    wq_x.append(copies.swap(qrows(own + DEEPER), qrows(own + DEEPER), SIDE))
+    wq_core.append(core_query(own + DEEPER))
+    arrive("o", 1)
+    line(2, out_block(False), "o")
+    send_z(1, own_piece[1], own)
+    send_z(2, own_piece[2], own)
+    for i in range(3):
+        copies.got(xhop[i])
+        piece = tile(mats[i][1], 0, across)
+        send_y(i, piece, 0, across)
+        core_tile(i, 0, across)
+    for item, spot in zip(wq_x, (across, across + DEEPER)):
+        copies.got(item)
+        wq_core.append(core_query(spot))
+    for c in range(2):
+        arrive(c, 1)
+        line(2, row_block(c, False), c)
+    arrive("o", 2)
+    line(3, out_block(False), "o")
+    for i in range(3):
+        send_z(i, tile(mats[i][1], 0, across), across)
+    cot_x = copies.swap(cot_here, cots.at[share:2 * share, :], SIDE)
+    for i in range(2):
+        copies.got(zhop[i][0])
+        send_y(i, tile(mats[i][1], 1, own), 1, own)
+        core_tile(i, 1, own)
+    arrive("o", 3)
+    out_y = copies.swap(columns(own), columns(own + DEEPER), DEEP)
+    out_x = [copies.swap(columns(own), columns(own), SIDE)]
+    out_core = [core_out(own)]
+    for c in range(2):
+        arrive(c, 2)
+        line(3, row_block(c, False), c)
+    copies.got(zhop[2][0])
+    send_y(2, tile(mats[2][1], 1, own), 1, own)
+    core_tile(2, 1, own)
+    for copy in locals_:
+        copy.wait()
+    cot_z = copies.swap(cot_here, cots.at[2 * share:3 * share, :], Z_LOW)
+    for item in wq_core:
+        copies.got(item)
+    copies.got(out_y)
+    out_x.append(copies.swap(columns(own + DEEPER), columns(own + DEEPER), SIDE))
+    out_core.append(core_out(own + DEEPER))
+    for c in range(2):
+        arrive(c, 3)
+    save_rows = copies.local(rows, rows_out)
+
+    def project(m, carry):
+        here = pl.ds(pl.multiple_of(m * share, share), share)
+        queries[here, :] = dot(rows[here, :], query[...], 1, 0).astype(bf16)
+        return carry
+
+    lax.fori_loop(0, 4, project, 0)
+
+    def one_head(h, carry):
+        attend_head(h, starts, queries, keys, values, context, lse)
+        return carry
+
+    lax.fori_loop(0, local // HEAD_DIM, one_head, 0)
+    tokens_in = []
+    for mask in (2, 3, 1):
+        other = place.partner(mask)[1]
+        tokens_in.append(copies.swap(context.at[pl.ds(other * share, share), :],
+                                     context_own.at[:, pl.ds(mp * local, local)], mask))
+    context_own[:, pl.ds(pl.multiple_of(mp * local, local), local)] = context[pl.ds(mp * share, share), :]
+    for i in range(3):
+        copies.got(zhop[i][1])
+        send_y(i, tile(mats[i][1], 1, across), 1, across)
+        core_tile(i, 1, across)
+    for j in range(2):
+        for i in range(3):
+            item, z, spot = yhop[i][j]
+            copies.got(item)
+            core_tile(i, z, spot)
+    copies.got(out_x[0])
+    out_core.append(core_out(across))
+    copies.got(cot_z)
+    copies.swap(cots.at[2 * share:3 * share, :], cots.at[3 * share:4 * share, :], SIDE)
+    copies.got(out_x[1])
+    out_core.append(core_out(across + DEEPER))
+    for i in range(3):
+        item, z, spot = yhop[i][2]
+        copies.got(item)
+        core_tile(i, z, spot)
+    for item in out_core + tokens_in:
+        copies.got(item)
+    save_out = copies.local(out, out_out)
+
+    def project_out(n, carry):
+        there = pl.ds(pl.multiple_of(n * 512, 512), 512)
+        residual[:, there] = x_here[:, there].astype(f32) + dot(context_own[...], out[:, there], 1, 0)
+        return carry
+
+    lax.fori_loop(0, width // 512, project_out, 0)
+
+    def norm_second(i, carry):
+        here = pl.ds(i * 32, 32)
+        value = residual[here, :]
+        inverse = lax.rsqrt(jnp.mean(value * value, axis=-1, keepdims=True) + epsilon)
+        normed[here, :] = (value * inverse * gain_two[...]).astype(bf16)
+        return carry
+
+    lax.fori_loop(0, share // 32, norm_second, 0)
+    for i in range(3):
+        item, z, spot = yhop[i][3]
+        copies.got(item)
+        core_tile(i, z, spot)
+    save_rows.wait()
+    save_out.wait()
+    copies.finish()
+
+
+def front_call(x, cot, gain_one, gain_two, wq, wo, wg, wu, wd, keys, values, starts, ident):
+    share, width = x.shape
+    hidden, blk = wd.shape
+    seq_len, local = keys.shape
+    V = pltpu.VMEM
+    S = jax.ShapeDtypeStruct
+    return pl.pallas_call(
+        front_kernel,
+        out_shape=(
+            S((seq_len, width), bf16), S((seq_len, width), bf16), S((hidden, width), bf16), S((hidden, width), bf16),
+            S((hidden, width), bf16), S((width, width), bf16), S((seq_len, local), bf16), S((share, width), bf16),
+            S((local // HEAD_DIM, 1, seq_len), f32), S((share, width), f32), S((share, width), bf16),
+            S((share, width), bf16), S((share, width), bf16), S((1, width), f32), S((1, width), f32)),
+        in_specs=[VM] * 12,
+        out_specs=(ANY,) * 6 + (VM,) * 9,
+        scratch_shapes=[
+            V((share, width), bf16), V((seq_len, width), bf16), V((width, local), bf16), V((width, width), bf16),
+            V((seq_len, local), bf16), DMA((96,)), DMA((96,)), DMA((8,))],
+        compiler_params=params(ident, 60 << 20), name="front",
+    )(x, cot, gain_one, gain_two, wq, wo, wg, wu, wd, keys, values, starts)
+
+
 def hidden_cuts(hidden):
     cuts = []
     start = 0
@@ -629,7 +537,7 @@
     return cuts
 
 
-def ffn_kernel(normed, cots_in, down_in, gate_in, up_in, total, fparts_out, sums_out,
+def ffn_kernel(normed, wq, cots_in, down_in, gate_in, up_in, total, query_0, query_y, fparts_out, sums_out,
                weights, tokens, acts, dparts, relay, landed, fparts,
                send_sems, recv_sems, local_sems, free_sem):
     place = Place()
@@ -641,7 +549,9 @@
     copies = Copies(place, send_sems, recv_sems, local_sems)
     load_cots = copies.local(cots_in, tokens.at[0])
     load_w = [copies.local(w, weights.at[i]) for i, w in enumerate((down_in, gate_in, up_in))]
-    greet(place, (Z_LOW, SIDE, CORE))
+    mp = place.mp
+    local = wq.shape[1]
+    greet(place, (1, 2, 3, SIDE, CORE, DEEP))
 
     def at(quarter, part):
         return tokens.at[1, pl.ds(quarter * share + part * half, half), :]
@@ -652,6 +562,24 @@
     low_b = copies.swap(normed.at[b, :], at(2, 1), Z_LOW)
     side_a = copies.swap(normed.at[a, :], at(1, 0), SIDE)
     tokens[1, 0:share, :] = normed[...]
+
+    def wide_block(source_is_input):
+        def get(m):
+            target = query_0.at[:, pl.ds(pl.multiple_of(m * local, local), local)]
+            return (wq if source_is_input else target), target
+        return get
+
+    hops = []
+    for hop in (1, 2, 3):
+        block_of = wide_block(hop == 1)
+        hops.append((
+            copies.prepare_step(block_of, mp - (hop - 1), mp - hop, 1, (mp >= hop - 1) & (mp < 3), mp >= hop),
+            copies.prepare_step(block_of, mp + (hop - 1), mp + hop, -1,
+                                (mp <= 3 - (hop - 1)) & (mp > 0), mp <= 3 - hop)))
+    over_deep = copies.prepare(query_0, query_y, DEEP)
+    query_0[:, pl.ds(pl.multiple_of(mp * local, local), local)] = wq[...]
+    for item in hops[0]:
+        copies.start(item)
 
     def block(r):
         here = pl.ds(r * share, share)
@@ -688,13 +616,27 @@
             side_b["copy"].wait_recv()
             forward[0].start()
             forward[1].start()
+            for item in hops[0]:
+                copies.received(item)
+            for item in hops[1]:
+                copies.start(item)
             side_a["copy"].wait_recv()
             low_b["copy"].wait_recv()
+
+        @pl.when(r == 2)
+        def _():
+            for item in hops[1]:
+                copies.received(item)
+            for item in hops[2]:
+                copies.start(item)
 
         @pl.when(r == 3)
         def _():
             forward[0].wait_recv()
             forward[1].wait_recv()
+            for item in hops[2]:
+                copies.received(item)
+            copies.start(over_deep)
         block(r)
         return carry
 
@@ -760,31 +702,27 @@
     copies.finish()
 
 
-def ffn_call(normed, cots, down, gate, up, ident):
+def ffn_call(normed, wq, cots, down, gate, up, ident):
     share, width = normed.shape
     hidden = down.shape[0]
     V = pltpu.VMEM
     flops = 2 * share * 4 * width * hidden * 9
     return pl.pallas_call(
         ffn_kernel,
-        out_shape=(jax.ShapeDtypeStruct((share, width), f32), jax.ShapeDtypeStruct((share * 4, width), bf16),
+        out_shape=(jax.ShapeDtypeStruct((share, width), f32), jax.ShapeDtypeStruct((share, width), bf16),
+                   jax.ShapeDtypeStruct((share, width), bf16), jax.ShapeDtypeStruct((share * 4, width), bf16),
                    jax.ShapeDtypeStruct((3, hidden, width // 2), bf16)),
-        in_specs=[VM] + [ANY] * 4,
-        out_specs=(VM, ANY, ANY),
+        in_specs=[VM] * 2 + [ANY] * 4,
+        out_specs=(VM, VM, VM, ANY, ANY),
         scratch_shapes=[
             V((3, hidden, width), bf16), V((2, share * 4, width), bf16), V((3, share * 4, hidden), bf16),
             V((share * 4, width), bf16), V((2, share // 2, width), bf16), V((2, share, width), bf16),
             V((share * 4, width), bf16),
-            DMA((16,)), DMA((16,)), DMA((8,)), pltpu.SemaphoreType.REGULAR],
+            DMA((24,)), DMA((24,)), DMA((8,)), pltpu.SemaphoreType.REGULAR],
         compiler_params=params(ident, 63 << 20),
         cost_estimate=pl.CostEstimate(flops=flops, bytes_accessed=40 << 20, transcendentals=share * 4 * hidden),
         name="feed_forward",
-    )(normed, cots, down, gate, up)
-
-
-def absolute(place, spot):
-    core, deep, side = spot // 4, (spot // 2) % 2, spot % 2
-    return place.flip(place.dp, core + 4 * deep) - 2 * place.bit(SIDE) + 2 * side
+    )(normed, wq, cots, down, gate, up)
 
 
 def back_first_kernel(dn2, residual, cot, gain, context, out_whole, sums, query_0,
@@ -1136,103 +1074,6 @@
         compiler_params=params(ident, 63 << 20), name="back_last",
     )(grad_q, rows_first, dres, inputs, gain, query_y, query_0, query_x,
       sums, down_sums, out_sums, fparts, residual, gain_part)
-
-
-class Grid:
-    def __init__(self, dp):
-        self.dp = dp
-        self.size = dp * MP
-        self.rest = []
-        mask = 16
-        while mask < self.size:
-            self.rest.append(mask)
-            mask *= 2
-        self.relative = [CORE] + self.rest
-        self.me = lax.axis_index("dp") * MP + lax.axis_index("mp")
-        self.me_mp = lax.axis_index("mp")
-        self.me_dp = lax.axis_index("dp")
-
-    def swap(self, value, mask):
-        return lax.ppermute(value, ("dp", "mp"), [(i, i ^ mask) for i in range(self.size)])
-
-    def bit(self, mask):
-        return (self.me // mask) % 2
-
-    def spread(self, value):
-        block = value.shape[-1] // self.dp
-        pieces = []
-        for spot in range(self.dp):
-            flips = 0
-            digits = spot >> 1
-            for place, mask in enumerate(reversed(self.relative)):
-                if (digits >> place) & 1:
-                    flips |= mask // MP
-            source = ((self.me_dp ^ flips) & ~(SIDE // MP)) | ((spot & 1) * (SIDE // MP))
-            pieces.append(lax.dynamic_slice_in_dim(value, source * block, block, value.ndim - 1))
-        return jnp.concatenate(pieces, axis=-1)
-
-    def restore(self, value):
-        block = value.shape[-1] // self.dp
-        pieces = []
-        for target in range(self.dp):
-            flips = (self.me_dp ^ target) * MP
-            spot = 0
-            for mask in self.relative:
-                spot = spot * 2 + (flips // mask) % 2
-            spot = spot * 2 + (target * MP // SIDE) % 2
-            pieces.append(lax.dynamic_slice_in_dim(value, spot * block, block, value.ndim - 1))
-        return jnp.concatenate(pieces, axis=-1)
-
-    def ordered(self, mine, theirs, mask, axis):
-        high = self.bit(mask) == 1
-        return jnp.concatenate(
-            [jnp.where(high, theirs, mine), jnp.where(high, mine, theirs)], axis=axis
-        )
-
-    def line_gather(self, value):
-        right, left = {0: value}, {0: value}
-        for step in range(1, MP):
-            right[step] = lax.ppermute(
-                right[step - 1], "mp", [(j, j + 1) for j in range(step - 1, MP - 1)]
-            )
-            left[step] = lax.ppermute(
-                left[step - 1], "mp", [(j, j - 1) for j in range(1, MP - step + 1)]
-            )
-        return [value] + [left[d] + right[MP - d] for d in range(1, MP)]
-
-    def exchange_mp(self, value, split, join):
-        return lax.all_to_all(value, "mp", split, join, tiled=True)
-
-    def quad_gather(self, value):
-        half = value.shape[0] // 2
-        from_side = self.swap(value, SIDE)
-        from_low = self.swap(value, Z_LOW)
-        across = jnp.concatenate(
-            [self.swap(from_low[:half], SIDE), self.swap(from_side[half:], Z_LOW)], axis=0
-        )
-        return [value, from_side, from_low, across]
-
-    def quad_start(self, across):
-        half = across.shape[0] // 2
-        return self.swap(across[:half], SIDE), self.swap(across[half:], Z_LOW)
-
-    def quad_finish(self, relayed, for_side, for_low, own):
-        by_side, by_low = relayed
-        half = own.shape[0] // 2
-        low_sum = jnp.concatenate(
-            [(for_low[:half] + by_side.astype(f32)), for_low[half:]], axis=0
-        ).astype(bf16)
-        side_sum = jnp.concatenate(
-            [for_side[:half], for_side[half:] + by_low.astype(f32)], axis=0
-        ).astype(bf16)
-        return own + self.swap(side_sum, SIDE).astype(f32) + self.swap(low_sum, Z_LOW).astype(f32)
-
-    def all_sum(self, value):
-        mask = 1
-        while mask < self.size:
-            value = value + self.swap(value, mask)
-            mask *= 2
-        return value
 
 
 def contract(left, right, left_dim, right_dim):
@@ -1452,40 +1293,22 @@
 
 def fast_body(inputs, keys_values, segment_ids, gain_first, gain_second, w_query, w_out, w_gate,
               w_up, w_down, cotangent):
-    grid = Grid(8)
-    share = inputs.shape[0]
-    hidden_half = w_down.shape[0] // 2
-    inputs_here = grid.spread(inputs)
-    tokens = inputs_here.astype(f32)
-    gain_one = grid.spread(gain_first)
-    gain_two = grid.spread(gain_second)
-    cot_here = grid.spread(cotangent)
-    inverse_first = root_inverse(tokens)
-    scaled_first = tokens * inverse_first
-    normed_first = (scaled_first * gain_one).astype(bf16)
-
-    rows_first, cots, query_part, query_0, out_whole, gate_here, up_here, down_here = gather_call(
-        normed_first, cot_here, w_query, w_out, w_gate.T, w_up.T, w_down)
-
-    queries = contract(rows_first, query_part, 1, 0).astype(bf16)
     starts = starts_of(segment_ids)
     keys = keys_values[:, 0, :]
     values = keys_values[:, 1, :]
-    context, log_totals = attend(starts, queries, keys, values)
-    context_own, query_y = to_tokens(context, query_0, 2)
-    residual = tokens + contract(context_own, out_whole, 1, 0)
-    inverse_second = root_inverse(residual)
-    scaled_second = residual * inverse_second
-    normed_second = (scaled_second * gain_two).astype(bf16)
-    grad_normed_second, ffn_parts, ffn_sums = ffn_call(normed_second, cots, down_here, gate_here, up_here, 3)
-
+    (rows_first, cots, gate_here, up_here, down_here, out_whole, queries, context_own, log_totals, residual,
+     normed_second, inputs_here, cot_here, gain_one, gain_two) = front_call(
+        inputs, cotangent, gain_first[None], gain_second[None], w_query, w_out, w_gate.T, w_up.T, w_down,
+        keys, values, starts, 1)
+    grad_normed_second, query_0, query_y, ffn_parts, ffn_sums = ffn_call(
+        normed_second, w_query, cots, down_here, gate_here, up_here, 3)
     grad_residual, grad_context, gain_second_part, query_x, down_sums, out_sums = back_first(
-        grad_normed_second, residual, cot_here, gain_two[None], context_own, out_whole, ffn_sums, query_0, 5)
+        grad_normed_second, residual, cot_here, gain_two, context_own, out_whole, ffn_sums, query_0, 5)
     grad_queries, grad_keys, grad_values = attend_back(
         starts, queries, keys, values, grad_context, log_totals)
     grad_kv = jnp.stack([grad_keys, grad_values], axis=1)
     down_shard, gate_shard, up_shard, out_shard, query_shard, grad_input, output, gains, _ = back_last(
-        grad_queries, rows_first, grad_residual, inputs_here, gain_one[None], query_y, query_0, query_x,
+        grad_queries, rows_first, grad_residual, inputs_here, gain_one, query_y, query_0, query_x,
         ffn_sums, down_sums, out_sums, ffn_parts, residual, gain_second_part, 6)
     return (output, grad_input, grad_kv, gains[0], gains[1], query_shard, out_shard,
             gate_shard.T, up_shard.T, down_shard)

time: 636 us -> 592 us (0.931)
  local copies, waits for them, and re-layouts: 51.2 us -> 21.4 us
  matrix products: 11.2 us -> 0 us
    unnamed x92 -> x24, local copies, waits for them, and re-layouts: 44.1 us -> 13.2 us
    dot_general x2 -> x0, matrix products: 11.2 us -> none  [contract(): lax.dot_general(left, right, (((left_dim,), (right_dim,)), ((), ())), pre...]
    pallas_call x3 -> x1, Pallas kernels: 236 us -> 231 us  [front_call(): pl.pallas_call(front_kernel, out_shape=(S((seq_len, width), bf16), S((seq...]
where the time goes in v4:
time: 592 us; the launch traced here: 588 us
  Pallas kernels  561 us (95%)
  local copies, waits for them, and re-layouts  21.4 us (4%)
    pallas_call x1, Pallas kernels, front_call(): pl.pallas_call(front_kernel, out_shape=(S((seq_len, width), bf16), S((seq...  231 us
    pallas_call x1, Pallas kernels, back_last(): pl.pallas_call(back_last_kernel, out_shape=(S((hidden, blk), f32),) * 3 +...  172 us
    pallas_call x1, Pallas kernels, ffn_call(): pl.pallas_call(ffn_kernel, out_shape=(jax.ShapeDtypeStruct((share, width)...  105 us
    pallas_call x1, Pallas kernels, back_first(): pl.pallas_call(back_first_kernel, out_shape=(S((share, width), f32), S((s...  40.9 us
    unnamed x24, local copies, waits for them, and re-layouts  13.2 us
    pallas_call x1, Pallas kernels, attend_back(): pl.pallas_call(backward_kernel, grid=(heads,), in_specs=[row, head, head,...  13.1 us

profile of v4, /device:TPU:0, one launch (start us, length us, event | category | flops | bytes accessed | tf_op | source)
XLA Modules:
  0.0 587.8 jit_solution(15179782747776241137)
XLA Ops:
  0.6 1.9 convert_reduce_fusion
  2.6 5.6 fusion
  8.2 1.9 copy_bitcast_fusion
  10.1 230.8 %front.1 = (bf16[1024,2048]{1,0:T(8,128)(2,1)}, bf16[1024,2048]{1,0:T(8,128)(2,1)}, bf16[1376,2048]{1,0:T(8,128)(2,1)}, bf16[1376,2048]{1,0:T(8,128)(2,1)}, bf16...) custom-call(bf16[256,2048]{1,0:T(8,128)(2,1)} %x.1, ...), custom_call_target="tpu_custom_call" | custom-call | tf_op jit(solution)/shard_map/front/pallas_call | solution.py:514
  240.9 104.8 %feed_forward.1 = (f32[256,2048]{1,0:T(8,128)}, bf16[256,2048]{1,0:T(8,128)(2,1)}, bf16[256,2048]{1,0:T(8,128)(2,1)}, bf16[1024,2048]{1,0:T(8,128)(2,1)}, bf16[3,1376,1024]{2,1,0:T(8,128)(2,1)}) custom-call(bf16[256,2048]{1,0:T(8,128)(2,1)} %get-tuple-element.48.normed, bf16[256,512]{1,0:T(8,128)(2,1)} %wq.3, bf16[1024,2048]{1,0:T(8,128)(2,1)} %get-tuple-element.49.cots_in, ...), custom_call_target="tpu_custom_call" | custom-call | flops 51942260736 | bytes 41943040 | tf_op jit(solution)/shard_map/feed_forward/pallas_call | solution.py:710
  345.7 40.9 %back_first.1 = (f32[256,2048]{1,0:T(8,128)}, bf16[1024,512]{1,0:T(8,128)(2,1)}, f32[1,2048]{1,0:T(1,128)}, bf16[256,2048]{1,0:T(8,128)(2,1)}, bf16[1376,512]{1,0:T(8,128)(2,1)}, /*index=5*/bf16[2048,1024]{1,0:T(8,128)(2,1)}) custom-call(f32[256,2048]{1,0:T(8,128)} %get-tuple-element.53.dn2, f32[256,2048]{1,0:T(8,128)} %get-tuple-element.54.residual, ...), custom_call_target="tpu_custom_call" | custom-call | tf_op jit(solution)/shard_map/back_first/pallas_call | solution.py:819
  386.6 13.1 %attend_back.1 = (bf16[1024,512]{1,0:T(8,128)(2,1)}, f32[1024,512]{1,0:T(8,128)}, f32[1024,512]{1,0:T(8,128)}) custom-call(s32[1,1024]{1,0:T(1,128)} %bitcast.23, bf16[1024,512]{1,0:T(8,128)(2,1)} %get-tuple-element.47.q_ref, bf16[1024,512]{1,0:T(8,128)(2,1)} %get-tuple-element.109.keys.k_ref, bf16[1024,512]{1,0:T(8,128)(2,1)} %get-tuple-element.108.values.v_ref, ...), custom_call_target="tpu_custom_call" | custom-call | flops 3758096384 | bytes 9437184 | tf_op jit(solution)/shard_map/attend_back/pallas_call | solution.py:271
  399.7 171.5 %back_last.1 = (f32[1376,256]{1,0:T(8,128)}, f32[1376,256]{1,0:T(8,128)}, f32[1376,256]{1,0:T(8,128)}, f32[512,256]{1,0:T(8,128)}, f32[256,512]{1,0:T(8,128)}, /...) custom-call(bf16[1024,512]{1,0:T(8,128)(2,1)} %get-tuple-element.63.grad_q, ...), custom_call_target="tpu_custom_call" | custom-call | tf_op jit(solution)/shard_map/back_last/pallas_call | solution.py:1056
  571.2 2.7 pad_maximum_fusion
  573.9 0.0 copy-start.7
  573.9 0.0 copy-start.4
  573.9 5.2 copy.26
  579.1 0.0 copy-done.7
  579.1 0.0 copy-start
  579.1 0.6 fusion.1
  579.8 0.0 copy-done.4
  579.8 1.0 copy.38
  580.7 0.0 copy-done
  580.7 0.0 copy-start.6
  580.7 0.0 copy-start.5
  580.8 1.3 copy.39
  582.1 0.1 copy-done.6
  582.1 0.0 copy-start.3
  582.1 0.8 copy.40
  582.9 0.0 copy-done.5
  582.9 0.8 copy.41
  583.7 0.0 copy-done.3
  583.7 1.1 copy.42
  584.8 0.0 copy-done.2
  584.8 1.1 copy.43
  585.9 0.8 copy-done.1
  586.7 1.1 copy.44
  (2 shorter events, 0.0 us)
Async XLA Ops:
  573.9 5.3 copy-start.7
  573.9 5.9 %copy-start.4 = (bf16[256,2048]{1,0:T(8,128)(2,1)S(1)}, bf16[256,2048]{1,0:T(8,128)(2,1)}, u32[]{:S(2)}) copy-start(bf16[256,2048]{1,0:T(8,128)(2,1)} %get-tuple-element.120) | copy-start | bytes 3145732
  579.1 1.6 copy-start
  580.7 1.4 copy-start.6
  580.7 2.2 copy-start.5
  582.1 1.6 copy-start.3
  582.9 1.9 copy-start.2
  584.8 1.9 copy-start.1

commit v5 on v4

--- a/solution.py
+++ b/solution.py
@@ -171,12 +171,25 @@
         self.share = parts.shape[0] // 4
         self.half = self.share // 2
 
+    def prepare(self):
+        share, half = self.share, self.half
+        self.first = self.copies.prepare(self.parts.at[pl.ds(3 * share, half), :], self.relay.at[0], SIDE)
+        self.second = self.copies.prepare(self.parts.at[pl.ds(3 * share + half, half), :], self.relay.at[1], Z_LOW)
+        self.side = [self.copies.prepare(self.parts.at[pl.ds(share, half), :], self.landed.at[0, pl.ds(0, half), :], SIDE)]
+        self.low = [self.copies.prepare(self.parts.at[pl.ds(2 * share + half, half), :], self.landed.at[1, pl.ds(half, half), :], Z_LOW)]
+
+    def start_across(self):
+        self.copies.start(self.first)
+        self.copies.start(self.second)
+        self.copies.start(self.side[0])
+
+    def start_rest(self):
+        self.copies.start(self.low[0])
+
     def start(self):
-        share, half = self.share, self.half
-        self.first = self.copies.swap(self.parts.at[pl.ds(3 * share, half), :], self.relay.at[0], SIDE)
-        self.second = self.copies.swap(self.parts.at[pl.ds(3 * share + half, half), :], self.relay.at[1], Z_LOW)
-        self.side = [self.copies.swap(self.parts.at[pl.ds(share, half), :], self.landed.at[0, pl.ds(0, half), :], SIDE)]
-        self.low = [self.copies.swap(self.parts.at[pl.ds(2 * share + half, half), :], self.landed.at[1, pl.ds(half, half), :], Z_LOW)]
+        self.prepare()
+        self.start_across()
+        self.start_rest()
 
     def relayed(self):
         share, half = self.share, self.half
@@ -194,6 +207,7 @@
 
 ROWS=256
 DOC_MOST=512
+DOCS=16
 
 
 def key_range(block, seq_len):
@@ -225,65 +239,42 @@
         lse_ref[h, :, here] = top + jnp.log(total)
 
 
-def backward_kernel(starts_ref, q_ref, k_ref, v_ref, grad_ref, lse_ref, dq_ref, dk_ref, dv_ref):
+def attend_head_back(h, starts_ref, q_ref, k_ref, v_ref, grad_ref, lse_ref, dq_ref, pair_ref, dk_ref, dv_ref):
     seq_len = q_ref.shape[0]
     scale = HEAD_DIM ** -0.5
+    lanes = pl.ds(pl.multiple_of(h * HEAD_DIM, HEAD_DIM), HEAD_DIM)
     for block in range(seq_len // ROWS):
         low, high = key_range(block, seq_len)
         here = pl.ds(block * ROWS, ROWS)
-        k = k_ref[low:high, :]
-        v = v_ref[low:high, :]
-        q = q_ref[here, :]
-        grad = grad_ref[here, :]
+        k = k_ref[low:high, lanes]
+        v = v_ref[low:high, lanes]
+        q = q_ref[here, lanes]
+        grad = grad_ref[here, lanes]
         s = scores_turned(q, k, starts_ref[:, here], low, block * ROWS, scale)
-        probs = jnp.exp(s - lse_ref[0, :, here])
+        probs = jnp.exp(s - lse_ref[h, :, here])
         grad_probs = dot(v, grad, 1, 1)
         spread = jnp.sum(probs * grad_probs, axis=0, keepdims=True)
         grad_s = (probs * (grad_probs - spread)).astype(bf16)
-        dq_ref[here, :] = (dot(grad_s, k, 0, 0) * scale).astype(bf16)
+        dq_ref[here, lanes] = (dot(grad_s, k, 0, 0) * scale).astype(bf16)
         dk = dot(grad_s, q, 1, 0) * scale
         dv = dot(probs.astype(bf16), grad, 1, 0)
-        old = max(low, min(high, block * ROWS))
-        if low == 0 and block == 0:
-            dk_ref[low:high, :] = dk
-            dv_ref[low:high, :] = dv
-        else:
+        old = block * ROWS
+        if block:
             n = old - low
             dk_ref[low:old, :] += dk[:n]
             dv_ref[low:old, :] += dv[:n]
             dk_ref[old:high, :] = dk[n:]
             dv_ref[old:high, :] = dv[n:]
-
-
-def specs(seq_len):
-    row = pl.BlockSpec((1, seq_len), lambda h: (0, 0))
-    head = pl.BlockSpec((seq_len, HEAD_DIM), lambda h: (0, h))
-    lse = pl.BlockSpec((1, 1, seq_len), lambda h: (h, 0, 0))
-    return row, head, lse
-
-
-def attend_back(starts, q, k, v, grad, lse_array):
-    seq_len, width = q.shape
-    heads = width // HEAD_DIM
-    row, head, lse = specs(seq_len)
-    flops = heads * seq_len * seq_len * HEAD_DIM * 7
-    wide = jax.ShapeDtypeStruct(q.shape, f32)
-    return pl.pallas_call(
-        backward_kernel, grid=(heads,),
-        in_specs=[row, head, head, head, head, lse], out_specs=(head, head, head),
-        out_shape=(jax.ShapeDtypeStruct(q.shape, bf16), wide, wide),
-        cost_estimate=pl.CostEstimate(flops=flops, bytes_accessed=9 * q.size * 2, transcendentals=heads * seq_len * seq_len // 2),
-        name="attend_back",
-    )(starts, q, k, v, grad, lse_array)
-
-
-def starts_of(segments):
-    return jnp.sum((segments[0][None, :] < segments[0][:, None]).astype(jnp.int32), axis=1)[None, :]
-
-
-def front_kernel(x, cot, gain_one_in, gain_two_in, wq, wo, wg, wu, wd, keys, values, starts,
+        else:
+            dk_ref[low:high, :] = dk
+            dv_ref[low:high, :] = dv
+    pair_ref[:, 0, lanes] = dk_ref[...]
+    pair_ref[:, 1, lanes] = dv_ref[...]
+
+
+def front_kernel(x, cot, gain_one_in, gain_two_in, wq, wo, wg, wu, wd, pairs, segments,
                  rows_out, cots, gate, up, down, out_out, queries, context_own, lse, residual, normed,
-                 x_here, cot_here, gain_one, gain_two,
+                 x_here, cot_here, gain_one, gain_two, keys, values, starts,
                  first, rows, query, out, context,
                  send_sems, recv_sems, local_sems):
     place = Place()
@@ -364,7 +355,6 @@
         send_y(i, own_piece[i], 0, own)
     wq_x = [copies.swap(wq, qrows(own), SIDE)]
     wq_core = [core_query(own, wq)]
-    send_z(0, own_piece[0], own)
 
     spots = [pl.ds(pl.multiple_of(absolute(place, s) * blk, blk), blk) for s in range(8)]
     for s in range(8):
@@ -384,6 +374,21 @@
     lax.fori_loop(0, share // 32, norm_first, 0)
     for c in range(2):
         line(1, row_block(c, True), c)
+
+    def split(i, carry):
+        here = pl.ds(i * 32, 32)
+        both = pairs[here, :, :]
+        keys[here, :] = both[:, 0, :]
+        values[here, :] = both[:, 1, :]
+        return carry
+
+    lax.fori_loop(0, pairs.shape[0] // 32, split, 0)
+    ids = segments[...]
+    begun = jnp.zeros_like(ids)
+    for document in range(DOCS - 1):
+        size = jnp.sum((ids == document).astype(jnp.int32), axis=1, keepdims=True)
+        begun = begun + jnp.where(ids > document, size, 0)
+    starts[...] = begun
     rows[pl.ds(mp * share, share), :] = first[...]
     query[pl.ds(own * blk, blk), :] = wq[...]
     out[pl.ds(mp * zrow, zrow), pl.ds(pl.multiple_of(own * blk, blk), blk)] = wo[...]
@@ -396,46 +401,41 @@
     wq_core.append(core_query(own + DEEPER))
     arrive("o", 1)
     line(2, out_block(False), "o")
-    send_z(1, own_piece[1], own)
-    send_z(2, own_piece[2], own)
     for i in range(3):
         copies.got(xhop[i])
         piece = tile(mats[i][1], 0, across)
         send_y(i, piece, 0, across)
         core_tile(i, 0, across)
+    for c in range(2):
+        arrive(c, 1)
+        line(2, row_block(c, False), c)
+    for i in range(3):
+        send_z(i, own_piece[i], own)
     for item, spot in zip(wq_x, (across, across + DEEPER)):
         copies.got(item)
         wq_core.append(core_query(spot))
-    for c in range(2):
-        arrive(c, 1)
-        line(2, row_block(c, False), c)
+    cot_x = copies.swap(cot_here, cots.at[share:2 * share, :], SIDE)
     arrive("o", 2)
     line(3, out_block(False), "o")
-    for i in range(3):
-        send_z(i, tile(mats[i][1], 0, across), across)
-    cot_x = copies.swap(cot_here, cots.at[share:2 * share, :], SIDE)
-    for i in range(2):
-        copies.got(zhop[i][0])
-        send_y(i, tile(mats[i][1], 1, own), 1, own)
-        core_tile(i, 1, own)
+    for c in range(2):
+        arrive(c, 2)
+        line(3, row_block(c, False), c)
+    cot_z = copies.swap(cot_here, cots.at[2 * share:3 * share, :], Z_LOW)
     arrive("o", 3)
     out_y = copies.swap(columns(own), columns(own + DEEPER), DEEP)
     out_x = [copies.swap(columns(own), columns(own), SIDE)]
     out_core = [core_out(own)]
-    for c in range(2):
-        arrive(c, 2)
-        line(3, row_block(c, False), c)
-    copies.got(zhop[2][0])
-    send_y(2, tile(mats[2][1], 1, own), 1, own)
-    core_tile(2, 1, own)
+
+    def across_z(i):
+        copies.got(zhop[i][0])
+        send_y(i, tile(mats[i][1], 1, own), 1, own)
+        core_tile(i, 1, own)
+
+    across_z(0)
     for copy in locals_:
         copy.wait()
-    cot_z = copies.swap(cot_here, cots.at[2 * share:3 * share, :], Z_LOW)
     for item in wq_core:
         copies.got(item)
-    copies.got(out_y)
-    out_x.append(copies.swap(columns(own + DEEPER), columns(own + DEEPER), SIDE))
-    out_core.append(core_out(own + DEEPER))
     for c in range(2):
         arrive(c, 3)
     save_rows = copies.local(rows, rows_out)
@@ -459,24 +459,23 @@
                                      context_own.at[:, pl.ds(mp * local, local)], mask))
     context_own[:, pl.ds(pl.multiple_of(mp * local, local), local)] = context[pl.ds(mp * share, share), :]
     for i in range(3):
-        copies.got(zhop[i][1])
-        send_y(i, tile(mats[i][1], 1, across), 1, across)
-        core_tile(i, 1, across)
+        send_z(i, tile(mats[i][1], 0, across), across)
+    across_z(1)
+    across_z(2)
+    copies.got(out_y)
+    out_x.append(copies.swap(columns(own + DEEPER), columns(own + DEEPER), SIDE))
+    out_core.append(core_out(own + DEEPER))
+    copies.got(out_x[0])
+    out_core.append(core_out(across))
+    copies.got(cot_z)
+    copies.swap(cots.at[2 * share:3 * share, :], cots.at[3 * share:4 * share, :], SIDE)
     for j in range(2):
         for i in range(3):
             item, z, spot = yhop[i][j]
             copies.got(item)
             core_tile(i, z, spot)
-    copies.got(out_x[0])
-    out_core.append(core_out(across))
-    copies.got(cot_z)
-    copies.swap(cots.at[2 * share:3 * share, :], cots.at[3 * share:4 * share, :], SIDE)
     copies.got(out_x[1])
     out_core.append(core_out(across + DEEPER))
-    for i in range(3):
-        item, z, spot = yhop[i][2]
-        copies.got(item)
-        core_tile(i, z, spot)
     for item in out_core + tokens_in:
         copies.got(item)
     save_out = copies.local(out, out_out)
@@ -497,18 +496,23 @@
 
     lax.fori_loop(0, share // 32, norm_second, 0)
     for i in range(3):
-        item, z, spot = yhop[i][3]
-        copies.got(item)
-        core_tile(i, z, spot)
+        copies.got(zhop[i][1])
+        send_y(i, tile(mats[i][1], 1, across), 1, across)
+        core_tile(i, 1, across)
+    for j in (2, 3):
+        for i in range(3):
+            item, z, spot = yhop[i][j]
+            copies.got(item)
+            core_tile(i, z, spot)
     save_rows.wait()
     save_out.wait()
     copies.finish()
 
 
-def front_call(x, cot, gain_one, gain_two, wq, wo, wg, wu, wd, keys, values, starts, ident):
+def front_call(x, cot, gain_one, gain_two, wq, wo, wg, wu, wd, pairs, segments, ident):
     share, width = x.shape
     hidden, blk = wd.shape
-    seq_len, local = keys.shape
+    seq_len, _, local = pairs.shape
     V = pltpu.VMEM
     S = jax.ShapeDtypeStruct
     return pl.pallas_call(
@@ -517,14 +521,15 @@
             S((seq_len, width), bf16), S((seq_len, width), bf16), S((hidden, width), bf16), S((hidden, width), bf16),
             S((hidden, width), bf16), S((width, width), bf16), S((seq_len, local), bf16), S((share, width), bf16),
             S((local // HEAD_DIM, 1, seq_len), f32), S((share, width), f32), S((share, width), bf16),
-            S((share, width), bf16), S((share, width), bf16), S((1, width), f32), S((1, width), f32)),
-        in_specs=[VM] * 12,
-        out_specs=(ANY,) * 6 + (VM,) * 9,
+            S((share, width), bf16), S((share, width), bf16), S((1, width), f32), S((1, width), f32),
+            S((seq_len, local), bf16), S((seq_len, local), bf16), S((1, seq_len), jnp.int32)),
+        in_specs=[VM] * 11,
+        out_specs=(ANY,) * 6 + (VM,) * 12,
         scratch_shapes=[
             V((share, width), bf16), V((seq_len, width), bf16), V((width, local), bf16), V((width, width), bf16),
             V((seq_len, local), bf16), DMA((96,)), DMA((96,)), DMA((8,))],
         compiler_params=params(ident, 60 << 20), name="front",
-    )(x, cot, gain_one, gain_two, wq, wo, wg, wu, wd, keys, values, starts)
+    )(x, cot, gain_one, gain_two, wq, wo, wg, wu, wd, pairs, segments)
 
 
 def hidden_cuts(hidden):
@@ -630,15 +635,20 @@
             for item in hops[2]:
                 copies.start(item)
 
+            forward[0].wait_recv()
+            forward[1].wait_recv()
+
         @pl.when(r == 3)
         def _():
-            forward[0].wait_recv()
-            forward[1].wait_recv()
             for item in hops[2]:
                 copies.received(item)
             copies.start(over_deep)
-        block(r)
-        return carry
+            reduce.start_across()
+        block(jnp.where(r < 2, r, 5 - r))
+        return carry
+
+    reduce = QuadReduce(copies, dparts, relay, landed)
+    reduce.prepare()
 
     forward = [copies.describe(at(2, 0), at(3, 0), place.partner(SIDE), copies.count),
                copies.describe(at(1, 1), at(3, 1), place.partner(Z_LOW), copies.count + 1)]
@@ -647,8 +657,7 @@
     for item in (low_a, side_b, low_b, side_a):
         item["got"] = True
     pl.semaphore_signal(free_sem, inc=1, device_id=place.partner(CORE), device_id_type=MESH)
-    reduce = QuadReduce(copies, dparts, relay, landed)
-    reduce.start()
+    reduce.start_rest()
     save = copies.local(fparts, fparts_out)
 
     base = copies.count
@@ -670,8 +679,8 @@
         give_copy(i).start()
         return carry
 
+    reduce.relayed()
     lax.fori_loop(0, 3, give, 0)
-    reduce.relayed()
 
     def keep(i, carry):
         give_copy(i).wait_recv()
@@ -725,22 +734,29 @@
     )(normed, wq, cots, down, gate, up)
 
 
-def back_first_kernel(dn2, residual, cot, gain, context, out_whole, sums, query_0,
-                      dres, heads, gain_part, query_x, down_sums, out_sums,
-                      keep_d, deep_d, grad_low, wout, dctx, give_o, core_o,
+def back_first_kernel(dn2, residual, cot, gain, context, queries, keys, values, lse, starts, query_0, query_y,
+                      out_whole, sums,
+                      dres, gain_part, query_x, query_xy, grad_q, pairs, down_sums, gate_sums, out_sums,
+                      heads, keep_d, deep_d, high_d, deep_g, grad_low, wout, dctx, give_o, core_o, dk, dv,
                       send_sems, recv_sems, local_sems):
     place = Place()
     mp = place.mp
     share, width = dn2.shape
     hidden = keep_d.shape[0]
+    half = hidden // 2
     local = heads.shape[1]
     wide = width // 2
+    quarter = wide // 2
+    blk = quarter // 2
     copies = Copies(place, send_sems, recv_sems, local_sems)
     loads = [copies.local(out_whole.at[pl.ds(z * local, local), :], wout.at[z]) for z in range(4)]
-    load_d = copies.local(sums.at[0, :, pl.ds(0, wide // 2)], keep_d)
+    load_d = copies.local(sums.at[0, :, pl.ds(0, quarter)], keep_d)
+    load_g = copies.local(sums.at[1, :, pl.ds(0, quarter)], gate_sums)
     greet(place, (1, 2, 3, CORE, SIDE, DEEP))
-    in_d = copies.swap(sums.at[0, :, pl.ds(wide // 2, wide // 2)], deep_d, DEEP)
+    in_d, in_g = ([copies.swap(sums.at[i, :, pl.ds(quarter + x * blk, blk)], target.at[:, pl.ds(x * blk, blk)], DEEP)
+                   for x in (0, 1)] for i, target in ((0, deep_d), (1, deep_g)))
     copies.swap(query_0, query_x, SIDE)
+    copies.swap(query_y, query_xy, SIDE)
     gain_part[...] = jnp.zeros_like(gain_part)
 
     def norm(i, carry):
@@ -760,13 +776,14 @@
     lax.fori_loop(0, share // 32, norm, 0)
     for copy in loads:
         copy.wait()
+    heads_in = []
     for mask in (2, 3, 1, 0):
         other = place.partner(mask)[1]
         there = pl.ds(pl.multiple_of(other * local, local), local)
         piece = dot(grad_low[...], wout[other], 1, 1).astype(bf16)
         if mask:
             dctx[:, there] = piece
-            copies.swap(dctx.at[:, there], heads.at[pl.ds(mp * share, share), :], mask)
+            heads_in.append(copies.swap(dctx.at[:, there], heads.at[pl.ds(mp * share, share), :], mask))
         else:
             heads[pl.ds(mp * share, share), :] = piece
     chunks = width // 512
@@ -794,14 +811,35 @@
 
     lax.fori_loop(0, chunks, keep, 0)
     load_d.wait()
-    copies.got(in_d)
+    give_rows = pl.ds(half, half)
+    across = []
+    for x in (0, 1):
+        there = pl.ds(x * blk, blk)
+        copies.got(in_d[x])
+        add_into(keep_d.at[:, there], (half, half), deep_d.at[give_rows, there], step=16)
+        across.append(copies.swap(keep_d.at[give_rows, there], high_d.at[:, there], Z_HIGH))
+        add_into(keep_d.at[:, there], (0, half), deep_d.at[:, there], step=16)
+    for item in heads_in:
+        copies.got(item)
+
+    def one_head(h, carry):
+        attend_head_back(h, starts, queries, keys, values, heads, lse, grad_q, pairs, dk, dv)
+        return carry
+
+    lax.fori_loop(0, local // HEAD_DIM, one_head, 0)
+    load_g.wait()
+    for x in (0, 1):
+        copies.got(in_g[x])
+    add_into(gate_sums, (0, hidden), deep_g)
+    for x in (0, 1):
+        copies.got(across[x])
 
     def add_d(n, carry):
-        rows = pl.ds(n * 32, 32)
-        down_sums[rows, :] = (keep_d[rows, :].astype(f32) + deep_d[rows, :].astype(f32)).astype(bf16)
-        return carry
-
-    lax.fori_loop(0, hidden // 32, add_d, 0)
+        rows = pl.ds(n * 16, 16)
+        down_sums[rows, :] = (keep_d[rows, :].astype(f32) + high_d[rows, :].astype(f32)).astype(bf16)
+        return carry
+
+    lax.fori_loop(0, half // 16, add_d, 0)
     copies.finish()
 
     def sent(n, carry):
@@ -811,31 +849,39 @@
     lax.fori_loop(0, chunks, sent, 0)
 
 
-def back_first(dn2, residual, cot, gain, context, out_whole, sums, query_0, ident):
+def back_first(dn2, residual, cot, gain, context, queries, keys, values, lse, starts, query_0, query_y,
+               out_whole, sums, ident):
     share, width = dn2.shape
     hidden = sums.shape[1]
+    half = hidden // 2
+    seq_len, local = queries.shape
+    quarter = width // 4
     V = pltpu.VMEM
     S = jax.ShapeDtypeStruct
     return pl.pallas_call(
         back_first_kernel,
-        out_shape=(S((share, width), f32), S((share * 4, width // 4), bf16), S((1, width), f32),
-                   S(query_0.shape, bf16), S((hidden, width // 4), bf16), S((width, width // 2), bf16)),
-        in_specs=[VM] * 5 + [ANY, ANY, VM],
-        out_specs=(VM,) * 6,
+        out_shape=(S((share, width), f32), S((1, width), f32), S(query_0.shape, bf16), S(query_0.shape, bf16),
+                   S((seq_len, local), bf16), S((seq_len, 2, local), f32),
+                   S((half, quarter), bf16), S((hidden, quarter), bf16), S((width, width // 2), bf16)),
+        in_specs=[VM] * 12 + [ANY, ANY],
+        out_specs=(VM,) * 9,
         scratch_shapes=[
-            V((hidden, width // 4), bf16), V((hidden, width // 4), bf16), V((share, width), bf16),
+            V((seq_len, local), bf16), V((hidden, quarter), bf16), V((hidden, quarter), bf16), V((half, quarter), bf16),
+            V((hidden, quarter), bf16), V((share, width), bf16),
             V((4, width // 4, width), bf16), V((share, width), bf16), V((width, width // 2), bf16),
-            V((width, width // 2), bf16), DMA((12,)), DMA((12,)), DMA((5,))],
-        compiler_params=params(ident, 60 << 20), name="back_first",
-    )(dn2, residual, cot, gain, context, out_whole, sums, query_0)
-
-
-def back_last_kernel(grad_q, rows_first, dres, inputs, gain, query_y, query_0, query_x,
-                     sums, down_sums, out_sums, fparts, residual, gain_part,
-                     down, gate, up, out, query, grad_input, output, gains, query_whole,
-                     keep_f, deep_f, high_f, side_f, own_o, side_o, deep_o, z_o,
+            V((width, width // 2), bf16), V((seq_len, HEAD_DIM), f32), V((seq_len, HEAD_DIM), f32),
+            DMA((20,)), DMA((20,)), DMA((6,))],
+        compiler_params=params(ident, 63 << 20), name="back_first",
+    )(dn2, residual, cot, gain, context, queries, keys, values, lse, starts, query_0, query_y, out_whole, sums)
+
+
+def back_last_kernel(grad_q, dres, inputs, gain, query_0, query_y, query_x, query_xy, residual, gain_part,
+                     rows_first, sums, down_sums, gate_sums, out_sums, fparts,
+                     down, gate, up, out, query, grad_input, output, gains,
+                     keep_d, keep_g, keep_u, deep_u, high_g, high_u, side_f,
+                     own_o, deep_o, side_o, z_o,
                      give_q, own_q, core_q, side_q, deep_q, parts, relay, landed,
-                     grad_own, stream, dn1, gain_rows, gains_got,
+                     grad_own, rows, query_far, dn1, gain_rows, gains_got,
                      send_sems, recv_sems, local_sems):
     place = Place()
     mp = place.mp
@@ -846,77 +892,65 @@
     local = grad_q.shape[1]
     zrow = out.shape[0]
     quarter = 2 * blk
+    wide = width // 2
     copies = Copies(place, send_sems, recv_sems, local_sems)
-    load_rows = copies.local(rows_first, stream.at[pl.ds(0, share * 4), :])
-    load_d = copies.local(down_sums, keep_f.at[0])
+    load_rows = copies.local(rows_first, rows)
+    load_g = copies.local(gate_sums, keep_g)
+    load_d = copies.local(down_sums, keep_d)
+    load_o = copies.local(out_sums, own_o)
+    load_u = copies.local(sums.at[2, :, pl.ds(0, quarter)], keep_u)
     load_p = copies.local(fparts, parts)
-    load_f = [copies.local(sums.at[i, :, pl.ds(0, quarter)], keep_f.at[i]) for i in (1, 2)]
-    load_o = copies.local(out_sums, own_o)
-
-    def qrows(spot):
-        return query_whole.at[pl.ds(spot * blk, blk), :]
-
     greet(place, (1, 2, 3, CORE, SIDE, DEEP))
     tokens_in = []
     for mask in (2, 3, 1):
         other = place.partner(mask)[1]
         tokens_in.append(copies.swap(grad_q.at[pl.ds(other * share, share), :],
                                      grad_own.at[:, pl.ds(mp * local, local)], mask))
-    wq_across = copies.swap(query_y, qrows(side + 2), SIDE)
-    deep_in = [None]
-    for i in (1, 2):
-        deep_in.append([copies.swap(sums.at[i, :, pl.ds(quarter + x * blk, blk)], deep_f.at[i - 1, :, pl.ds(x * blk, blk)], DEEP)
-                        for x in (0, 1)])
-    held = [copies.local(query_0, qrows(side)), copies.local(query_y, qrows(side + 2)),
-            copies.local(query_x, qrows(1 - side))]
-    wq_core = [copies.swap(query_0, qrows(side + 4), CORE), copies.swap(query_y, qrows(side + 6), CORE),
-               copies.swap(query_x, qrows(1 - side + 4), CORE)]
+    in_u = [copies.swap(sums.at[2, :, pl.ds(quarter + x * blk, blk)], deep_u.at[:, pl.ds(x * blk, blk)], DEEP)
+            for x in (0, 1)]
+    near = (query_0, query_y, query_x, query_xy)
+    far_in = [copies.swap(piece, query_far.at[n], CORE) for n, piece in enumerate(near)]
+    give_rows = pl.ds(half, half)
+    mine = pl.ds(pl.multiple_of(side * blk, blk), blk)
+    theirs = pl.ds(pl.multiple_of((1 - side) * blk, blk), blk)
+    load_g.wait()
+    high_in_g = [copies.swap(keep_g.at[give_rows, pl.ds(x * blk, blk)], high_g.at[:, pl.ds(x * blk, blk)], Z_HIGH)
+                 for x in (0, 1)]
     load_d.wait()
-    give_rows = pl.ds(half, half)
-    high_in = [[copies.swap(keep_f.at[0, give_rows, pl.ds(x * blk, blk)], high_f.at[0, :, pl.ds(x * blk, blk)], Z_HIGH)
-                for x in (0, 1)]]
-    grad_own[:, pl.ds(mp * local, local)] = grad_q[pl.ds(mp * share, share), :]
+    side_in = [copies.swap(keep_d.at[:, theirs], side_f.at[0], SIDE)]
+    load_o.wait()
+
+    def block_o(deep, column):
+        return own_o.at[:, pl.ds(pl.multiple_of((2 * deep + column) * blk, blk), blk)]
+
+    deep_in_o = {column: copies.swap(block_o(1, x), deep_o.at[n], DEEP)
+                 for n, (column, x) in enumerate((("theirs", 1 - side), ("mine", side)))}
+    grad_own[:, pl.ds(pl.multiple_of(mp * local, local), local)] = grad_q[pl.ds(mp * share, share), :]
     load_rows.wait()
-    wide = width // 2
 
     def product(first):
-        return dot(stream[0:share * 4, first:first + wide], grad_q[...], 0, 0)
+        return dot(rows[:, first:first + wide], grad_q[...], 0, 0)
 
     give_q[...] = product(wide).astype(bf16)
     core_in_q = copies.swap(give_q, core_q, CORE)
     load_p.wait()
     reduce = QuadReduce(copies, parts, relay, landed)
     reduce.start()
-    load_o.wait()
-
-    def block_o(spot):
-        return own_o.at[:, pl.ds(spot * blk, blk)]
-
-    side_in_o = {y: copies.swap(block_o(2 * y + 1 - side), side_o.at[y], SIDE) for y in (1, 0)}
     keep_q = product(0)
     copies.got(core_in_q)
     own_q[...] = (keep_q + core_q[...].astype(f32)).astype(bf16)
     side_in_q = {y: copies.swap(own_q.at[pl.ds((2 * y + 1 - side) * blk, blk), :], side_q.at[y], SIDE) for y in (1, 0)}
-    reduce.relayed()
-    for copy in held:
-        copy.wait()
+    for item in far_in:
+        copies.got(item)
     for item in tokens_in:
         copies.got(item)
-    copies.got(wq_across)
-    wq_core.append(copies.swap(qrows(1 - side + 2), qrows(1 - side + 6), CORE))
-    for item in wq_core:
-        copies.got(item)
-    load_wq = copies.local(query_whole, stream)
-    load_wq.wait()
-
-    def first_back(n, carry):
-        there = pl.ds(pl.multiple_of(n * 512, 512), 512)
-        dn1[:, there] = dot(grad_own[...], stream[there, :], 1, 1)
-        return carry
-
-    lax.fori_loop(0, width // 512, first_back, 0)
+    spot_of = (side, side + 2, 1 - side, 3 - side)
+    for n in range(4):
+        dn1[:, pl.ds(pl.multiple_of(spot_of[n] * blk, blk), blk)] = dot(grad_own[...], near[n][...], 1, 1)
+        dn1[:, pl.ds(pl.multiple_of((spot_of[n] + 4) * blk, blk), blk)] = dot(grad_own[...], query_far[n], 1, 1)
     gain_rows[0:1, :] = jnp.zeros((1, width), f32)
     gain_rows[1:2, :] = gain_part[...]
+    spots = [pl.ds(pl.multiple_of(absolute(place, s) * blk, blk), blk) for s in range(8)]
 
     def norm(i, carry):
         here = pl.ds(i * 32, 32)
@@ -927,16 +961,14 @@
         grad_scaled = grad * gain[...]
         back = inverse * (grad_scaled - scaled * jnp.mean(grad_scaled * scaled, axis=-1, keepdims=True))
         total = dres[here, :] + back
-        for spot in range(8):
-            there = pl.ds(pl.multiple_of(absolute(place, spot) * blk, blk), blk)
-            grad_input[here, there] = total[:, spot * blk:(spot + 1) * blk]
+        for s in range(8):
+            grad_input[here, spots[s]] = total[:, s * blk:(s + 1) * blk]
         gain_rows[0:1, :] += jnp.sum(grad * scaled, axis=0, keepdims=True)
         return carry
 
     lax.fori_loop(0, share // 32, norm, 0)
-    for spot in range(8):
-        there = pl.ds(pl.multiple_of(absolute(place, spot) * blk, blk), blk)
-        gains[:, there] = gain_rows[:, spot * blk:(spot + 1) * blk]
+    for s in range(8):
+        gains[:, spots[s]] = gain_rows[:, s * blk:(s + 1) * blk]
     gain_masks = (1, 2, CORE, SIDE, DEEP)
     gain_state = {"item": None, "at": 0}
 
@@ -952,50 +984,40 @@
             gain_state["item"] = copies.swap(gains, gains_got.at[gain_state["at"]], gain_masks[gain_state["at"]])
             gain_state["at"] += 1
 
-    def deep_sum(i):
-        sent = []
+    gain_hop()
+    load_u.wait()
+    high_in_u = []
+    for x in (0, 1):
+        there = pl.ds(x * blk, blk)
+        copies.got(in_u[x])
+        add_into(keep_u.at[:, there], (half, half), deep_u.at[give_rows, there], step=16)
+        high_in_u.append(copies.swap(keep_u.at[give_rows, there], high_u.at[:, there], Z_HIGH))
+        add_into(keep_u.at[:, there], (0, half), deep_u.at[:, there], step=16)
+    reduce.relayed()
+    gain_hop()
+
+    def high_sum(keep, high, items, i):
         for x in (0, 1):
-            copies.got(deep_in[i][x])
-            there = pl.ds(x * blk, blk)
-            add_into(keep_f.at[i, :, there], (half, half), deep_f.at[i - 1, give_rows, there], step=16)
-            sent.append(copies.swap(keep_f.at[i, give_rows, there], high_f.at[i, :, there], Z_HIGH))
-        for x in (0, 1):
-            there = pl.ds(x * blk, blk)
-            add_into(keep_f.at[i, :, there], (0, half), deep_f.at[i - 1, :, there], step=16)
-        high_in.append(sent)
-
-    def high_sum(i):
-        for x in (0, 1):
-            copies.got(high_in[i][x])
-            add_into(keep_f.at[i, :, pl.ds(x * blk, blk)], (0, half), high_f.at[i, :, pl.ds(x * blk, blk)], step=16)
-        there = pl.ds(pl.multiple_of((1 - side) * blk, blk), blk)
-        return copies.swap(keep_f.at[i, pl.ds(0, half), there], side_f.at[i], SIDE)
-
-    gain_hop()
-    load_f[0].wait()
-    deep_sum(1)
-    gain_hop()
-    side_in = [high_sum(0)]
-    gain_hop()
+            copies.got(items[x])
+        add_into(keep.at[:, theirs], (0, half), high.at[:, theirs], step=16)
+        side_in.append(copies.swap(keep.at[pl.ds(0, half), theirs], side_f.at[i], SIDE))
+        add_into(keep.at[:, mine], (0, half), high.at[:, mine], step=16)
+
     deep_in_q = None
     for y in (1, 0):
         copies.got(side_in_q[y])
-        spot = 2 * y + side
-        rows = pl.ds(pl.multiple_of(spot * blk, blk), blk)
-        own_q[rows, :] = (own_q[rows, :].astype(f32) + side_q[y].astype(f32)).astype(bf16)
+        here = pl.ds(pl.multiple_of((2 * y + side) * blk, blk), blk)
+        own_q[here, :] = (own_q[here, :].astype(f32) + side_q[y].astype(f32)).astype(bf16)
         if y:
-            deep_in_q = copies.swap(own_q.at[rows, :], deep_q, DEEP)
+            deep_in_q = copies.swap(own_q.at[here, :], deep_q, DEEP)
+    copies.got(deep_in_o["theirs"])
+    add_into(block_o(0, 1 - side), (0, width), deep_o.at[0])
+    side_in_o = copies.swap(block_o(0, 1 - side), side_o, SIDE)
     gain_hop()
-    load_f[1].wait()
-    deep_sum(2)
+    high_sum(keep_g, high_g, high_in_g, 1)
     gain_hop()
-    deep_in_o = None
-    for y in (1, 0):
-        copies.got(side_in_o[y])
-        there = pl.ds(pl.multiple_of((2 * y + side) * blk, blk), blk)
-        add_into(own_o.at[:, there], (0, width), side_o.at[y])
-        if y:
-            deep_in_o = copies.swap(own_o.at[:, there], deep_o, DEEP)
+    copies.got(deep_in_o["mine"])
+    add_into(block_o(0, side), (0, width), deep_o.at[1])
     gain_hop()
     reduce.arrived()
 
@@ -1003,23 +1025,21 @@
         here = pl.ds(i * 32, 32)
         total = (residual[here, :] + parts[here, :].astype(f32) + landed[0, here, :].astype(f32)
                  + landed[1, here, :].astype(f32)).astype(bf16)
-        for spot in range(8):
-            there = pl.ds(pl.multiple_of(absolute(place, spot) * blk, blk), blk)
-            output[here, there] = total[:, spot * blk:(spot + 1) * blk]
+        for s in range(8):
+            output[here, spots[s]] = total[:, s * blk:(s + 1) * blk]
         return carry
 
     lax.fori_loop(0, share // 32, finish_output, 0)
-    mine = pl.ds(pl.multiple_of(side * blk, blk), blk)
-    copies.got(deep_in_o)
-    add_into(own_o.at[:, mine], (0, width), deep_o)
+    gain_hop()
+    copies.got(side_in_o)
+    add_into(block_o(0, side), (0, width), side_o)
     z_in = []
     for n, mask in enumerate((2, 3, 1)):
         other = place.partner(mask)[1]
         z_in.append(copies.swap(own_o.at[pl.ds(other * zrow, zrow), mine], z_o.at[n], mask))
     copies.got(deep_in_q)
     query[...] = own_q[pl.ds(pl.multiple_of(side * blk, blk), blk), :].astype(f32) + deep_q[...].astype(f32)
-    side_in.append(high_sum(1))
-    side_in.append(high_sum(2))
+    high_sum(keep_u, high_u, high_in_u, 2)
     for item in z_in:
         copies.got(item)
 
@@ -1032,11 +1052,11 @@
         return carry
 
     lax.fori_loop(0, zrow // 32, add_z, 0)
-    for i, target in enumerate((down, gate, up)):
+    for i, (target, keep) in enumerate(((down, keep_d), (gate, keep_g), (up, keep_u))):
         copies.got(side_in[i])
 
-        def write(n, carry, i=i, target=target):
-            target[pl.ds(side * half + n * 16, 16), :] = keep_f[i, pl.ds(n * 16, 16), mine].astype(f32)
+        def write(n, carry, i=i, target=target, keep=keep):
+            target[pl.ds(side * half + n * 16, 16), :] = keep[pl.ds(n * 16, 16), mine].astype(f32)
             target[pl.ds((1 - side) * half + n * 16, 16), :] = side_f[i, pl.ds(n * 16, 16), :].astype(f32)
             return carry
 
@@ -1044,8 +1064,8 @@
     copies.finish()
 
 
-def back_last(grad_q, rows_first, dres, inputs, gain, query_y, query_0, query_x,
-              sums, down_sums, out_sums, fparts, residual, gain_part, ident):
+def back_last(grad_q, dres, inputs, gain, query_0, query_y, query_x, query_xy, residual, gain_part,
+              rows_first, sums, down_sums, gate_sums, out_sums, fparts, ident):
     share, width = dres.shape
     hidden = sums.shape[1]
     blk = width // 8
@@ -1057,23 +1077,23 @@
         back_last_kernel,
         out_shape=(S((hidden, blk), f32),) * 3
         + (S((width // 4, blk), f32), S((blk, local), f32), S((share, width), f32), S((share, width), bf16),
-           S((2, width), f32), S((width, width), bf16)),
-        in_specs=[VM, ANY] + [VM] * 6 + [ANY] * 4 + [VM] * 2,
-        out_specs=(VM,) * 8 + (ANY,),
+           S((2, width), f32)),
+        in_specs=[VM] * 10 + [ANY] * 6,
+        out_specs=(VM,) * 8,
         scratch_shapes=[
-            V((3, hidden, 2 * blk), bf16), V((2, hidden, 2 * blk), bf16), V((3, half, 2 * blk), bf16),
-            V((3, half, blk), bf16),
+            V((half, 2 * blk), bf16), V((hidden, 2 * blk), bf16), V((hidden, 2 * blk), bf16), V((hidden, 2 * blk), bf16),
+            V((half, 2 * blk), bf16), V((half, 2 * blk), bf16), V((3, half, blk), bf16),
             V((width, width // 2), bf16), V((2, width, blk), bf16), V((width, blk), bf16),
             V((3, width // 4, blk), bf16),
             V((width // 2, local), bf16), V((width // 2, local), bf16), V((width // 2, local), bf16),
             V((2, blk, local), bf16), V((blk, local), bf16),
             V((share * 4, width), bf16), V((2, share // 2, width), bf16), V((2, share, width), bf16),
-            V((share, width), bf16), V((width, width), bf16), V((share, width), f32),
+            V((share, width), bf16), V((share * 4, width), bf16), V((4, blk, width), bf16), V((share, width), f32),
             V((2, width), f32), V((5, 2, width), f32),
             DMA((48,)), DMA((48,)), DMA((12,))],
         compiler_params=params(ident, 63 << 20), name="back_last",
-    )(grad_q, rows_first, dres, inputs, gain, query_y, query_0, query_x,
-      sums, down_sums, out_sums, fparts, residual, gain_part)
+    )(grad_q, dres, inputs, gain, query_0, query_y, query_x, query_xy, residual, gain_part,
+      rows_first, sums, down_sums, gate_sums, out_sums, fparts)
 
 
 def contract(left, right, left_dim, right_dim):
@@ -1293,23 +1313,19 @@
 
 def fast_body(inputs, keys_values, segment_ids, gain_first, gain_second, w_query, w_out, w_gate,
               w_up, w_down, cotangent):
-    starts = starts_of(segment_ids)
-    keys = keys_values[:, 0, :]
-    values = keys_values[:, 1, :]
     (rows_first, cots, gate_here, up_here, down_here, out_whole, queries, context_own, log_totals, residual,
-     normed_second, inputs_here, cot_here, gain_one, gain_two) = front_call(
+     normed_second, inputs_here, cot_here, gain_one, gain_two, keys, values, starts) = front_call(
         inputs, cotangent, gain_first[None], gain_second[None], w_query, w_out, w_gate.T, w_up.T, w_down,
-        keys, values, starts, 1)
+        keys_values, segment_ids, 1)
     grad_normed_second, query_0, query_y, ffn_parts, ffn_sums = ffn_call(
         normed_second, w_query, cots, down_here, gate_here, up_here, 3)
-    grad_residual, grad_context, gain_second_part, query_x, down_sums, out_sums = back_first(
-        grad_normed_second, residual, cot_here, gain_two, context_own, out_whole, ffn_sums, query_0, 5)
-    grad_queries, grad_keys, grad_values = attend_back(
-        starts, queries, keys, values, grad_context, log_totals)
-    grad_kv = jnp.stack([grad_keys, grad_values], axis=1)
-    down_shard, gate_shard, up_shard, out_shard, query_shard, grad_input, output, gains, _ = back_last(
-        grad_queries, rows_first, grad_residual, inputs_here, gain_one, query_y, query_0, query_x,
-        ffn_sums, down_sums, out_sums, ffn_parts, residual, gain_second_part, 6)
+    (grad_residual, gain_second_part, query_x, query_xy, grad_queries, grad_kv, down_sums, gate_sums,
+     out_sums) = back_first(
+        grad_normed_second, residual, cot_here, gain_two, context_own, queries, keys, values, log_totals, starts,
+        query_0, query_y, out_whole, ffn_sums, 5)
+    down_shard, gate_shard, up_shard, out_shard, query_shard, grad_input, output, gains = back_last(
+        grad_queries, grad_residual, inputs_here, gain_one, query_0, query_y, query_x, query_xy, residual,
+        gain_second_part, rows_first, ffn_sums, down_sums, gate_sums, out_sums, ffn_parts, 6)
     return (output, grad_input, grad_kv, gains[0], gains[1], query_shard, out_shard,
             gate_shard.T, up_shard.T, down_shard)
 

time: 592 us -> 541 us (0.914)
  Pallas kernels: 561 us -> 525 us
  local copies, waits for them, and re-layouts: 21.4 us -> 14.4 us
    pallas_call x1, Pallas kernels: 172 us -> 128 us  [back_last(): pl.pallas_call(back_last_kernel, out_shape=(S((hidden, blk), f32),) * 3 +...]
    pallas_call x2 -> x1, Pallas kernels: 54 us -> 75.4 us  [back_first(): pl.pallas_call(back_first_kernel, out_shape=(S((share, width), f32), S((1...]
    pallas_call x1, Pallas kernels: 231 us -> 224 us  [front_call(): pl.pallas_call(front_kernel, out_shape=(S((seq_len, width), bf16), S((seq...]
    pallas_call x1, Pallas kernels: 105 us -> 98.3 us  [ffn_call(): pl.pallas_call(ffn_kernel, out_shape=(jax.ShapeDtypeStruct((share, width)...]
    unnamed x24 -> x22, local copies, waits for them, and re-layouts: 13.2 us -> 12.9 us
where the time goes in v5:
time: 541 us; the launch traced here: 540 us
  Pallas kernels  525 us (97%)
  local copies, waits for them, and re-layouts  14.4 us (3%)
    pallas_call x1, Pallas kernels, front_call(): pl.pallas_call(front_kernel, out_shape=(S((seq_len, width), bf16), S((seq...  224 us
    pallas_call x1, Pallas kernels, back_last(): pl.pallas_call(back_last_kernel, out_shape=(S((hidden, blk), f32),) * 3 +...  128 us
    pallas_call x1, Pallas kernels, ffn_call(): pl.pallas_call(ffn_kernel, out_shape=(jax.ShapeDtypeStruct((share, width)...  98.3 us
    pallas_call x1, Pallas kernels, back_first(): pl.pallas_call(back_first_kernel, out_shape=(S((share, width), f32), S((1...  75.4 us
    unnamed x22, local copies, waits for them, and re-layouts  12.9 us

profile of v5, /device:TPU:0, one launch (start us, length us, event | category | flops | bytes accessed | tf_op | source)
XLA Modules:
  0.0 540.3 jit_solution(2520440604761803742)
XLA Ops:
  0.6 223.6 %front.1 = (bf16[1024,2048]{1,0:T(8,128)(2,1)}, bf16[1024,2048]{1,0:T(8,128)(2,1)}, bf16[1376,2048]{1,0:T(8,128)(2,1)}, bf16[1376,2048]{1,0:T(8,128)(2,1)}, bf16...) custom-call(bf16[256,2048]{1,0:T(8,128)(2,1)} %x.1, ...), custom_call_target="tpu_custom_call" | custom-call | tf_op jit(solution)/shard_map/front/pallas_call | solution.py:518
  224.2 98.3 %feed_forward.1 = (f32[256,2048]{1,0:T(8,128)}, bf16[256,2048]{1,0:T(8,128)(2,1)}, bf16[256,2048]{1,0:T(8,128)(2,1)}, bf16[1024,2048]{1,0:T(8,128)(2,1)}, bf16[3,1376,1024]{2,1,0:T(8,128)(2,1)}) custom-call(bf16[256,2048]{1,0:T(8,128)(2,1)} %get-tuple-element.50.normed, bf16[256,512]{1,0:T(8,128)(2,1)} %wq.3, bf16[1024,2048]{1,0:T(8,128)(2,1)} %get-tuple-element.51.cots_in, ...), custom_call_target="tpu_custom_call" | custom-call | flops 51942260736 | bytes 41943040 | tf_op jit(solution)/shard_map/feed_forward/pallas_call | solution.py:719
  322.6 75.4 %back_first.1 = (f32[256,2048]{1,0:T(8,128)}, f32[1,2048]{1,0:T(1,128)}, bf16[256,2048]{1,0:T(8,128)(2,1)}, bf16[256,2048]{1,0:T(8,128)(2,1)}, bf16[1024,512]{1,...) custom-call(f32[256,2048]{1,0:T(8,128)} %get-tuple-element.55.dn2, ...), custom_call_target="tpu_custom_call" | custom-call | tf_op jit(solution)/shard_map/back_first/pallas_call | solution.py:861
  398.0 127.9 %back_last.1 = (f32[1376,256]{1,0:T(8,128)}, f32[1376,256]{1,0:T(8,128)}, f32[1376,256]{1,0:T(8,128)}, f32[512,256]{1,0:T(8,128)}, f32[256,512]{1,0:T(8,128)}, /...) custom-call(bf16[1024,512]{1,0:T(8,128)(2,1)} %get-tuple-element.69.grad_q, ...), custom_call_target="tpu_custom_call" | custom-call | tf_op jit(solution)/shard_map/back_last/pallas_call | solution.py:1076
  525.8 0.0 copy-start.1
  525.8 1.5 fusion
  527.3 2.3 copy.29
  529.6 0.0 copy-done.1
  529.7 0.0 copy-start
  529.7 1.3 copy.30
  531.0 1.6 copy-done
  532.6 0.0 copy-start.6
  532.6 0.0 copy-start.5
  532.6 2.0 copy.31
  534.6 0.0 copy-done.6
  534.6 0.0 copy-start.4
  534.6 0.8 copy.32
  535.4 0.0 copy-done.5
  535.4 0.0 copy-start.3
  535.4 0.8 copy.33
  536.2 0.0 copy-done.4
  536.2 1.1 copy.34
  537.3 0.0 copy-done.3
  537.3 0.0 copy-start.2
  537.3 1.1 copy.35
  538.4 0.8 copy-done.2
  539.2 1.1 copy.36
Async XLA Ops:
  525.8 3.8 copy-start.1
  529.7 2.9 copy-start
  532.6 2.0 copy-start.6
  532.6 2.8 copy-start.5
  534.6 1.6 copy-start.4
  535.4 1.9 copy-start.3
  537.3 1.9 copy-start.2

commit v6 on v5

--- a/solution.py
+++ b/solution.py
@@ -87,6 +87,16 @@
         self.pending.append(item)
         return item
 
+    def prepare_jump(self, source, target, landing, distance, send_if, get_if):
+        slot = self.count
+        self.count += 1
+        place = self.place
+        device = (place.dp, jnp.clip(place.mp + distance, 0, 3))
+        item = {"copy": self.describe(source, target, device, slot), "got": False, "send_if": send_if,
+                "get_if": get_if, "get": self.describe(source, landing, device, slot)}
+        self.pending.append(item)
+        return item
+
     def start(self, item):
         if "send_if" in item:
             @pl.when(item["send_if"])
@@ -101,6 +111,8 @@
         return item
 
     def received(self, item):
+        if item["got"]:
+            return
         item["got"] = True
         if "get_if" in item:
             @pl.when(item["get_if"])
@@ -173,10 +185,13 @@
 
     def prepare(self):
         share, half = self.share, self.half
-        self.first = self.copies.prepare(self.parts.at[pl.ds(3 * share, half), :], self.relay.at[0], SIDE)
-        self.second = self.copies.prepare(self.parts.at[pl.ds(3 * share + half, half), :], self.relay.at[1], Z_LOW)
-        self.side = [self.copies.prepare(self.parts.at[pl.ds(share, half), :], self.landed.at[0, pl.ds(0, half), :], SIDE)]
-        self.low = [self.copies.prepare(self.parts.at[pl.ds(2 * share + half, half), :], self.landed.at[1, pl.ds(half, half), :], Z_LOW)]
+        prepare, parts, landed = self.copies.prepare, self.parts, self.landed
+        self.first = prepare(parts.at[pl.ds(3 * share, half), :], self.relay.at[0], SIDE)
+        self.second = prepare(parts.at[pl.ds(3 * share + half, half), :], self.relay.at[1], Z_LOW)
+        self.side = [prepare(parts.at[pl.ds(share, half), :], landed.at[0, pl.ds(0, half), :], SIDE),
+                     prepare(parts.at[pl.ds(share + half, half), :], landed.at[0, pl.ds(half, half), :], SIDE)]
+        self.low = [prepare(parts.at[pl.ds(2 * share + half, half), :], landed.at[1, pl.ds(half, half), :], Z_LOW),
+                    prepare(parts.at[pl.ds(2 * share, half), :], landed.at[1, pl.ds(0, half), :], Z_LOW)]
 
     def start_across(self):
         self.copies.start(self.first)
@@ -191,14 +206,19 @@
         self.start_across()
         self.start_rest()
 
+    def relayed_low(self):
+        self.copies.received(self.first)
+        add_into(self.parts, (2 * self.share, self.half), self.relay.at[0])
+        self.copies.start(self.low[1])
+
+    def relayed_side(self):
+        self.copies.received(self.second)
+        add_into(self.parts, (self.share + self.half, self.half), self.relay.at[1])
+        self.copies.start(self.side[1])
+
     def relayed(self):
-        share, half = self.share, self.half
-        self.copies.got(self.first)
-        add_into(self.parts, (2 * share, half), self.relay.at[0])
-        self.low.append(self.copies.swap(self.parts.at[pl.ds(2 * share, half), :], self.landed.at[1, pl.ds(0, half), :], Z_LOW))
-        self.copies.got(self.second)
-        add_into(self.parts, (share + half, half), self.relay.at[1])
-        self.side.append(self.copies.swap(self.parts.at[pl.ds(share + half, half), :], self.landed.at[0, pl.ds(half, half), :], SIDE))
+        self.relayed_low()
+        self.relayed_side()
 
     def arrived(self):
         for item in self.side + self.low:
@@ -222,21 +242,22 @@
     return jnp.where((key_pos >= starts) & (key_pos <= query_pos), s, -1e30)
 
 
-def attend_head(h, starts_ref, q_ref, k_ref, v_ref, ctx_ref, lse_ref):
+def attend_block(h, block, starts_ref, q_ref, k_ref, v_ref, ctx_ref, lse_ref):
     seq_len = q_ref.shape[0]
     scale = HEAD_DIM ** -0.5
+    window = min(seq_len, DOC_MOST + ROWS)
     lanes = pl.ds(pl.multiple_of(h * HEAD_DIM, HEAD_DIM), HEAD_DIM)
-    for block in range(seq_len // ROWS):
-        low, high = key_range(block, seq_len)
-        here = pl.ds(block * ROWS, ROWS)
-        keys_here = pl.ds(low, high - low)
-        s = scores_turned(q_ref[here, lanes], k_ref[keys_here, lanes], starts_ref[:, here], low, block * ROWS, scale)
-        top = jnp.max(s, axis=0, keepdims=True)
-        raised = jnp.exp(s - top)
-        total = jnp.sum(raised, axis=0, keepdims=True)
-        low_probs = (raised * (1.0 / total)).astype(bf16)
-        ctx_ref[here, lanes] = dot(low_probs, v_ref[keys_here, lanes], 0, 0).astype(bf16)
-        lse_ref[h, :, here] = top + jnp.log(total)
+    first = pl.multiple_of(block * ROWS, ROWS)
+    low = pl.multiple_of(jnp.clip(first - DOC_MOST, 0, seq_len - window), ROWS)
+    here = pl.ds(first, ROWS)
+    keys_here = pl.ds(low, window)
+    s = scores_turned(q_ref[here, lanes], k_ref[keys_here, lanes], starts_ref[:, here], low, first, scale)
+    top = jnp.max(s, axis=0, keepdims=True)
+    raised = jnp.exp(s - top)
+    total = jnp.sum(raised, axis=0, keepdims=True)
+    low_probs = (raised * (1.0 / total)).astype(bf16)
+    ctx_ref[here, lanes] = dot(low_probs, v_ref[keys_here, lanes], 0, 0).astype(bf16)
+    lse_ref[h, :, here] = top + jnp.log(total)
 
 
 def attend_head_back(h, starts_ref, q_ref, k_ref, v_ref, grad_ref, lse_ref, dq_ref, pair_ref, dk_ref, dv_ref):
@@ -272,6 +293,13 @@
     pair_ref[:, 1, lanes] = dv_ref[...]
 
 
+FRONT_ORDER = (
+    2, 21, 48, 18, 0, 1, 8, 11, 57, 35, 5, 3, 13, 33, 4, 20, 19, 17, 28, 27, 42, 26, 66, 9, 36, 64, 12, 24,
+    15, 6, 68, 67, 10, 34, 63, 29, 44, 23, 30, 14, 16, 73, 22, 50, 41, 37, 49, 54, 25, 46, 39, 65, 31, 56,
+    53, 75, 59, 7, 43, 55, 52, 38, 40, 70, 72, 45, 69, 51, 74, 60, 61, 71, 58, 76, 32, 62, 47, 77,
+)
+
+
 def front_kernel(x, cot, gain_one_in, gain_two_in, wq, wo, wg, wu, wd, pairs, segments,
                  rows_out, cots, gate, up, down, out_out, queries, context_own, lse, residual, normed,
                  x_here, cot_here, gain_one, gain_two, keys, values, starts,
@@ -314,198 +342,172 @@
             return (wo if source_is_input else target), target
         return get
 
-    store = {}
-
-    def line(step, block_of, key):
-        store[("r", key, step)] = copies.step(block_of, mp - (step - 1), mp - step, 1,
-                                              (mp >= step - 1) & (mp < 3), mp >= step)
-        store[("l", key, step)] = copies.step(block_of, mp + (step - 1), mp + step, -1,
-                                              (mp <= 3 - (step - 1)) & (mp > 0), mp <= 3 - step)
-
-    def arrive(key, step):
-        copies.got(store[("r", key, step)])
-        copies.got(store[("l", key, step)])
+    items = {}
+
+    def note(name, *copied):
+        items[name] = list(copied)
+
+    def line(step, block_of, name):
+        note(name,
+             copies.step(block_of, mp - (step - 1), mp - step, 1, (mp >= step - 1) & (mp < 3), mp >= step),
+             copies.step(block_of, mp + (step - 1), mp + step, -1, (mp <= 3 - (step - 1)) & (mp > 0), mp <= 3 - step))
 
     own_piece = [weight.at[pl.ds(side * half, half), :] for weight, _ in mats]
-    zhop = [[], [], []]
-    yhop = [[], [], []]
-
-    def send_z(i, source, spot):
-        zhop[i].append(copies.swap(source, tile(mats[i][1], 1, spot), Z_HIGH))
-
-    def send_y(i, source, z, spot):
-        yhop[i].append((copies.swap(source, tile(mats[i][1], z, spot + DEEPER), DEEP), z, spot + DEEPER))
-
-    def core_tile(i, z, spot, source=None):
-        piece = tile(mats[i][1], z, spot)
-        copies.swap(piece if source is None else source, tile(mats[i][1], z, spot + OTHER), CORE)
-
-    def core_query(spot, source=None):
-        return copies.swap(qrows(spot) if source is None else source, qrows(spot + OTHER), CORE)
-
-    def core_out(spot):
-        return copies.swap(columns(spot), columns(spot + OTHER), CORE)
-
-    greet(place, (1, 2, 3, CORE, SIDE, DEEP))
-    line(1, out_block(True), "o")
-    xhop = [copies.swap(weight.at[pl.ds((1 - side) * half, half), :], tile(whole, 0, own), SIDE)
-            for weight, whole in mats]
-    wq_y = copies.swap(wq, qrows(own + DEEPER), DEEP)
-    for i in range(3):
-        send_y(i, own_piece[i], 0, own)
-    wq_x = [copies.swap(wq, qrows(own), SIDE)]
-    wq_core = [core_query(own, wq)]
-
     spots = [pl.ds(pl.multiple_of(absolute(place, s) * blk, blk), blk) for s in range(8)]
-    for s in range(8):
-        gain_one[:, s * blk:(s + 1) * blk] = gain_one_in[:, spots[s]]
-        gain_two[:, s * blk:(s + 1) * blk] = gain_two_in[:, spots[s]]
-
-    def norm_first(i, carry):
-        here = pl.ds(i * 32, 32)
-        for s in range(8):
-            x_here[here, s * blk:(s + 1) * blk] = x[here, spots[s]]
-            cot_here[here, s * blk:(s + 1) * blk] = cot[here, spots[s]]
-        value = x_here[here, :].astype(f32)
-        inverse = lax.rsqrt(jnp.mean(value * value, axis=-1, keepdims=True) + epsilon)
-        first[here, :] = (value * inverse * gain_one[...]).astype(bf16)
-        return carry
-
-    lax.fori_loop(0, share // 32, norm_first, 0)
-    for c in range(2):
-        line(1, row_block(c, True), c)
-
-    def split(i, carry):
-        here = pl.ds(i * 32, 32)
-        both = pairs[here, :, :]
-        keys[here, :] = both[:, 0, :]
-        values[here, :] = both[:, 1, :]
-        return carry
-
-    lax.fori_loop(0, pairs.shape[0] // 32, split, 0)
-    ids = segments[...]
-    begun = jnp.zeros_like(ids)
-    for document in range(DOCS - 1):
-        size = jnp.sum((ids == document).astype(jnp.int32), axis=1, keepdims=True)
-        begun = begun + jnp.where(ids > document, size, 0)
-    starts[...] = begun
-    rows[pl.ds(mp * share, share), :] = first[...]
-    query[pl.ds(own * blk, blk), :] = wq[...]
-    out[pl.ds(mp * zrow, zrow), pl.ds(pl.multiple_of(own * blk, blk), blk)] = wo[...]
-    locals_.append(copies.local(cot_here, cots.at[0:share, :]))
-    for i in range(3):
-        locals_.append(copies.local(own_piece[i], tile(mats[i][1], 0, own)))
-        core_tile(i, 0, own, own_piece[i])
-    copies.got(wq_y)
-    wq_x.append(copies.swap(qrows(own + DEEPER), qrows(own + DEEPER), SIDE))
-    wq_core.append(core_query(own + DEEPER))
-    arrive("o", 1)
-    line(2, out_block(False), "o")
-    for i in range(3):
-        copies.got(xhop[i])
-        piece = tile(mats[i][1], 0, across)
-        send_y(i, piece, 0, across)
-        core_tile(i, 0, across)
-    for c in range(2):
-        arrive(c, 1)
-        line(2, row_block(c, False), c)
-    for i in range(3):
-        send_z(i, own_piece[i], own)
-    for item, spot in zip(wq_x, (across, across + DEEPER)):
-        copies.got(item)
-        wq_core.append(core_query(spot))
-    cot_x = copies.swap(cot_here, cots.at[share:2 * share, :], SIDE)
-    arrive("o", 2)
-    line(3, out_block(False), "o")
-    for c in range(2):
-        arrive(c, 2)
-        line(3, row_block(c, False), c)
-    cot_z = copies.swap(cot_here, cots.at[2 * share:3 * share, :], Z_LOW)
-    arrive("o", 3)
-    out_y = copies.swap(columns(own), columns(own + DEEPER), DEEP)
-    out_x = [copies.swap(columns(own), columns(own), SIDE)]
-    out_core = [core_out(own)]
-
-    def across_z(i):
-        copies.got(zhop[i][0])
-        send_y(i, tile(mats[i][1], 1, own), 1, own)
-        core_tile(i, 1, own)
-
-    across_z(0)
-    for copy in locals_:
-        copy.wait()
-    for item in wq_core:
-        copies.got(item)
-    for c in range(2):
-        arrive(c, 3)
-    save_rows = copies.local(rows, rows_out)
-
-    def project(m, carry):
+    inside = lambda m: (m >= 0) & (m <= 3)
+
+    def context_jump(distance):
+        source = context.at[pl.ds(jnp.clip(mp + distance, 0, 3) * share, share), :]
+
+        def landing(m):
+            return context_own.at[:, pl.ds(pl.multiple_of(jnp.clip(m, 0, 3) * local, local), local)]
+
+        return copies.prepare_jump(source, landing(mp), landing(mp - distance), distance,
+                                   inside(mp + distance), inside(mp - distance))
+
+    jumps = {distance: context_jump(distance) for distance in (1, -1, 2, -2, 3, -3)}
+
+    def attend_tokens(m):
         here = pl.ds(pl.multiple_of(m * share, share), share)
         queries[here, :] = dot(rows[here, :], query[...], 1, 0).astype(bf16)
-        return carry
-
-    lax.fori_loop(0, 4, project, 0)
-
-    def one_head(h, carry):
-        attend_head(h, starts, queries, keys, values, context, lse)
-        return carry
-
-    lax.fori_loop(0, local // HEAD_DIM, one_head, 0)
-    tokens_in = []
-    for mask in (2, 3, 1):
-        other = place.partner(mask)[1]
-        tokens_in.append(copies.swap(context.at[pl.ds(other * share, share), :],
-                                     context_own.at[:, pl.ds(mp * local, local)], mask))
-    context_own[:, pl.ds(pl.multiple_of(mp * local, local), local)] = context[pl.ds(mp * share, share), :]
-    for i in range(3):
-        send_z(i, tile(mats[i][1], 0, across), across)
-    across_z(1)
-    across_z(2)
-    copies.got(out_y)
-    out_x.append(copies.swap(columns(own + DEEPER), columns(own + DEEPER), SIDE))
-    out_core.append(core_out(own + DEEPER))
-    copies.got(out_x[0])
-    out_core.append(core_out(across))
-    copies.got(cot_z)
-    copies.swap(cots.at[2 * share:3 * share, :], cots.at[3 * share:4 * share, :], SIDE)
-    for j in range(2):
+
+        def one_head(h, carry):
+            attend_block(h, m, starts, queries, keys, values, context, lse)
+            return carry
+
+        lax.fori_loop(0, local // HEAD_DIM, one_head, 0)
+
+    def attend_from(distance):
+        for away in (distance, -distance):
+            @pl.when(inside(mp + away))
+            def _(away=away):
+                attend_tokens(mp + away)
+                jumps[away]["copy"].start()
+        note("A%d" % distance, jumps[distance], jumps[-distance])
+
+    def norm_rows():
+        for s in range(8):
+            gain_one[:, s * blk:(s + 1) * blk] = gain_one_in[:, spots[s]]
+            gain_two[:, s * blk:(s + 1) * blk] = gain_two_in[:, spots[s]]
+
+        def norm_first(i, carry):
+            here = pl.ds(i * 32, 32)
+            for s in range(8):
+                x_here[here, s * blk:(s + 1) * blk] = x[here, spots[s]]
+                cot_here[here, s * blk:(s + 1) * blk] = cot[here, spots[s]]
+            value = x_here[here, :].astype(f32)
+            inverse = lax.rsqrt(jnp.mean(value * value, axis=-1, keepdims=True) + epsilon)
+            first[here, :] = (value * inverse * gain_one[...]).astype(bf16)
+            return carry
+
+        lax.fori_loop(0, share // 32, norm_first, 0)
+        rows[pl.ds(mp * share, share), :] = first[...]
+
+    def split_pairs():
+        def split(i, carry):
+            here = pl.ds(i * 32, 32)
+            both = pairs[here, :, :]
+            keys[here, :] = both[:, 0, :]
+            values[here, :] = both[:, 1, :]
+            return carry
+
+        lax.fori_loop(0, pairs.shape[0] // 32, split, 0)
+        ids = segments[...]
+        begun = jnp.zeros_like(ids)
+        for document in range(DOCS - 1):
+            size = jnp.sum((ids == document).astype(jnp.int32), axis=1, keepdims=True)
+            begun = begun + jnp.where(ids > document, size, 0)
+        starts[...] = begun
+        query[pl.ds(own * blk, blk), :] = wq[...]
+        out[pl.ds(mp * zrow, zrow), pl.ds(pl.multiple_of(own * blk, blk), blk)] = wo[...]
+        locals_.append(copies.local(cot_here, cots.at[0:share, :]))
         for i in range(3):
-            item, z, spot = yhop[i][j]
-            copies.got(item)
-            core_tile(i, z, spot)
-    copies.got(out_x[1])
-    out_core.append(core_out(across + DEEPER))
-    for item in out_core + tokens_in:
-        copies.got(item)
-    save_out = copies.local(out, out_out)
-
-    def project_out(n, carry):
-        there = pl.ds(pl.multiple_of(n * 512, 512), 512)
-        residual[:, there] = x_here[:, there].astype(f32) + dot(context_own[...], out[:, there], 1, 0)
-        return carry
-
-    lax.fori_loop(0, width // 512, project_out, 0)
-
-    def norm_second(i, carry):
-        here = pl.ds(i * 32, 32)
-        value = residual[here, :]
-        inverse = lax.rsqrt(jnp.mean(value * value, axis=-1, keepdims=True) + epsilon)
-        normed[here, :] = (value * inverse * gain_two[...]).astype(bf16)
-        return carry
-
-    lax.fori_loop(0, share // 32, norm_second, 0)
-    for i in range(3):
-        copies.got(zhop[i][1])
-        send_y(i, tile(mats[i][1], 1, across), 1, across)
-        core_tile(i, 1, across)
-    for j in (2, 3):
-        for i in range(3):
-            item, z, spot = yhop[i][j]
-            copies.got(item)
-            core_tile(i, z, spot)
-    save_rows.wait()
-    save_out.wait()
+            locals_.append(copies.local(own_piece[i], tile(mats[i][1], 0, own)))
+
+    def send(name, source, target, mask):
+        note(name, copies.swap(source, target, mask))
+
+    tasks = {}
+
+    def task(name, needs, action, *arguments):
+        tasks[name] = (needs, lambda: action(*arguments))
+
+    def copy(name, needs, source, target, mask):
+        task(name, needs, send, name, source, target, mask)
+
+    task("N", (), norm_rows)
+    task("S", ("N",), split_pairs)
+    task("o1", (), line, 1, out_block(True), "o1")
+    task("o2", ("o1",), line, 2, out_block(False), "o2")
+    task("o3", ("o2", "S"), line, 3, out_block(False), "o3")
+    for c in range(2):
+        task("n1%d" % c, ("N",), line, 1, row_block(c, True), "n1%d" % c)
+        task("n2%d" % c, ("n1%d" % c,), line, 2, row_block(c, False), "n2%d" % c)
+        task("n3%d" % c, ("n2%d" % c,), line, 3, row_block(c, False), "n3%d" % c)
+    copy("qy", (), wq, qrows(own + DEEPER), DEEP)
+    copy("qx", (), wq, qrows(own), SIDE)
+    copy("qyx", ("qy",), qrows(own + DEEPER), qrows(own + DEEPER), SIDE)
+    copy("q", (), wq, qrows(own + OTHER), CORE)
+    for name, spot in (("qy", own + DEEPER), ("qx", across), ("qyx", across + DEEPER)):
+        copy(name + "C", (name,), qrows(spot), qrows(spot + OTHER), CORE)
+    for i, (weight, whole) in enumerate(mats):
+        n = "%d" % i
+        copy("x" + n, (), weight.at[pl.ds((1 - side) * half, half), :], tile(whole, 0, own), SIDE)
+        for kind, needs, source, z, spot in (
+                ("O", (), own_piece[i], 0, own), ("X", ("x" + n,), tile(whole, 0, across), 0, across)):
+            copy("z" + kind + n, needs, source, tile(whole, 1, spot), Z_HIGH)
+            for far, far_needs, far_source, row in (("", needs, source, 0), ("z", ("z" + kind + n,), tile(whole, 1, spot), 1)):
+                name = far + kind + n
+                copy("y" + name, far_needs, far_source, tile(whole, row, spot + DEEPER), DEEP)
+                copy("c" + name, far_needs, far_source, tile(whole, row, spot + OTHER), CORE)
+                copy("yc" + name, ("y" + name,), tile(whole, row, spot + DEEPER), tile(whole, row, spot + DEEPER + OTHER), CORE)
+    copy("cx", ("N",), cot_here, cots.at[share:2 * share, :], SIDE)
+    copy("cz", ("N",), cot_here, cots.at[2 * share:3 * share, :], Z_LOW)
+    copy("czx", ("cz",), cots.at[2 * share:3 * share, :], cots.at[3 * share:4 * share, :], SIDE)
+    copy("oy", ("o3",), columns(own), columns(own + DEEPER), DEEP)
+    copy("ox", ("o3",), columns(own), columns(own), SIDE)
+    copy("oyx", ("oy",), columns(own + DEEPER), columns(own + DEEPER), SIDE)
+    for name, needs, spot in (("o", "o3", own), ("oy", "oy", own + DEEPER), ("ox", "ox", across), ("oyx", "oyx", across + DEEPER)):
+        copy(name + "C", (needs,), columns(spot), columns(spot + OTHER), CORE)
+    whole_query = ("q", "qyC", "qxC", "qyxC", "S")
+    task("A0", whole_query, attend_tokens, mp)
+    for distance in (1, 2, 3):
+        task("A%d" % distance, ("A0", "n%d0" % distance, "n%d1" % distance), attend_from, distance)
+
+    def finish_tokens():
+        context_own[:, pl.ds(pl.multiple_of(mp * local, local), local)] = context[pl.ds(mp * share, share), :]
+        locals_.append(copies.local(rows, rows_out))
+        locals_.append(copies.local(out, out_out))
+
+        def project_out(n, carry):
+            there = pl.ds(pl.multiple_of(n * 512, 512), 512)
+            residual[:, there] = x_here[:, there].astype(f32) + dot(context_own[...], out[:, there], 1, 0)
+            return carry
+
+        lax.fori_loop(0, width // 512, project_out, 0)
+
+        def norm_second(i, carry):
+            here = pl.ds(i * 32, 32)
+            value = residual[here, :]
+            inverse = lax.rsqrt(jnp.mean(value * value, axis=-1, keepdims=True) + epsilon)
+            normed[here, :] = (value * inverse * gain_two[...]).astype(bf16)
+            return carry
+
+        lax.fori_loop(0, share // 32, norm_second, 0)
+
+    task("F", ("A3", "oC", "oyC", "oxC", "oyxC", "A1", "A2"), finish_tokens)
+
+    greet(place, (1, 2, 3, CORE, SIDE, DEEP))
+    names = list(tasks)
+    for index in FRONT_ORDER or range(len(names)):
+        needs, action = tasks.pop(names[index])
+        for need in needs:
+            for item in items.get(need, ()):
+                copies.got(item)
+        action()
+    assert not tasks
+    for local_copy in locals_:
+        local_copy.wait()
     copies.finish()
 
 
@@ -582,11 +584,11 @@
             copies.prepare_step(block_of, mp + (hop - 1), mp + hop, -1,
                                 (mp <= 3 - (hop - 1)) & (mp > 0), mp <= 3 - hop)))
     over_deep = copies.prepare(query_0, query_y, DEEP)
-    query_0[:, pl.ds(pl.multiple_of(mp * local, local), local)] = wq[...]
     for item in hops[0]:
         copies.start(item)
-
-    def block(r):
+    query_0[:, pl.ds(pl.multiple_of(mp * local, local), local)] = wq[...]
+
+    def block(r, between):
         here = pl.ds(r * share, share)
         for start, size in cuts:
             rows = tokens[1, here, :]
@@ -600,6 +602,8 @@
                 grad * up * sigmoid * (1.0 + gate * (1.0 - sigmoid))).astype(bf16)
             acts[2, here, start:start + size] = (grad * silu).astype(bf16)
 
+        between()
+
         def columns(n, carry):
             there = pl.ds(pl.multiple_of(n * 512, 512), 512)
             dparts[here, there] = (dot(acts[1, here, :], weights[1, :, there], 1, 0)
@@ -613,6 +617,14 @@
         copy.wait()
     load_cots.wait()
     got = {"across": None}
+
+    def pass_on(r, turn, landed_hop, next_hop):
+        @pl.when(r == turn)
+        def _():
+            for item in landed_hop:
+                copies.received(item)
+            for item in next_hop:
+                copies.start(item)
 
     def step(r, carry):
         @pl.when(r == 1)
@@ -621,30 +633,21 @@
             side_b["copy"].wait_recv()
             forward[0].start()
             forward[1].start()
-            for item in hops[0]:
-                copies.received(item)
-            for item in hops[1]:
-                copies.start(item)
             side_a["copy"].wait_recv()
             low_b["copy"].wait_recv()
 
         @pl.when(r == 2)
         def _():
-            for item in hops[1]:
-                copies.received(item)
-            for item in hops[2]:
-                copies.start(item)
-
             forward[0].wait_recv()
             forward[1].wait_recv()
 
+        pass_on(r, 2, hops[0], hops[1])
+        pass_on(r, 3, hops[2], (over_deep,))
+
         @pl.when(r == 3)
         def _():
-            for item in hops[2]:
-                copies.received(item)
-            copies.start(over_deep)
             reduce.start_across()
-        block(jnp.where(r < 2, r, 5 - r))
+        block(jnp.where(r < 2, r, 5 - r), lambda: pass_on(r, 2, hops[1], hops[2]))
         return carry
 
     reduce = QuadReduce(copies, dparts, relay, landed)
@@ -677,9 +680,16 @@
         def _():
             pl.semaphore_wait(free_sem, 1)
         give_copy(i).start()
+
+        @pl.when(i == 0)
+        def _():
+            reduce.relayed_low()
+
+        @pl.when(i == 1)
+        def _():
+            reduce.relayed_side()
         return carry
 
-    reduce.relayed()
     lax.fori_loop(0, 3, give, 0)
 
     def keep(i, carry):
@@ -751,10 +761,10 @@
     copies = Copies(place, send_sems, recv_sems, local_sems)
     loads = [copies.local(out_whole.at[pl.ds(z * local, local), :], wout.at[z]) for z in range(4)]
     load_d = copies.local(sums.at[0, :, pl.ds(0, quarter)], keep_d)
-    load_g = copies.local(sums.at[1, :, pl.ds(0, quarter)], gate_sums)
+    load_g = copies.local(sums.at[1, :, pl.ds(0, blk)], gate_sums)
     greet(place, (1, 2, 3, CORE, SIDE, DEEP))
-    in_d, in_g = ([copies.swap(sums.at[i, :, pl.ds(quarter + x * blk, blk)], target.at[:, pl.ds(x * blk, blk)], DEEP)
-                   for x in (0, 1)] for i, target in ((0, deep_d), (1, deep_g)))
+    in_d = [copies.swap(sums.at[0, :, pl.ds(quarter + x * blk, blk)], deep_d.at[:, pl.ds(x * blk, blk)], DEEP)
+            for x in (0, 1)]
     copies.swap(query_0, query_x, SIDE)
     copies.swap(query_y, query_xy, SIDE)
     gain_part[...] = jnp.zeros_like(gain_part)
@@ -810,6 +820,7 @@
         return carry
 
     lax.fori_loop(0, chunks, keep, 0)
+    in_g = copies.swap(sums.at[1, :, pl.ds(quarter, blk)], deep_g, DEEP)
     load_d.wait()
     give_rows = pl.ds(half, half)
     across = []
@@ -828,8 +839,7 @@
 
     lax.fori_loop(0, local // HEAD_DIM, one_head, 0)
     load_g.wait()
-    for x in (0, 1):
-        copies.got(in_g[x])
+    copies.got(in_g)
     add_into(gate_sums, (0, hidden), deep_g)
     for x in (0, 1):
         copies.got(across[x])
@@ -862,12 +872,12 @@
         back_first_kernel,
         out_shape=(S((share, width), f32), S((1, width), f32), S(query_0.shape, bf16), S(query_0.shape, bf16),
                    S((seq_len, local), bf16), S((seq_len, 2, local), f32),
-                   S((half, quarter), bf16), S((hidden, quarter), bf16), S((width, width // 2), bf16)),
+                   S((half, quarter), bf16), S((hidden, quarter // 2), bf16), S((width, width // 2), bf16)),
         in_specs=[VM] * 12 + [ANY, ANY],
         out_specs=(VM,) * 9,
         scratch_shapes=[
             V((seq_len, local), bf16), V((hidden, quarter), bf16), V((hidden, quarter), bf16), V((half, quarter), bf16),
-            V((hidden, quarter), bf16), V((share, width), bf16),
+            V((hidden, quarter // 2), bf16), V((share, width), bf16),
             V((4, width // 4, width), bf16), V((share, width), bf16), V((width, width // 2), bf16),
             V((width, width // 2), bf16), V((seq_len, HEAD_DIM), f32), V((seq_len, HEAD_DIM), f32),
             DMA((20,)), DMA((20,)), DMA((6,))],
@@ -875,10 +885,16 @@
     )(dn2, residual, cot, gain, context, queries, keys, values, lse, starts, query_0, query_y, out_whole, sums)
 
 
+BACK_ORDER = (
+    3, 0, 10, 5, 9, 7, 12, 17, 4, 6, 1, 13, 22, 2, 14, 15, 18, 19, 21, 11, 8, 16, 24, 23, 28, 34, 25, 26,
+    27, 20, 30, 31, 32, 36, 29, 35, 33,
+)
+
+
 def back_last_kernel(grad_q, dres, inputs, gain, query_0, query_y, query_x, query_xy, residual, gain_part,
                      rows_first, sums, down_sums, gate_sums, out_sums, fparts,
                      down, gate, up, out, query, grad_input, output, gains,
-                     keep_d, keep_g, keep_u, deep_u, high_g, high_u, side_f,
+                     keep_d, keep_g, keep_u, deep_g, deep_u, high_g, high_u, side_f,
                      own_o, deep_o, side_o, z_o,
                      give_q, own_q, core_q, side_q, deep_q, parts, relay, landed,
                      grad_own, rows, query_far, dn1, gain_rows, gains_got,
@@ -895,172 +911,246 @@
     wide = width // 2
     copies = Copies(place, send_sems, recv_sems, local_sems)
     load_rows = copies.local(rows_first, rows)
-    load_g = copies.local(gate_sums, keep_g)
+    load_g = copies.local(gate_sums, keep_g.at[:, pl.ds(0, blk)])
+    load_h = copies.local(sums.at[1, :, pl.ds(blk, blk)], keep_g.at[:, pl.ds(blk, blk)])
     load_d = copies.local(down_sums, keep_d)
     load_o = copies.local(out_sums, own_o)
     load_u = copies.local(sums.at[2, :, pl.ds(0, quarter)], keep_u)
     load_p = copies.local(fparts, parts)
-    greet(place, (1, 2, 3, CORE, SIDE, DEEP))
-    tokens_in = []
-    for mask in (2, 3, 1):
-        other = place.partner(mask)[1]
-        tokens_in.append(copies.swap(grad_q.at[pl.ds(other * share, share), :],
-                                     grad_own.at[:, pl.ds(mp * local, local)], mask))
-    in_u = [copies.swap(sums.at[2, :, pl.ds(quarter + x * blk, blk)], deep_u.at[:, pl.ds(x * blk, blk)], DEEP)
-            for x in (0, 1)]
     near = (query_0, query_y, query_x, query_xy)
-    far_in = [copies.swap(piece, query_far.at[n], CORE) for n, piece in enumerate(near)]
+    spot_of = (side, side + 2, 1 - side, 3 - side)
     give_rows = pl.ds(half, half)
     mine = pl.ds(pl.multiple_of(side * blk, blk), blk)
     theirs = pl.ds(pl.multiple_of((1 - side) * blk, blk), blk)
-    load_g.wait()
-    high_in_g = [copies.swap(keep_g.at[give_rows, pl.ds(x * blk, blk)], high_g.at[:, pl.ds(x * blk, blk)], Z_HIGH)
-                 for x in (0, 1)]
-    load_d.wait()
-    side_in = [copies.swap(keep_d.at[:, theirs], side_f.at[0], SIDE)]
-    load_o.wait()
+    spots = [pl.ds(pl.multiple_of(absolute(place, s) * blk, blk), blk) for s in range(8)]
+    reduce = QuadReduce(copies, parts, relay, landed)
+    items = {}
+    tasks = {}
+    loaded = set()
+
+    def note(name, *copied):
+        items[name] = list(copied)
+
+    def task(name, needs, action, *arguments):
+        tasks[name] = (needs, lambda: action(*arguments))
+
+    def ready(name, *loads):
+        if name not in loaded:
+            loaded.add(name)
+            for load in loads:
+                load.wait()
 
     def block_o(deep, column):
         return own_o.at[:, pl.ds(pl.multiple_of((2 * deep + column) * blk, blk), blk)]
 
-    deep_in_o = {column: copies.swap(block_o(1, x), deep_o.at[n], DEEP)
-                 for n, (column, x) in enumerate((("theirs", 1 - side), ("mine", side)))}
-    grad_own[:, pl.ds(pl.multiple_of(mp * local, local), local)] = grad_q[pl.ds(mp * share, share), :]
-    load_rows.wait()
+    def rows_q(deep, column):
+        return pl.ds(pl.multiple_of((2 * deep + column) * blk, blk), blk)
+
+    def send_tokens():
+        sent = []
+        for mask in (2, 3, 1):
+            other = place.partner(mask)[1]
+            sent.append(copies.swap(grad_q.at[pl.ds(other * share, share), :],
+                                    grad_own.at[:, pl.ds(mp * local, local)], mask))
+        note("dq", *sent)
+        grad_own[:, pl.ds(pl.multiple_of(mp * local, local), local)] = grad_q[pl.ds(mp * share, share), :]
+
+    def send_up(x):
+        note("u%d" % x, copies.swap(sums.at[2, :, pl.ds(quarter + x * blk, blk)], deep_u.at[:, pl.ds(x * blk, blk)], DEEP))
+
+    def send_near():
+        note("f", *[copies.swap(piece, query_far.at[n], CORE) for n, piece in enumerate(near)])
+
+    def send_gate():
+        ready("g", load_g)
+        there = pl.ds(0, blk)
+        note("zg0", copies.swap(keep_g.at[give_rows, there], high_g.at[:, there], Z_HIGH))
+
+    def send_gate_deep():
+        note("g1", copies.swap(sums.at[1, :, pl.ds(quarter + blk, blk)], deep_g, DEEP))
+
+    def gate_sum():
+        ready("h", load_h)
+        there = pl.ds(blk, blk)
+        add_into(keep_g.at[:, there], (half, half), deep_g.at[give_rows, :], step=16)
+        note("zg1", copies.swap(keep_g.at[give_rows, there], high_g.at[:, there], Z_HIGH))
+        add_into(keep_g.at[:, there], (0, half), deep_g, step=16)
+
+    def send_down():
+        ready("d", load_d)
+        note("xd", copies.swap(keep_d.at[:, theirs], side_f.at[0], SIDE))
+
+    def send_out(name, n, x):
+        ready("o", load_o)
+        note(name, copies.swap(block_o(1, x), deep_o.at[n], DEEP))
 
     def product(first):
+        ready("w", load_rows)
         return dot(rows[:, first:first + wide], grad_q[...], 0, 0)
 
-    give_q[...] = product(wide).astype(bf16)
-    core_in_q = copies.swap(give_q, core_q, CORE)
-    load_p.wait()
-    reduce = QuadReduce(copies, parts, relay, landed)
-    reduce.start()
-    keep_q = product(0)
-    copies.got(core_in_q)
-    own_q[...] = (keep_q + core_q[...].astype(f32)).astype(bf16)
-    side_in_q = {y: copies.swap(own_q.at[pl.ds((2 * y + 1 - side) * blk, blk), :], side_q.at[y], SIDE) for y in (1, 0)}
-    for item in far_in:
-        copies.got(item)
-    for item in tokens_in:
-        copies.got(item)
-    spot_of = (side, side + 2, 1 - side, 3 - side)
-    for n in range(4):
-        dn1[:, pl.ds(pl.multiple_of(spot_of[n] * blk, blk), blk)] = dot(grad_own[...], near[n][...], 1, 1)
-        dn1[:, pl.ds(pl.multiple_of((spot_of[n] + 4) * blk, blk), blk)] = dot(grad_own[...], query_far[n], 1, 1)
-    gain_rows[0:1, :] = jnp.zeros((1, width), f32)
-    gain_rows[1:2, :] = gain_part[...]
-    spots = [pl.ds(pl.multiple_of(absolute(place, s) * blk, blk), blk) for s in range(8)]
-
-    def norm(i, carry):
-        here = pl.ds(i * 32, 32)
-        value = inputs[here, :].astype(f32)
-        inverse = lax.rsqrt(jnp.mean(value * value, axis=-1, keepdims=True) + epsilon)
-        scaled = value * inverse
-        grad = dn1[here, :]
-        grad_scaled = grad * gain[...]
-        back = inverse * (grad_scaled - scaled * jnp.mean(grad_scaled * scaled, axis=-1, keepdims=True))
-        total = dres[here, :] + back
+    def query_give():
+        give_q[...] = product(wide).astype(bf16)
+        note("qc", copies.swap(give_q, core_q, CORE))
+
+    def query_keep():
+        own_q[...] = (product(0) + core_q[...].astype(f32)).astype(bf16)
+        for y in (1, 0):
+            note("qs%d" % y, copies.swap(own_q.at[rows_q(y, 1 - side), :], side_q.at[y], SIDE))
+
+    def query_side(y):
+        here = rows_q(y, side)
+        own_q[here, :] = (own_q[here, :].astype(f32) + side_q[y].astype(f32)).astype(bf16)
+        if y:
+            note("qd", copies.swap(own_q.at[here, :], deep_q, DEEP))
+
+    def query_done():
+        query[...] = own_q[rows_q(0, side), :].astype(f32) + deep_q[...].astype(f32)
+
+    def reduce_start():
+        ready("p", load_p)
+        reduce.start()
+        note("r1", reduce.first, reduce.second)
+
+    def first_product():
+        for n in range(4):
+            dn1[:, pl.ds(pl.multiple_of(spot_of[n] * blk, blk), blk)] = dot(grad_own[...], near[n][...], 1, 1)
+            dn1[:, pl.ds(pl.multiple_of((spot_of[n] + 4) * blk, blk), blk)] = dot(grad_own[...], query_far[n], 1, 1)
+
+    def first_norm():
+        gain_rows[0:1, :] = jnp.zeros((1, width), f32)
+        gain_rows[1:2, :] = gain_part[...]
+
+        def norm(i, carry):
+            here = pl.ds(i * 32, 32)
+            value = inputs[here, :].astype(f32)
+            inverse = lax.rsqrt(jnp.mean(value * value, axis=-1, keepdims=True) + epsilon)
+            scaled = value * inverse
+            grad = dn1[here, :]
+            grad_scaled = grad * gain[...]
+            back = inverse * (grad_scaled - scaled * jnp.mean(grad_scaled * scaled, axis=-1, keepdims=True))
+            total = dres[here, :] + back
+            for s in range(8):
+                grad_input[here, spots[s]] = total[:, s * blk:(s + 1) * blk]
+            gain_rows[0:1, :] += jnp.sum(grad * scaled, axis=0, keepdims=True)
+            return carry
+
+        lax.fori_loop(0, share // 32, norm, 0)
         for s in range(8):
-            grad_input[here, spots[s]] = total[:, s * blk:(s + 1) * blk]
-        gain_rows[0:1, :] += jnp.sum(grad * scaled, axis=0, keepdims=True)
-        return carry
-
-    lax.fori_loop(0, share // 32, norm, 0)
-    for s in range(8):
-        gains[:, spots[s]] = gain_rows[:, s * blk:(s + 1) * blk]
+            gains[:, spots[s]] = gain_rows[:, s * blk:(s + 1) * blk]
+
     gain_masks = (1, 2, CORE, SIDE, DEEP)
-    gain_state = {"item": None, "at": 0}
-
-    def gain_hop():
-        if gain_state["item"] is not None:
-            item = gain_state["item"]
-            copies.got(item)
+
+    def gain_hop(n):
+        if n:
+            item = items["h%d" % (n - 1)][0]
             item["copy"].wait_send()
             item["sent"] = True
-            gains[...] = gains[...] + gains_got[gain_state["at"] - 1]
-            gain_state["item"] = None
-        if gain_state["at"] < len(gain_masks):
-            gain_state["item"] = copies.swap(gains, gains_got.at[gain_state["at"]], gain_masks[gain_state["at"]])
-            gain_state["at"] += 1
-
-    gain_hop()
-    load_u.wait()
-    high_in_u = []
-    for x in (0, 1):
+            gains[...] = gains[...] + gains_got[n - 1]
+        if n < len(gain_masks):
+            note("h%d" % n, copies.swap(gains, gains_got.at[n], gain_masks[n]))
+
+    def up_sum(x):
+        ready("u", load_u)
         there = pl.ds(x * blk, blk)
-        copies.got(in_u[x])
         add_into(keep_u.at[:, there], (half, half), deep_u.at[give_rows, there], step=16)
-        high_in_u.append(copies.swap(keep_u.at[give_rows, there], high_u.at[:, there], Z_HIGH))
+        note("zu%d" % x, copies.swap(keep_u.at[give_rows, there], high_u.at[:, there], Z_HIGH))
         add_into(keep_u.at[:, there], (0, half), deep_u.at[:, there], step=16)
-    reduce.relayed()
-    gain_hop()
-
-    def high_sum(keep, high, items, i):
-        for x in (0, 1):
-            copies.got(items[x])
+
+    def high_sum(name, keep, high, i):
         add_into(keep.at[:, theirs], (0, half), high.at[:, theirs], step=16)
-        side_in.append(copies.swap(keep.at[pl.ds(0, half), theirs], side_f.at[i], SIDE))
+        note(name, copies.swap(keep.at[pl.ds(0, half), theirs], side_f.at[i], SIDE))
         add_into(keep.at[:, mine], (0, half), high.at[:, mine], step=16)
 
-    deep_in_q = None
-    for y in (1, 0):
-        copies.got(side_in_q[y])
-        here = pl.ds(pl.multiple_of((2 * y + side) * blk, blk), blk)
-        own_q[here, :] = (own_q[here, :].astype(f32) + side_q[y].astype(f32)).astype(bf16)
-        if y:
-            deep_in_q = copies.swap(own_q.at[here, :], deep_q, DEEP)
-    copies.got(deep_in_o["theirs"])
-    add_into(block_o(0, 1 - side), (0, width), deep_o.at[0])
-    side_in_o = copies.swap(block_o(0, 1 - side), side_o, SIDE)
-    gain_hop()
-    high_sum(keep_g, high_g, high_in_g, 1)
-    gain_hop()
-    copies.got(deep_in_o["mine"])
-    add_into(block_o(0, side), (0, width), deep_o.at[1])
-    gain_hop()
-    reduce.arrived()
-
-    def finish_output(i, carry):
-        here = pl.ds(i * 32, 32)
-        total = (residual[here, :] + parts[here, :].astype(f32) + landed[0, here, :].astype(f32)
-                 + landed[1, here, :].astype(f32)).astype(bf16)
-        for s in range(8):
-            output[here, spots[s]] = total[:, s * blk:(s + 1) * blk]
-        return carry
-
-    lax.fori_loop(0, share // 32, finish_output, 0)
-    gain_hop()
-    copies.got(side_in_o)
-    add_into(block_o(0, side), (0, width), side_o)
-    z_in = []
-    for n, mask in enumerate((2, 3, 1)):
-        other = place.partner(mask)[1]
-        z_in.append(copies.swap(own_o.at[pl.ds(other * zrow, zrow), mine], z_o.at[n], mask))
-    copies.got(deep_in_q)
-    query[...] = own_q[pl.ds(pl.multiple_of(side * blk, blk), blk), :].astype(f32) + deep_q[...].astype(f32)
-    high_sum(keep_u, high_u, high_in_u, 2)
-    for item in z_in:
-        copies.got(item)
-
-    def add_z(i, carry):
-        here = pl.ds(i * 32, 32)
-        sum_ = own_o[pl.ds(mp * zrow + i * 32, 32), mine].astype(f32)
-        for n in range(3):
-            sum_ = sum_ + z_o[n, here, :].astype(f32)
-        out[here, :] = sum_
-        return carry
-
-    lax.fori_loop(0, zrow // 32, add_z, 0)
-    for i, (target, keep) in enumerate(((down, keep_d), (gate, keep_g), (up, keep_u))):
-        copies.got(side_in[i])
-
-        def write(n, carry, i=i, target=target, keep=keep):
+    def out_side():
+        add_into(block_o(0, 1 - side), (0, width), deep_o.at[0])
+        note("os", copies.swap(block_o(0, 1 - side), side_o, SIDE))
+
+    def out_mine():
+        add_into(block_o(0, side), (0, width), deep_o.at[1])
+
+    def out_rows():
+        add_into(block_o(0, side), (0, width), side_o)
+        note("oz", *[copies.swap(own_o.at[pl.ds(place.partner(mask)[1] * zrow, zrow), mine], z_o.at[n], mask)
+                     for n, mask in enumerate((2, 3, 1))])
+
+    def out_done():
+        def add_z(i, carry):
+            here = pl.ds(i * 32, 32)
+            sum_ = own_o[pl.ds(mp * zrow + i * 32, 32), mine].astype(f32)
+            for n in range(3):
+                sum_ = sum_ + z_o[n, here, :].astype(f32)
+            out[here, :] = sum_
+            return carry
+
+        lax.fori_loop(0, zrow // 32, add_z, 0)
+
+    def output_done():
+        reduce.arrived()
+
+        def finish_output(i, carry):
+            here = pl.ds(i * 32, 32)
+            total = (residual[here, :] + parts[here, :].astype(f32) + landed[0, here, :].astype(f32)
+                     + landed[1, here, :].astype(f32)).astype(bf16)
+            for s in range(8):
+                output[here, spots[s]] = total[:, s * blk:(s + 1) * blk]
+            return carry
+
+        lax.fori_loop(0, share // 32, finish_output, 0)
+
+    def weight_done(i, target, keep):
+        def write(n, carry):
             target[pl.ds(side * half + n * 16, 16), :] = keep[pl.ds(n * 16, 16), mine].astype(f32)
             target[pl.ds((1 - side) * half + n * 16, 16), :] = side_f[i, pl.ds(n * 16, 16), :].astype(f32)
             return carry
 
         lax.fori_loop(0, half // 16, write, 0)
+
+    task("dq", (), send_tokens)
+    task("g1", (), send_gate_deep)
+    task("u0", (), send_up, 0)
+    task("u1", (), send_up, 1)
+    task("f", (), send_near)
+    task("zg0", (), send_gate)
+    task("xd", (), send_down)
+    task("ot", (), send_out, "ot", 0, 1 - side)
+    task("om", (), send_out, "om", 1, side)
+    task("qc", (), query_give)
+    task("r1", (), reduce_start)
+    task("zg1", ("g1",), gate_sum)
+    task("qk", ("qc",), query_keep)
+    task("dn1", ("f", "dq"), first_product)
+    task("N", ("dn1",), first_norm)
+    task("h0", ("N",), gain_hop, 0)
+    task("zu0", ("u0",), up_sum, 0)
+    task("zu1", ("u1",), up_sum, 1)
+    task("r2", ("r1",), reduce.relayed)
+    task("h1", ("h0",), gain_hop, 1)
+    task("qy1", ("qk", "qs1"), query_side, 1)
+    task("qy0", ("qk", "qs0"), query_side, 0)
+    task("os", ("ot",), out_side)
+    task("h2", ("h1",), gain_hop, 2)
+    task("xg", ("zg0", "zg1"), high_sum, "xg", keep_g, high_g, 1)
+    task("h3", ("h2",), gain_hop, 3)
+    task("O", ("om",), out_mine)
+    task("h4", ("h3",), gain_hop, 4)
+    task("R", ("r2",), output_done)
+    task("h5", ("h4",), gain_hop, 5)
+    task("oz", ("os", "O"), out_rows)
+    task("Q", ("qy1", "qy0", "qd"), query_done)
+    task("xu", ("zu0", "zu1"), high_sum, "xu", keep_u, high_u, 2)
+    task("OD", ("oz",), out_done)
+    task("DD", ("xd",), weight_done, 0, down, keep_d)
+    task("GD", ("xg",), weight_done, 1, gate, keep_g)
+    task("UD", ("xu",), weight_done, 2, up, keep_u)
+    greet(place, (1, 2, 3, CORE, SIDE, DEEP))
+    names = list(tasks)
+    for index in BACK_ORDER or range(len(names)):
+        needs, action = tasks.pop(names[index])
+        for need in needs:
+            for item in items.get(need, ()):
+                copies.got(item)
+        action()
+    assert not tasks
     copies.finish()
 
 
@@ -1081,7 +1171,8 @@
         in_specs=[VM] * 10 + [ANY] * 6,
         out_specs=(VM,) * 8,
         scratch_shapes=[
-            V((half, 2 * blk), bf16), V((hidden, 2 * blk), bf16), V((hidden, 2 * blk), bf16), V((hidden, 2 * blk), bf16),
+            V((half, 2 * blk), bf16), V((hidden, 2 * blk), bf16), V((hidden, 2 * blk), bf16), V((hidden, blk), bf16),
+            V((hidden, 2 * blk), bf16),
             V((half, 2 * blk), bf16), V((half, 2 * blk), bf16), V((3, half, blk), bf16),
             V((width, width // 2), bf16), V((2, width, blk), bf16), V((width, blk), bf16),
             V((3, width // 4, blk), bf16),
@@ -1094,6 +1185,30 @@
         compiler_params=params(ident, 63 << 20), name="back_last",
     )(grad_q, dres, inputs, gain, query_0, query_y, query_x, query_xy, residual, gain_part,
       rows_first, sums, down_sums, gate_sums, out_sums, fparts)
+
+
+def hand_over_kernel(*refs):
+    count = (len(refs) - 2) // 3
+    sources, targets, held = refs[:count], refs[count:2 * count], refs[2 * count:3 * count]
+    in_sems, out_sems = refs[-2:]
+    loads = [pltpu.make_async_copy(sources[n], held[n], in_sems.at[n]) for n in range(count)]
+    stores = [pltpu.make_async_copy(held[n], targets[n], out_sems.at[n]) for n in range(count)]
+    for load in loads:
+        load.start()
+    for load, store in zip(loads, stores):
+        load.wait()
+        store.start()
+    for store in stores:
+        store.wait()
+
+
+def hand_over(*arrays):
+    n = len(arrays)
+    return pl.pallas_call(
+        hand_over_kernel, out_shape=tuple(jax.ShapeDtypeStruct(a.shape, a.dtype) for a in arrays),
+        in_specs=[ANY] * n, out_specs=(ANY,) * n,
+        scratch_shapes=[pltpu.VMEM(a.shape, a.dtype) for a in arrays] + [DMA((n,)), DMA((n,))],
+        compiler_params=pltpu.CompilerParams(vmem_limit_bytes=63 << 20), name="hand_over")(*arrays)
 
 
 def contract(left, right, left_dim, right_dim):
@@ -1326,6 +1441,8 @@
     down_shard, gate_shard, up_shard, out_shard, query_shard, grad_input, output, gains = back_last(
         grad_queries, grad_residual, inputs_here, gain_one, query_0, query_y, query_x, query_xy, residual,
         gain_second_part, rows_first, ffn_sums, down_sums, gate_sums, out_sums, ffn_parts, 6)
+    (grad_kv, grad_input, output, down_shard, out_shard, query_shard, gate_shard, up_shard) = hand_over(
+        grad_kv, grad_input, output, down_shard, out_shard, query_shard, gate_shard, up_shard)
     return (output, grad_input, grad_kv, gains[0], gains[1], query_shard, out_shard,
             gate_shard.T, up_shard.T, down_shard)
 

time: 541 us -> 488 us (0.902)
  Pallas kernels: 525 us -> 483 us
  local copies, waits for them, and re-layouts: 14.4 us -> 0.62 us
    pallas_call x1, Pallas kernels: 224 us -> 188 us  [front_call(): pl.pallas_call(front_kernel, out_shape=(S((seq_len, width), bf16), S((seq...]
    unnamed x22 -> x2, local copies, waits for them, and re-layouts: 12.9 us -> 0.01 us
    pallas_call x0 -> x1, Pallas kernels: none -> 9.36 us  [hand_over(): pl.pallas_call(hand_over_kernel, out_shape=tuple((jax.ShapeDtypeStruct(a....]
    pallas_call x1, Pallas kernels: 128 us -> 121 us  [back_last(): pl.pallas_call(back_last_kernel, out_shape=(S((hidden, blk), f32),) * 3 +...]
    pallas_call x1, Pallas kernels: 75.4 us -> 69.1 us  [back_first(): pl.pallas_call(back_first_kernel, out_shape=(S((share, width), f32), S((1...]
where the time goes in v6:
time: 488 us; the launch traced here: 484 us
  Pallas kernels  483 us (99%)
    pallas_call x1, Pallas kernels, front_call(): pl.pallas_call(front_kernel, out_shape=(S((seq_len, width), bf16), S((seq...  188 us
    pallas_call x1, Pallas kernels, back_last(): pl.pallas_call(back_last_kernel, out_shape=(S((hidden, blk), f32),) * 3 +...  121 us
    pallas_call x1, Pallas kernels, ffn_call(): pl.pallas_call(ffn_kernel, out_shape=(jax.ShapeDtypeStruct((share, width)...  94.3 us
    pallas_call x1, Pallas kernels, back_first(): pl.pallas_call(back_first_kernel, out_shape=(S((share, width), f32), S((1...  69.1 us

profile of v6, /device:TPU:0, one launch (start us, length us, event | category | flops | bytes accessed | tf_op | source)
XLA Modules:
  0.0 484.0 jit_solution(11432071909684472557)
XLA Ops:
  0.6 188.4 %front.1 = (bf16[1024,2048]{1,0:T(8,128)(2,1)}, bf16[1024,2048]{1,0:T(8,128)(2,1)}, bf16[1376,2048]{1,0:T(8,128)(2,1)}, bf16[1376,2048]{1,0:T(8,128)(2,1)}, bf16...) custom-call(bf16[256,2048]{1,0:T(8,128)(2,1)} %x.1, ...), custom_call_target="tpu_custom_call" | custom-call | tf_op jit(solution)/shard_map/front/pallas_call | solution.py:520
  189.1 94.3 %feed_forward.1 = (f32[256,2048]{1,0:T(8,128)}, bf16[256,2048]{1,0:T(8,128)(2,1)}, bf16[256,2048]{1,0:T(8,128)(2,1)}, bf16[1024,2048]{1,0:T(8,128)(2,1)}, bf16[3,1376,1024]{2,1,0:T(8,128)(2,1)}) custom-call(bf16[256,2048]{1,0:T(8,128)(2,1)} %get-tuple-element.58.normed, bf16[256,512]{1,0:T(8,128)(2,1)} %wq.3, bf16[1024,2048]{1,0:T(8,128)(2,1)} %get-tuple-element.59.cots_in, ...), custom_call_target="tpu_custom_call" | custom-call | flops 51942260736 | bytes 41943040 | tf_op jit(solution)/shard_map/feed_forward/pallas_call | solution.py:729
  283.4 69.1 %back_first.1 = (f32[256,2048]{1,0:T(8,128)}, f32[1,2048]{1,0:T(1,128)}, bf16[256,2048]{1,0:T(8,128)(2,1)}, bf16[256,2048]{1,0:T(8,128)(2,1)}, bf16[1024,512]{1,...) custom-call(f32[256,2048]{1,0:T(8,128)} %get-tuple-element.63.dn2, ...), custom_call_target="tpu_custom_call" | custom-call | tf_op jit(solution)/shard_map/back_first/pallas_call | solution.py:871
  352.5 121.5 %back_last.1 = (f32[1376,256]{1,0:T(8,128)}, f32[1376,256]{1,0:T(8,128)}, f32[1376,256]{1,0:T(8,128)}, f32[512,256]{1,0:T(8,128)}, f32[256,512]{1,0:T(8,128)}, /...) custom-call(bf16[1024,512]{1,0:T(8,128)(2,1)} %get-tuple-element.78.grad_q, ...), custom_call_target="tpu_custom_call" | custom-call | tf_op jit(solution)/shard_map/back_last/pallas_call | solution.py:1166
  474.0 0.0 copy-start
  474.0 9.4 %hand_over.1 = (f32[1024,2,512]{2,1,0:T(2,128)}, f32[256,2048]{1,0:T(8,128)}, bf16[256,2048]{1,0:T(8,128)(2,1)}, f32[1376,256]{1,0:T(8,128)}, f32[512,256]{1,0:T...) custom-call(f32[1024,2,512]{2,1,0:T(2,128)} %get-tuple-element.77.refs_0_, ...), custom_call_target="tpu_custom_call" | custom-call | tf_op jit(solution)/shard_map/hand_over/pallas_call | solution.py:1207
  483.4 0.0 copy-done
  483.4 0.6 fusion
Async XLA Ops:
  474.0 9.4 %copy-start = (f32[2,2048]{1,0:T(2,128)S(1)}, f32[2,2048]{1,0:T(2,128)}, u32[]{:S(2)}) copy-start(f32[2,2048]{1,0:T(2,128)} %get-tuple-element.100) | copy-start | bytes 49156

commit v7 on v6

--- a/solution.py
+++ b/solution.py
@@ -301,9 +301,9 @@
 
 
 def front_kernel(x, cot, gain_one_in, gain_two_in, wq, wo, wg, wu, wd, pairs, segments,
-                 rows_out, cots, gate, up, down, out_out, queries, context_own, lse, residual, normed,
-                 x_here, cot_here, gain_one, gain_two, keys, values, starts,
-                 first, rows, query, out, context,
+                 rows_out, cots, gate, up, down, out_out, queries_to, context_own, lse, residual, normed,
+                 x_to, cot_to, gain_one, gain_two, keys_to, values_to, starts,
+                 queries, x_here, cot_here, keys, values, first, rows, query, out, context,
                  send_sems, recv_sems, local_sems):
     place = Place()
     dp, mp = place.dp, place.mp
@@ -402,6 +402,8 @@
 
         lax.fori_loop(0, share // 32, norm_first, 0)
         rows[pl.ds(mp * share, share), :] = first[...]
+        locals_.append(copies.local(x_here, x_to))
+        locals_.append(copies.local(cot_here, cot_to))
 
     def split_pairs():
         def split(i, carry):
@@ -418,6 +420,8 @@
             size = jnp.sum((ids == document).astype(jnp.int32), axis=1, keepdims=True)
             begun = begun + jnp.where(ids > document, size, 0)
         starts[...] = begun
+        locals_.append(copies.local(keys, keys_to))
+        locals_.append(copies.local(values, values_to))
         query[pl.ds(own * blk, blk), :] = wq[...]
         out[pl.ds(mp * zrow, zrow), pl.ds(pl.multiple_of(own * blk, blk), blk)] = wo[...]
         locals_.append(copies.local(cot_here, cots.at[0:share, :]))
@@ -477,6 +481,7 @@
     def finish_tokens():
         context_own[:, pl.ds(pl.multiple_of(mp * local, local), local)] = context[pl.ds(mp * share, share), :]
         locals_.append(copies.local(rows, rows_out))
+        locals_.append(copies.local(queries, queries_to))
         locals_.append(copies.local(out, out_out))
 
         def project_out(n, carry):
@@ -526,10 +531,12 @@
             S((share, width), bf16), S((share, width), bf16), S((1, width), f32), S((1, width), f32),
             S((seq_len, local), bf16), S((seq_len, local), bf16), S((1, seq_len), jnp.int32)),
         in_specs=[VM] * 11,
-        out_specs=(ANY,) * 6 + (VM,) * 12,
+        out_specs=(ANY,) * 7 + (VM,) * 4 + (ANY,) * 2 + (VM,) * 2 + (ANY,) * 2 + (VM,),
         scratch_shapes=[
+            V((seq_len, local), bf16), V((share, width), bf16), V((share, width), bf16), V((seq_len, local), bf16),
+            V((seq_len, local), bf16),
             V((share, width), bf16), V((seq_len, width), bf16), V((width, local), bf16), V((width, width), bf16),
-            V((seq_len, local), bf16), DMA((96,)), DMA((96,)), DMA((8,))],
+            V((seq_len, local), bf16), DMA((96,)), DMA((96,)), DMA((12,))],
         compiler_params=params(ident, 60 << 20), name="front",
     )(x, cot, gain_one, gain_two, wq, wo, wg, wu, wd, pairs, segments)
 
@@ -744,10 +751,10 @@
     )(normed, wq, cots, down, gate, up)
 
 
-def back_first_kernel(dn2, residual, cot, gain, context, queries, keys, values, lse, starts, query_0, query_y,
-                      out_whole, sums,
-                      dres, gain_part, query_x, query_xy, grad_q, pairs, down_sums, gate_sums, out_sums,
-                      heads, keep_d, deep_d, high_d, deep_g, grad_low, wout, dctx, give_o, core_o, dk, dv,
+def back_first_kernel(dn2, residual, cot, gain, lse, starts, context_in, queries_in, keys_in, values_in,
+                      query_0, query_y, out_whole, sums,
+                      dres_out, gain_part, query_x, query_xy, grad_q, pairs_out, down_sums, gate_sums, sums_out,
+                      context, queries, keys, values, dres, pairs, out_sums, heads, keep_d, deep_d, high_d, deep_g, grad_low, wout, dctx, give_o, core_o, dk, dv,
                       send_sems, recv_sems, local_sems):
     place = Place()
     mp = place.mp
@@ -761,6 +768,8 @@
     copies = Copies(place, send_sems, recv_sems, local_sems)
     loads = [copies.local(out_whole.at[pl.ds(z * local, local), :], wout.at[z]) for z in range(4)]
     load_d = copies.local(sums.at[0, :, pl.ds(0, quarter)], keep_d)
+    late = [copies.local(*pair) for pair in ((context_in, context), (queries_in, queries), (keys_in, keys),
+                                             (values_in, values))]
     load_g = copies.local(sums.at[1, :, pl.ds(0, blk)], gate_sums)
     greet(place, (1, 2, 3, CORE, SIDE, DEEP))
     in_d = [copies.swap(sums.at[0, :, pl.ds(quarter + x * blk, blk)], deep_d.at[:, pl.ds(x * blk, blk)], DEEP)
@@ -784,7 +793,8 @@
         return carry
 
     lax.fori_loop(0, share // 32, norm, 0)
-    for copy in loads:
+    saves = [copies.local(dres, dres_out)]
+    for copy in loads + late:
         copy.wait()
     heads_in = []
     for mask in (2, 3, 1, 0):
@@ -820,6 +830,7 @@
         return carry
 
     lax.fori_loop(0, chunks, keep, 0)
+    saves.append(copies.local(out_sums, sums_out))
     in_g = copies.swap(sums.at[1, :, pl.ds(quarter, blk)], deep_g, DEEP)
     load_d.wait()
     give_rows = pl.ds(half, half)
@@ -838,6 +849,7 @@
         return carry
 
     lax.fori_loop(0, local // HEAD_DIM, one_head, 0)
+    saves.append(copies.local(pairs, pairs_out))
     load_g.wait()
     copies.got(in_g)
     add_into(gate_sums, (0, hidden), deep_g)
@@ -850,6 +862,8 @@
         return carry
 
     lax.fori_loop(0, half // 16, add_d, 0)
+    for copy in saves:
+        copy.wait()
     copies.finish()
 
     def sent(n, carry):
@@ -873,16 +887,18 @@
         out_shape=(S((share, width), f32), S((1, width), f32), S(query_0.shape, bf16), S(query_0.shape, bf16),
                    S((seq_len, local), bf16), S((seq_len, 2, local), f32),
                    S((half, quarter), bf16), S((hidden, quarter // 2), bf16), S((width, width // 2), bf16)),
-        in_specs=[VM] * 12 + [ANY, ANY],
-        out_specs=(VM,) * 9,
+        in_specs=[VM] * 6 + [ANY] * 8,
+        out_specs=(ANY, VM, ANY, ANY, VM, ANY, VM, VM, ANY),
         scratch_shapes=[
+            V((share, width), bf16), V((seq_len, local), bf16), V((seq_len, local), bf16), V((seq_len, local), bf16),
+            V((share, width), f32), V((seq_len, 2, local), f32), V((width, width // 2), bf16),
             V((seq_len, local), bf16), V((hidden, quarter), bf16), V((hidden, quarter), bf16), V((half, quarter), bf16),
             V((hidden, quarter // 2), bf16), V((share, width), bf16),
             V((4, width // 4, width), bf16), V((share, width), bf16), V((width, width // 2), bf16),
             V((width, width // 2), bf16), V((seq_len, HEAD_DIM), f32), V((seq_len, HEAD_DIM), f32),
-            DMA((20,)), DMA((20,)), DMA((6,))],
+            DMA((20,)), DMA((20,)), DMA((13,))],
         compiler_params=params(ident, 63 << 20), name="back_first",
-    )(dn2, residual, cot, gain, context, queries, keys, values, lse, starts, query_0, query_y, out_whole, sums)
+    )(dn2, residual, cot, gain, lse, starts, context, queries, keys, values, query_0, query_y, out_whole, sums)
 
 
 BACK_ORDER = (
@@ -891,10 +907,10 @@
 )
 
 
-def back_last_kernel(grad_q, dres, inputs, gain, query_0, query_y, query_x, query_xy, residual, gain_part,
+def back_last_kernel(grad_q, gain, gain_part, dres_in, inputs_in, residual_in, query_0, query_y, query_x, query_xy,
                      rows_first, sums, down_sums, gate_sums, out_sums, fparts,
-                     down, gate, up, out, query, grad_input, output, gains,
-                     keep_d, keep_g, keep_u, deep_g, deep_u, high_g, high_u, side_f,
+                     down_to, gate_to, up, out, query, input_to, output_to, gains,
+                     dres, inputs, residual, near, down, gate, grad_input, output, keep_d, keep_g, keep_u, deep_g, deep_u, high_g, high_u, side_f,
                      own_o, deep_o, side_o, z_o,
                      give_q, own_q, core_q, side_q, deep_q, parts, relay, landed,
                      grad_own, rows, query_far, dn1, gain_rows, gains_got,
@@ -903,10 +919,11 @@
     mp = place.mp
     side = place.bit(SIDE)
     share, width = dres.shape
-    hidden, blk = down.shape
+    hidden, blk = up.shape
     half = hidden // 2
     local = grad_q.shape[1]
     zrow = out.shape[0]
+    saves = []
     quarter = 2 * blk
     wide = width // 2
     copies = Copies(place, send_sems, recv_sems, local_sems)
@@ -917,7 +934,9 @@
     load_o = copies.local(out_sums, own_o)
     load_u = copies.local(sums.at[2, :, pl.ds(0, quarter)], keep_u)
     load_p = copies.local(fparts, parts)
-    near = (query_0, query_y, query_x, query_xy)
+    near_in = (query_0, query_y, query_x, query_xy)
+    load_near = [copies.local(piece, near.at[n]) for n, piece in enumerate(near_in)]
+    load_late = [copies.local(*pair) for pair in ((dres_in, dres), (inputs_in, inputs), (residual_in, residual))]
     spot_of = (side, side + 2, 1 - side, 3 - side)
     give_rows = pl.ds(half, half)
     mine = pl.ds(pl.multiple_of(side * blk, blk), blk)
@@ -959,7 +978,7 @@
         note("u%d" % x, copies.swap(sums.at[2, :, pl.ds(quarter + x * blk, blk)], deep_u.at[:, pl.ds(x * blk, blk)], DEEP))
 
     def send_near():
-        note("f", *[copies.swap(piece, query_far.at[n], CORE) for n, piece in enumerate(near)])
+        note("f", *[copies.swap(piece, query_far.at[n], CORE) for n, piece in enumerate(near_in)])
 
     def send_gate():
         ready("g", load_g)
@@ -1012,11 +1031,14 @@
         note("r1", reduce.first, reduce.second)
 
     def first_product():
+        for load in load_near:
+            load.wait()
         for n in range(4):
-            dn1[:, pl.ds(pl.multiple_of(spot_of[n] * blk, blk), blk)] = dot(grad_own[...], near[n][...], 1, 1)
+            dn1[:, pl.ds(pl.multiple_of(spot_of[n] * blk, blk), blk)] = dot(grad_own[...], near[n], 1, 1)
             dn1[:, pl.ds(pl.multiple_of((spot_of[n] + 4) * blk, blk), blk)] = dot(grad_own[...], query_far[n], 1, 1)
 
     def first_norm():
+        ready("v", *load_late)
         gain_rows[0:1, :] = jnp.zeros((1, width), f32)
         gain_rows[1:2, :] = gain_part[...]
 
@@ -1035,6 +1057,7 @@
             return carry
 
         lax.fori_loop(0, share // 32, norm, 0)
+        saves.append(copies.local(grad_input, input_to))
         for s in range(8):
             gains[:, spots[s]] = gain_rows[:, s * blk:(s + 1) * blk]
 
@@ -1085,6 +1108,7 @@
         lax.fori_loop(0, zrow // 32, add_z, 0)
 
     def output_done():
+        ready("v", *load_late)
         reduce.arrived()
 
         def finish_output(i, carry):
@@ -1096,14 +1120,17 @@
             return carry
 
         lax.fori_loop(0, share // 32, finish_output, 0)
-
-    def weight_done(i, target, keep):
+        saves.append(copies.local(output, output_to))
+
+    def weight_done(i, target, keep, final):
         def write(n, carry):
             target[pl.ds(side * half + n * 16, 16), :] = keep[pl.ds(n * 16, 16), mine].astype(f32)
             target[pl.ds((1 - side) * half + n * 16, 16), :] = side_f[i, pl.ds(n * 16, 16), :].astype(f32)
             return carry
 
         lax.fori_loop(0, half // 16, write, 0)
+        if final is not None:
+            saves.append(copies.local(target, final))
 
     task("dq", (), send_tokens)
     task("g1", (), send_gate_deep)
@@ -1139,9 +1166,9 @@
     task("Q", ("qy1", "qy0", "qd"), query_done)
     task("xu", ("zu0", "zu1"), high_sum, "xu", keep_u, high_u, 2)
     task("OD", ("oz",), out_done)
-    task("DD", ("xd",), weight_done, 0, down, keep_d)
-    task("GD", ("xg",), weight_done, 1, gate, keep_g)
-    task("UD", ("xu",), weight_done, 2, up, keep_u)
+    task("DD", ("xd",), weight_done, 0, down, keep_d, down_to)
+    task("GD", ("xg",), weight_done, 1, gate, keep_g, gate_to)
+    task("UD", ("xu",), weight_done, 2, up, keep_u, None)
     greet(place, (1, 2, 3, CORE, SIDE, DEEP))
     names = list(tasks)
     for index in BACK_ORDER or range(len(names)):
@@ -1151,6 +1178,8 @@
                 copies.got(item)
         action()
     assert not tasks
+    for copy in saves:
+        copy.wait()
     copies.finish()
 
 
@@ -1168,9 +1197,11 @@
         out_shape=(S((hidden, blk), f32),) * 3
         + (S((width // 4, blk), f32), S((blk, local), f32), S((share, width), f32), S((share, width), bf16),
            S((2, width), f32)),
-        in_specs=[VM] * 10 + [ANY] * 6,
-        out_specs=(VM,) * 8,
+        in_specs=[VM] * 3 + [ANY] * 13,
+        out_specs=(ANY, ANY, VM, VM, VM, ANY, ANY, VM),
         scratch_shapes=[
+            V((share, width), f32), V((share, width), bf16), V((share, width), f32), V((4, blk, width), bf16),
+            V((hidden, blk), f32), V((hidden, blk), f32), V((share, width), f32), V((share, width), bf16),
             V((half, 2 * blk), bf16), V((hidden, 2 * blk), bf16), V((hidden, 2 * blk), bf16), V((hidden, blk), bf16),
             V((hidden, 2 * blk), bf16),
             V((half, 2 * blk), bf16), V((half, 2 * blk), bf16), V((3, half, blk), bf16),
@@ -1181,9 +1212,9 @@
             V((share * 4, width), bf16), V((2, share // 2, width), bf16), V((2, share, width), bf16),
             V((share, width), bf16), V((share * 4, width), bf16), V((4, blk, width), bf16), V((share, width), f32),
             V((2, width), f32), V((5, 2, width), f32),
-            DMA((48,)), DMA((48,)), DMA((12,))],
+            DMA((48,)), DMA((48,)), DMA((20,))],
         compiler_params=params(ident, 63 << 20), name="back_last",
-    )(grad_q, dres, inputs, gain, query_0, query_y, query_x, query_xy, residual, gain_part,
+    )(grad_q, gain, gain_part, dres, inputs, residual, query_0, query_y, query_x, query_xy,
       rows_first, sums, down_sums, gate_sums, out_sums, fparts)
 
 

time: 488 us -> 476 us (0.975)
  Pallas kernels: 483 us -> 471 us
    pallas_call x1, Pallas kernels: 69.1 us -> 63.7 us  [back_first(): pl.pallas_call(back_first_kernel, out_shape=(S((share, width), f32), S((1...]
where the time goes in v7:
time: 476 us; the launch traced here: 473 us
  Pallas kernels  471 us (99%)
    pallas_call x1, Pallas kernels, front_call(): pl.pallas_call(front_kernel, out_shape=(S((seq_len, width), bf16), S((seq...  187 us
    pallas_call x1, Pallas kernels, back_last(): pl.pallas_call(back_last_kernel, out_shape=(S((hidden, blk), f32),) * 3 +...  117 us
    pallas_call x1, Pallas kernels, ffn_call(): pl.pallas_call(ffn_kernel, out_shape=(jax.ShapeDtypeStruct((share, width)...  94.3 us
    pallas_call x1, Pallas kernels, back_first(): pl.pallas_call(back_first_kernel, out_shape=(S((share, width), f32), S((1...  63.7 us

profile of v7, /device:TPU:0, one launch (start us, length us, event | category | flops | bytes accessed | tf_op | source)
XLA Modules:
  0.0 472.8 jit_solution(2366101872635891447)
XLA Ops:
  0.6 187.2 %front.1 = (bf16[1024,2048]{1,0:T(8,128)(2,1)}, bf16[1024,2048]{1,0:T(8,128)(2,1)}, bf16[1376,2048]{1,0:T(8,128)(2,1)}, bf16[1376,2048]{1,0:T(8,128)(2,1)}, bf16...) custom-call(bf16[256,2048]{1,0:T(8,128)(2,1)} %x.1, ...), custom_call_target="tpu_custom_call" | custom-call | tf_op jit(solution)/shard_map/front/pallas_call | solution.py:525
  187.9 94.3 %feed_forward.1 = (f32[256,2048]{1,0:T(8,128)}, bf16[256,2048]{1,0:T(8,128)(2,1)}, bf16[256,2048]{1,0:T(8,128)(2,1)}, bf16[1024,2048]{1,0:T(8,128)(2,1)}, bf16[3,1376,1024]{2,1,0:T(8,128)(2,1)}) custom-call(bf16[256,2048]{1,0:T(8,128)(2,1)} %get-tuple-element.58.normed, bf16[256,512]{1,0:T(8,128)(2,1)} %wq.3, bf16[1024,2048]{1,0:T(8,128)(2,1)} %get-tuple-element.59.cots_in, ...), custom_call_target="tpu_custom_call" | custom-call | flops 51942260736 | bytes 41943040 | tf_op jit(solution)/shard_map/feed_forward/pallas_call | solution.py:736
  282.2 63.7 %back_first.1 = (f32[256,2048]{1,0:T(8,128)}, f32[1,2048]{1,0:T(1,128)}, bf16[256,2048]{1,0:T(8,128)(2,1)}, bf16[256,2048]{1,0:T(8,128)(2,1)}, bf16[1024,512]{1,...) custom-call(f32[256,2048]{1,0:T(8,128)} %get-tuple-element.63.dn2, ...), custom_call_target="tpu_custom_call" | custom-call | tf_op jit(solution)/shard_map/back_first/pallas_call | solution.py:885
  345.9 116.9 %back_last.1 = (f32[1376,256]{1,0:T(8,128)}, f32[1376,256]{1,0:T(8,128)}, f32[1376,256]{1,0:T(8,128)}, f32[512,256]{1,0:T(8,128)}, f32[256,512]{1,0:T(8,128)}, /...) custom-call(bf16[1024,512]{1,0:T(8,128)(2,1)} %get-tuple-element.78.grad_q, ...), custom_call_target="tpu_custom_call" | custom-call | tf_op jit(solution)/shard_map/back_last/pallas_call | solution.py:1195
  462.8 0.0 copy-start
  462.8 9.4 %hand_over.1 = (f32[1024,2,512]{2,1,0:T(2,128)}, f32[256,2048]{1,0:T(8,128)}, bf16[256,2048]{1,0:T(8,128)(2,1)}, f32[1376,256]{1,0:T(8,128)}, f32[512,256]{1,0:T...) custom-call(f32[1024,2,512]{2,1,0:T(2,128)} %get-tuple-element.77.refs_0_, ...), custom_call_target="tpu_custom_call" | custom-call | tf_op jit(solution)/shard_map/hand_over/pallas_call | solution.py:1238
  472.2 0.0 copy-done
  472.2 0.6 fusion
Async XLA Ops:
  462.8 9.4 %copy-start = (f32[2,2048]{1,0:T(2,128)S(1)}, f32[2,2048]{1,0:T(2,128)}, u32[]{:S(2)}) copy-start(f32[2,2048]{1,0:T(2,128)} %get-tuple-element.100) | copy-start | bytes 49156

commit v8 on v7

--- a/solution.py
+++ b/solution.py
@@ -1124,8 +1124,8 @@
 
     def weight_done(i, target, keep, final):
         def write(n, carry):
-            target[pl.ds(side * half + n * 16, 16), :] = keep[pl.ds(n * 16, 16), mine].astype(f32)
-            target[pl.ds((1 - side) * half + n * 16, 16), :] = side_f[i, pl.ds(n * 16, 16), :].astype(f32)
+            target[pl.ds(side * half + n * 16, 16), :] = keep[pl.ds(n * 16, 16), mine]
+            target[pl.ds((1 - side) * half + n * 16, 16), :] = side_f[i, pl.ds(n * 16, 16), :]
             return carry
 
         lax.fori_loop(0, half // 16, write, 0)
@@ -1194,14 +1194,14 @@
     S = jax.ShapeDtypeStruct
     return pl.pallas_call(
         back_last_kernel,
-        out_shape=(S((hidden, blk), f32),) * 3
+        out_shape=(S((hidden, blk), bf16),) * 3
         + (S((width // 4, blk), f32), S((blk, local), f32), S((share, width), f32), S((share, width), bf16),
            S((2, width), f32)),
         in_specs=[VM] * 3 + [ANY] * 13,
         out_specs=(ANY, ANY, VM, VM, VM, ANY, ANY, VM),
         scratch_shapes=[
             V((share, width), f32), V((share, width), bf16), V((share, width), f32), V((4, blk, width), bf16),
-            V((hidden, blk), f32), V((hidden, blk), f32), V((share, width), f32), V((share, width), bf16),
+            V((hidden, blk), bf16), V((hidden, blk), bf16), V((share, width), f32), V((share, width), bf16),
             V((half, 2 * blk), bf16), V((hidden, 2 * blk), bf16), V((hidden, 2 * blk), bf16), V((hidden, blk), bf16),
             V((hidden, 2 * blk), bf16),
             V((half, 2 * blk), bf16), V((half, 2 * blk), bf16), V((3, half, blk), bf16),
@@ -1219,26 +1219,36 @@
 
 
 def hand_over_kernel(*refs):
-    count = (len(refs) - 2) // 3
+    count = (len(refs) - 5) // 3
     sources, targets, held = refs[:count], refs[count:2 * count], refs[2 * count:3 * count]
+    widened = refs[3 * count:3 * count + 3]
     in_sems, out_sems = refs[-2:]
     loads = [pltpu.make_async_copy(sources[n], held[n], in_sems.at[n]) for n in range(count)]
-    stores = [pltpu.make_async_copy(held[n], targets[n], out_sems.at[n]) for n in range(count)]
     for load in loads:
         load.start()
-    for load, store in zip(loads, stores):
-        load.wait()
+    stores = []
+    for n in range(count):
+        loads[n].wait()
+        holder = held[n]
+        if n >= count - 3:
+            holder = widened[n - count + 3]
+            holder[...] = held[n][...].astype(f32)
+        store = pltpu.make_async_copy(holder, targets[n], out_sems.at[n])
         store.start()
+        stores.append(store)
     for store in stores:
         store.wait()
 
 
 def hand_over(*arrays):
     n = len(arrays)
+    wide = [jax.ShapeDtypeStruct(a.shape, f32) for a in arrays[-3:]]
     return pl.pallas_call(
-        hand_over_kernel, out_shape=tuple(jax.ShapeDtypeStruct(a.shape, a.dtype) for a in arrays),
+        hand_over_kernel,
+        out_shape=tuple([jax.ShapeDtypeStruct(a.shape, a.dtype) for a in arrays[:-3]] + wide),
         in_specs=[ANY] * n, out_specs=(ANY,) * n,
-        scratch_shapes=[pltpu.VMEM(a.shape, a.dtype) for a in arrays] + [DMA((n,)), DMA((n,))],
+        scratch_shapes=[pltpu.VMEM(a.shape, a.dtype) for a in arrays]
+        + [pltpu.VMEM(w.shape, f32) for w in wide] + [DMA((n,)), DMA((n,))],
         compiler_params=pltpu.CompilerParams(vmem_limit_bytes=63 << 20), name="hand_over")(*arrays)
 
 
@@ -1472,8 +1482,8 @@
     down_shard, gate_shard, up_shard, out_shard, query_shard, grad_input, output, gains = back_last(
         grad_queries, grad_residual, inputs_here, gain_one, query_0, query_y, query_x, query_xy, residual,
         gain_second_part, rows_first, ffn_sums, down_sums, gate_sums, out_sums, ffn_parts, 6)
-    (grad_kv, grad_input, output, down_shard, out_shard, query_shard, gate_shard, up_shard) = hand_over(
-        grad_kv, grad_input, output, down_shard, out_shard, query_shard, gate_shard, up_shard)
+    (grad_kv, grad_input, output, out_shard, query_shard, down_shard, gate_shard, up_shard) = hand_over(
+        grad_kv, grad_input, output, out_shard, query_shard, down_shard, gate_shard, up_shard)
     return (output, grad_input, grad_kv, gains[0], gains[1], query_shard, out_shard,
             gate_shard.T, up_shard.T, down_shard)
 

time: 476 us -> 475 us (level)
  no operation moved by 1% of the time
where the time goes in v8:
time: 475 us; the launch traced here: 471 us
  Pallas kernels  469 us (99%)
    pallas_call x1, Pallas kernels, front_call(): pl.pallas_call(front_kernel, out_shape=(S((seq_len, width), bf16), S((seq...  187 us
    pallas_call x1, Pallas kernels, back_last(): pl.pallas_call(back_last_kernel, out_shape=(S((hidden, blk), bf16),) * 3...  117 us
    pallas_call x1, Pallas kernels, ffn_call(): pl.pallas_call(ffn_kernel, out_shape=(jax.ShapeDtypeStruct((share, width)...  94.3 us
    pallas_call x1, Pallas kernels, back_first(): pl.pallas_call(back_first_kernel, out_shape=(S((share, width), f32), S((1...  63.7 us

profile of v8, /device:TPU:0, one launch (start us, length us, event | category | flops | bytes accessed | tf_op | source)
XLA Modules:
  0.0 471.5 jit_solution(8386567183763822221)
XLA Ops:
  0.6 187.2 %front.1 = (bf16[1024,2048]{1,0:T(8,128)(2,1)}, bf16[1024,2048]{1,0:T(8,128)(2,1)}, bf16[1376,2048]{1,0:T(8,128)(2,1)}, bf16[1376,2048]{1,0:T(8,128)(2,1)}, bf16...) custom-call(bf16[256,2048]{1,0:T(8,128)(2,1)} %x.1, ...), custom_call_target="tpu_custom_call" | custom-call | tf_op jit(solution)/shard_map/front/pallas_call | solution.py:525
  187.9 94.3 %feed_forward.1 = (f32[256,2048]{1,0:T(8,128)}, bf16[256,2048]{1,0:T(8,128)(2,1)}, bf16[256,2048]{1,0:T(8,128)(2,1)}, bf16[1024,2048]{1,0:T(8,128)(2,1)}, bf16[3,1376,1024]{2,1,0:T(8,128)(2,1)}) custom-call(bf16[256,2048]{1,0:T(8,128)(2,1)} %get-tuple-element.58.normed, bf16[256,512]{1,0:T(8,128)(2,1)} %wq.3, bf16[1024,2048]{1,0:T(8,128)(2,1)} %get-tuple-element.59.cots_in, ...), custom_call_target="tpu_custom_call" | custom-call | flops 51942260736 | bytes 41943040 | tf_op jit(solution)/shard_map/feed_forward/pallas_call | solution.py:736
  282.2 63.7 %back_first.1 = (f32[256,2048]{1,0:T(8,128)}, f32[1,2048]{1,0:T(1,128)}, bf16[256,2048]{1,0:T(8,128)(2,1)}, bf16[256,2048]{1,0:T(8,128)(2,1)}, bf16[1024,512]{1,...) custom-call(f32[256,2048]{1,0:T(8,128)} %get-tuple-element.63.dn2, ...), custom_call_target="tpu_custom_call" | custom-call | tf_op jit(solution)/shard_map/back_first/pallas_call | solution.py:885
  345.9 116.6 %back_last.1 = (bf16[1376,256]{1,0:T(8,128)(2,1)}, bf16[1376,256]{1,0:T(8,128)(2,1)}, bf16[1376,256]{1,0:T(8,128)(2,1)}, f32[512,256]{1,0:T(8,128)}, f32[256,512...) custom-call(bf16[1024,512]{1,0:T(8,128)(2,1)} %get-tuple-element.78.grad_q, ...), custom_call_target="tpu_custom_call" | custom-call | tf_op jit(solution)/shard_map/back_last/pallas_call | solution.py:1195
  462.5 1.4 fusion
  463.9 7.4 %hand_over.1 = (f32[1024,2,512]{2,1,0:T(2,128)}, f32[256,2048]{1,0:T(8,128)}, bf16[256,2048]{1,0:T(8,128)(2,1)}, f32[512,256]{1,0:T(8,128)}, f32[256,512]{1,0:T(...) custom-call(f32[1024,2,512]{2,1,0:T(2,128)} %get-tuple-element.77.refs_0_, ...), custom_call_target="tpu_custom_call" | custom-call | tf_op jit(solution)/shard_map/hand_over/pallas_call | solution.py:1246
